TPU v7x, 32 devices: a whole 2x2x4 slice. The times are simulated.
32 devices in a mesh: mult: 4 (over x, core), chan: 8 (over z, y).
Axes of the slice: x: 2, y: 2, z: 4, core: 2. Of those that a mesh axis runs over, the one named last changes fastest.
Arguments:
- columns: float32 [64, 1024, 128], P('chan'), may hold values from -6 to 6
- panels: float32 [8, 2, 1024, 1024], P('mult', None, 'chan'), may hold values from -0.1875 to 0.1875
- coefficients: float32 [64, 16, 8], P('chan', None, 'mult'), may hold values from -2 to 2
- channel_cols: int32 [64, 16], P('chan'), may hold values from 0 to 63, as said below
- used_slots: int32 [64], P('chan'), may hold values from 1 to 16, as said below
- lambda_low: int32 [64, 16], P('chan'), may hold values from 0 to 3
- lambda_high: int32 [64, 16], P('chan'), may hold values from 5 to 8
- energies: float32 [64], P('chan'), may hold values from 0 to 2
- contour: float32 [2], replicated, may hold values from 0.5 to 1.5
Outputs:
- filtered: float32 [64, 1024, 128], P('chan', 'mult')
Inputs may be any that keep to these rules, and one draw needn't show every extreme that they name: channel_cols[i, s] // 8 differs from i // 8 by at most 2, and channel_cols[i, 0] = i. `used_slots`: some channel uses all 16 slots.
All inputs are finite; a program needn't handle non-finite values.
Results may differ from a plain program's by a relative error of at most 0.0001.
Values sent between devices are 32-bit elements; how exact they have to be, the bound alone decides.
No kernel may reach another device: no remote copies, remote signals or barrier semaphores. Data moves between devices by JAX's collectives and lax.ppermute only.
A program may use at most 192 MiB of HBM per device.

v0:
```python
import jax
import jax.numpy as jnp
from jax import lax
from jax.sharding import PartitionSpec as P

MAXNZ = 16
R = 2


def shifted(value, axis, by):
    peers = lax.axis_size(axis)
    pairs = [(i, i + by) for i in range(peers) if 0 <= i + by < peers]
    return lax.ppermute(value, axis, pairs)


def apply_panels(panels, operand, half_width):
    panel_part = lax.all_gather(panels, "chan", axis=2, tiled=True)
    real_panel = panel_part[:, 0]
    imag_panel = panel_part[:, 1]
    real_prod = jnp.einsum("lrb,clbk->clrk", real_panel, operand, precision=lax.Precision.HIGHEST)
    imag_prod = jnp.einsum("lrb,clbk->clrk", imag_panel, operand, precision=lax.Precision.HIGHEST)
    return jnp.concatenate(
        [
            real_prod[..., :half_width] - imag_prod[..., half_width:],
            real_prod[..., half_width:] + imag_prod[..., :half_width],
        ],
        axis=-1,
    )


def body(
    columns,
    panels,
    coefficients,
    channel_cols,
    used_slots,
    lambda_low,
    lambda_high,
    energies,
    contour,
):
    block_len = columns.shape[0]
    half_width = columns.shape[2] // 2
    lam_local = panels.shape[0]
    chan_index = lax.axis_index("chan")
    mult_index = lax.axis_index("mult")
    span = 2 * R + 1
    base_channel = (chan_index - R) * block_len
    local_cols = channel_cols - base_channel
    slot_ids = jnp.arange(MAXNZ, dtype=jnp.int32)
    live_slot = slot_ids[None, :] < used_slots[:, None]
    lambda_ids = mult_index * lam_local + jnp.arange(lam_local, dtype=jnp.int32)
    in_range = (lambda_ids[None, None, :] >= lambda_low[:, :, None]) & (
        lambda_ids[None, None, :] < lambda_high[:, :, None]
    )
    weights = jnp.where(
        live_slot[:, :, None] & in_range, coefficients, jnp.zeros_like(coefficients)
    )
    window_ids = jnp.arange(span * block_len, dtype=jnp.int32)
    one_hot = (local_cols[:, :, None] == window_ids[None, None, :]).astype(jnp.float32)
    mixing = jnp.einsum("isc,isl->icl", one_hot, weights, precision=lax.Precision.HIGHEST)
    shift_list = list(range(R, 0, -1)) + list(range(-1, -R - 1, -1))
    nearby = [shifted(columns, "chan", distance) for distance in shift_list]
    window = jnp.concatenate(nearby[:R] + [columns] + nearby[R:], axis=0)
    combined = jnp.einsum("icl,cnk->ilnk", mixing, window, precision=lax.Precision.HIGHEST)
    coupled = jnp.sum(apply_panels(panels, combined, half_width), axis=1)
    summed = lax.psum_scatter(-coupled, "mult", scatter_dimension=1, tiled=True)
    row_count = columns.shape[1] // lax.axis_size("mult")
    own_cols = lax.dynamic_slice_in_dim(columns, mult_index * row_count, row_count, 1)
    energy_shift = (contour[0] - energies)[:, None, None]
    imag_shift = contour[1]
    real_part = own_cols[..., :half_width]
    imag_part = own_cols[..., half_width:]
    out_real = energy_shift * real_part - imag_shift * imag_part + summed[..., :half_width]
    out_imag = energy_shift * imag_part + imag_shift * real_part + summed[..., half_width:]
    return jnp.concatenate([out_real, out_imag], axis=-1)


def solution(mesh):
    return jax.shard_map(
        body,
        mesh=mesh,
        in_specs=(
            P("chan", None, None),
            P("mult", None, "chan", None),
            P("chan", None, "mult"),
            P("chan", None),
            P("chan"),
            P("chan", None),
            P("chan", None),
            P("chan"),
            P(),
        ),
        out_specs=P("chan", "mult", None),
        check_vma=False,
    )
```

profile of v0, /device:TPU:0, one launch (start us, length us, event | category | flops | bytes accessed | tf_op | source)
XLA Modules:
  0.0 570.0 jit_solution(1351406280177618213)
XLA Ops:
  6.6 3.2 copy.24
  9.8 6.6 %copy.19 = f32[8,1024,128]{2,0,1:T(8,128)} copy(f32[8,1024,128]{2,1,0:T(8,128)} %param.9) | data formatting | bytes 8388608 | tf_op args[0]
  16.4 6.9 %collective-permute-start = (f32[8,1024,128]{2,0,1:T(8,128)}, f32[8,1024,128]{2,0,1:T(8,128)}, u32[]{:S(2)}, u32[]{:S(2)}) collective-permute-start(f32[8,1024,128]{2,0,1:T(8,128)} %copy.19), channel_id=1, source_target_pairs={{0,2},{1,3},{2,4},{3,5},{4,6},{5,7},{8,10},{9,11},{10,12},{11,13},... | collective-permute-start | bytes 12582920 | tf_op jit(solution)/shard_map/ppermute | solution.py:13
  23.3 5.4 collective-permute-start.1
  28.7 1.3 collective-permute-start.2
  30.0 1.8 collective-permute-start.3
  31.8 0.1 iota_compare_fusion.2
  31.9 0.2 convolution_bitcast_fusion
  32.2 162.5 %collective-permute-done = f32[8,1024,128]{2,0,1:T(8,128)} collective-permute-done((f32[8,1024,128]{2,0,1:T(8,128)}, f32[8,1024,128]{2,0,1:T(8,128)}, u32[]{:S(2)}, u32[]{:S(2)}) %collective-permute-start) | collective-permute-done | bytes 4194336 | tf_op jit(solution)/shard_map/ppermute | solution.py:13
  194.7 2.5 constant_dynamic-update-slice_fusion.4
  197.2 71.7 %collective-permute-done.1 = f32[8,1024,128]{2,0,1:T(8,128)} collective-permute-done((f32[8,1024,128]{2,0,1:T(8,128)}, f32[8,1024,128]{2,0,1:T(8,128)}, u32[]{:S(2)}, u32[]{:S(2)}) %collective-permute-start.1) | collective-permute-done | bytes 4194336 | tf_op jit(solution)/shard_map/ppermute | solution.py:13
  268.8 2.5 constant_dynamic-update-slice_fusion.3
  271.3 2.4 constant_dynamic-update-slice_fusion.2
  273.8 2.5 constant_dynamic-update-slice_fusion.1
  276.3 131.3 %collective-permute-done.3 = f32[8,1024,128]{2,0,1:T(8,128)} collective-permute-done((f32[8,1024,128]{2,0,1:T(8,128)}, f32[8,1024,128]{2,0,1:T(8,128)}, u32[]{:S(2)}, u32[]{:S(2)}) %collective-permute-start.3) | collective-permute-done | bytes 4194336 | tf_op jit(solution)/shard_map/ppermute | solution.py:13
  407.6 2.5 constant_dynamic-update-slice_fusion
  410.0 13.2 %fusion = f32[8,2,1024,128]{3,0,2,1:T(8,128)} fusion(f32[40,1024,128]{2,0,1:T(8,128)S(1)} %constant_dynamic-update-slice_fusion, f32[8,40,2,1]{1,2,0,3:T(2,128)S(1)} %convolution_bitcast_fusion), kind=kOutput, calls=%fused_computation | convolution fusion | flops 1006632960 | bytes 29362688 | tf_op jit(solution)/shard_map/icl,cnk->ilnk/dot_general | solution.py:65
  423.3 8.7 %copy.25 = f32[8,2,1024,128]{2,3,0,1:T(8,128)} copy(f32[8,2,1024,128]{3,0,2,1:T(8,128)} %fusion) | data formatting | bytes 16777216 | tf_op jit(solution)/shard_map/icl,cnk->ilnk/dot_general | solution.py:65
  432.0 31.5 %fusion.4 = f32[8,2,1024,128]{2,3,0,1:T(8,128)} fusion(f32[8,2,1024,128]{2,3,0,1:T(8,128)} %copy.25, f32[2,2,1024,1024]{3,2,0,1:T(8,128)} %all-gather.2.cloned.1.call-done), kind=kOutput, calls=%fused_computation.9 | convolution fusion | flops 25769803776 | bytes 25165824 | tf_op jit(solution)/shard_map/lrb,clbk->clrk/dot_general | solution.py:20
  463.5 29.4 %fusion.5 = f32[8,2,1024,128]{2,3,0,1:T(8,128)} fusion(f32[8,2,1024,128]{2,3,0,1:T(8,128)S(1)} %copy-done.1, f32[2,2,1024,1024]{3,2,0,1:T(8,128)S(1)} %copy-done.4), kind=kOutput, calls=%fused_computation.10 | convolution fusion | flops 25769803776 | bytes 25165824 | tf_op jit(solution)/shard_map/lrb,clbk->clrk/dot_general | solution.py:21
  492.9 10.3 %slice_subtract_fusion = (f32[8,2,1024,64]{2,3,0,1:T(8,128)S(1)}, f32[8,2,1024,64]{2,3,0,1:T(8,128)}) fusion(f32[8,2,1024,128]{2,3,0,1:T(8,128)} %fusion.5, f32[8,2,1024,128]{2,3,0,1:T(8,128)} %fusion.4), kind=kLoop, calls=%fused_computation.8 | loop fusion | flops 2097152 | bytes 25165824 | tf_op jit(solution)/shard_map/sub | solution.py:24
  503.2 3.6 maximum_reduce_fusion
  506.9 2.4 neg.3
  509.3 1.9 constant_dynamic-slice_fusion.1
  511.2 0.3 copy.35
  511.5 0.3 copy.36
  511.9 0.6 fusion.14
  512.5 0.6 broadcast_subtract_fusion.1
  513.2 46.3 %reduce-scatter.2.cloned.1.call-done = f32[8,256,128]{1,2,0:T(8,128)} async-done(((f32[8,1024,128]{1,2,0:T(8,128)}), f32[8,256,128]{1,2,0:T(8,128)}) %reduce-scatter.2.cloned.1.call-update) | async-done | bytes 1048592 | tf_op jit(solution)/shard_map/reduce_scatter | solution.py:67
  559.5 2.0 slice_add_fusion.2
  561.5 0.1 pad_maximum_fusion
  561.6 1.3 copy.27
  (28 shorter events, 0.2 us)
Async XLA Ops:
  6.5 25.3 %copy-start.8 = (s32[8]{0:T(128)S(1)}, s32[8]{0:T(128)}, u32[]{:S(2)}) copy-start(s32[8]{0:T(128)} %param.13) | copy-start | bytes 100
  6.5 25.4 %copy-start.2 = (s32[8,16]{1,0:T(8,128)S(1)}, s32[8,16]{1,0:T(8,128)}, u32[]{:S(2)}) copy-start(s32[8,16]{1,0:T(8,128)} %param.12) | copy-start | bytes 1540
  6.5 25.4 %copy-start.5 = (f32[8,16,2]{1,2,0:T(2,128)S(1)}, f32[8,16,2]{1,2,0:T(2,128)}, u32[]{:S(2)}) copy-start(f32[8,16,2]{1,2,0:T(2,128)} %param.11) | copy-start | bytes 3076
  6.5 25.4 %copy-start.7 = (s32[8,16]{1,0:T(8,128)S(1)}, s32[8,16]{1,0:T(8,128)}, u32[]{:S(2)}) copy-start(s32[8,16]{1,0:T(8,128)} %param.14) | copy-start | bytes 1540
  6.5 25.4 %copy-start.6 = (s32[8,16]{1,0:T(8,128)S(1)}, s32[8,16]{1,0:T(8,128)}, u32[]{:S(2)}) copy-start(s32[8,16]{1,0:T(8,128)} %param.15) | copy-start | bytes 1540
  6.5 425.4 %all-gather.2.cloned.1.call-start = ((), (), s32[]{:S(2)}) async-start(), calls=%async_computation.1 | async-start | bytes 18874368 | tf_op jit(solution)/shard_map/all_gather | solution.py:17
  9.8 549.7 %reduce-scatter.2.cloned.1.call-start = ((), (), s32[]{:S(2)}) async-start(), calls=%async_computation.2 | async-start | bytes 5242880 | tf_op jit(solution)/shard_map/reduce_scatter | solution.py:67
  16.4 178.3 %collective-permute-start = (f32[8,1024,128]{2,0,1:T(8,128)}, f32[8,1024,128]{2,0,1:T(8,128)}, u32[]{:S(2)}, u32[]{:S(2)}) collective-permute-start(f32[8,1024,128]{2,0,1:T(8,128)} %copy.19), channel_id=1, source_target_pairs={{0,2},{1,3},{2,4},{3,5},{4,6},{5,7},{8,10},{9,11},{10,12},{11,13},... | collective-permute-start | bytes 12582920 | tf_op jit(solution)/shard_map/ppermute | solution.py:13
  23.3 245.5 %collective-permute-start.1 = (f32[8,1024,128]{2,0,1:T(8,128)}, f32[8,1024,128]{2,0,1:T(8,128)}, u32[]{:S(2)}, u32[]{:S(2)}) collective-permute-start(f32[8,1024,128]{2,0,1:T(8,128)} %copy.19), channel_id=1, source_target_pairs={{0,1},{1,2},{2,3},{3,4},{4,5},{5,6},{6,7},{8,9},{9,10},{10,11},{11... | collective-permute-start | bytes 12582920 | tf_op jit(solution)/shard_map/ppermute | solution.py:13
  28.7 245.0 %collective-permute-start.2 = (f32[8,1024,128]{2,0,1:T(8,128)}, f32[8,1024,128]{2,0,1:T(8,128)}, u32[]{:S(2)}, u32[]{:S(2)}) collective-permute-start(f32[8,1024,128]{2,0,1:T(8,128)} %copy.19), channel_id=1, source_target_pairs={{1,0},{2,1},{3,2},{4,3},{5,4},{6,5},{7,6},{9,8},{10,9},{11,10},{12... | collective-permute-start | bytes 12582920 | tf_op jit(solution)/shard_map/ppermute | solution.py:13
  30.0 377.6 %collective-permute-start.3 = (f32[8,1024,128]{2,0,1:T(8,128)}, f32[8,1024,128]{2,0,1:T(8,128)}, u32[]{:S(2)}, u32[]{:S(2)}) collective-permute-start(f32[8,1024,128]{2,0,1:T(8,128)} %copy.19), channel_id=1, source_target_pairs={{2,0},{3,1},{4,2},{5,3},{6,4},{7,5},{10,8},{11,9},{12,10},{13,11},... | collective-permute-start | bytes 12582920 | tf_op jit(solution)/shard_map/ppermute | solution.py:13
  32.2 239.1 %copy-start = (f32[8,1024,128]{2,1,0:T(8,128)S(1)}, f32[8,1024,128]{2,1,0:T(8,128)}, u32[]{:S(2)}) copy-start(f32[8,1024,128]{2,1,0:T(8,128)} %param.9) | copy-start | bytes 12582916
  432.0 31.5 %copy-start.1 = (f32[8,2,1024,128]{2,3,0,1:T(8,128)S(1)}, f32[8,2,1024,128]{2,3,0,1:T(8,128)}, u32[]{:S(2)}) copy-start(f32[8,2,1024,128]{2,3,0,1:T(8,128)} %copy.25) | copy-start | bytes 25165828
  432.0 31.5 %copy-start.4 = (f32[2,2,1024,1024]{3,2,0,1:T(8,128)S(1)}, f32[2,2,1024,1024]{3,2,0,1:T(8,128)}, u32[]{:S(2)}) copy-start(f32[2,2,1024,1024]{3,2,0,1:T(8,128)} %all-gather.2.cloned.1.call-done) | copy-start | bytes 50331652
  506.8 5.0 copy-start.3
  506.9 5.7 copy-start.9
Sparse Core Ops, SparseCore 0:
  9.9 372.5 all-gather.1
  509.4 50.0 reduce-scatter.1
where the time goes:
time: 574 us; the launch traced here: 570 us
  waiting for transfers between devices  412 us (72%)
  matrix products  74.4 us (13%)
  local copies, waits for them, and re-layouts  35.4 us (6%)
  other arithmetic  19.2 us (3%)
  starting transfers between devices  15.5 us (3%)
  between operations  13.9 us (2%)
    ppermute x4, waiting for transfers between devices, shifted(): return lax.ppermute(value, axis, pairs)  365 us
    reduce_scatter x1, waiting for transfers between devices, body(): summed = lax.psum_scatter(-coupled, 'mult', scatter_dimension=1, tiled=True)  46.3 us
    dot_general x1, matrix products, apply_panels(): jnp.einsum('lrb,clbk->clrk', real_panel, operand, precision=lax.Precision...  31.5 us
    dot_general x1, matrix products, apply_panels(): jnp.einsum('lrb,clbk->clrk', imag_panel, operand, precision=lax.Precision...  29.4 us
    unnamed x28, local copies, waits for them, and re-layouts  20.3 us
    ppermute x4, starting transfers between devices, shifted(): return lax.ppermute(value, axis, pairs)  15.4 us
    dot_general x1, matrix products, body(): jnp.einsum('icl,cnk->ilnk', mixing, window, precision=lax.Precision.HIGHEST)  13.2 us
  transfers between devices with their start and end apart: 6, of which 4 were waited for; matrix products, arithmetic and copies ran while one was open for 8% of the time, Pallas kernels for 0%

commit v1 on v0

v1 whole, which is shorter than its diff:
```python
import functools

import jax
import jax.numpy as jnp
from jax import lax
from jax.experimental import pallas as pl
from jax.experimental.pallas import tpu as pltpu
from jax.sharding import PartitionSpec as P


R = 2
SPAN = 2 * R + 1
LANES = 128
F32 = jnp.float32
BF16 = jnp.bfloat16


def ring_order(peers):
    return list(range(0, peers, 2)) + list(range(peers - 1 - peers % 2, 0, -2))


def ring_shift(value, axis, by):
    order = ring_order(lax.axis_size(axis))
    n = len(order)
    return lax.ppermute(value, axis, [(order[i], order[(i + by) % n]) for i in range(n)])


def flip(value, axis, bit):
    return lax.ppermute(value, axis, [(i, i ^ bit) for i in range(lax.axis_size(axis))])


def split(v):
    hi = v.astype(BF16)
    return hi, (v - hi.astype(F32)).astype(BF16)


def lane_group(shape, width):
    return lax.broadcasted_iota(jnp.int32, shape, len(shape) - 1) // width


def pack_kernel(sc_ref, col_ref, out_ref, *, kw):
    m = sc_ref[0]
    n_ch, rows, lanes = col_ref.shape
    groups = lanes // kw
    half = groups // 2
    grp = lane_group((rows, lanes), kw)
    re = im = None
    for j in range(n_ch):
        v = col_ref[j]
        if j:
            v = pltpu.roll(v, j * kw, 1)
        if re is None:
            re = im = v
        else:
            re = jnp.where(grp == lax.rem(m + j, groups), v, re)
            im = jnp.where(grp == lax.rem(m + half + j, groups), v, im)
    out_ref[:, :lanes] = pltpu.roll(re, lax.rem((groups - m) * kw, lanes), 1)
    out_ref[:, lanes:] = pltpu.roll(im, lax.rem((groups + half - m) * kw, lanes), 1)


def pack(columns, meta, kw):
    n_ch, nb, lanes = columns.shape
    steps = 4
    return pl.pallas_call(
        functools.partial(pack_kernel, kw=kw),
        out_shape=jax.ShapeDtypeStruct((nb, 2 * lanes), F32),
        grid_spec=pltpu.PrefetchScalarGridSpec(
            num_scalar_prefetch=1,
            grid=(steps,),
            in_specs=[pl.BlockSpec((n_ch, nb // steps, lanes), lambda g, sc: (0, g, 0))],
            out_specs=pl.BlockSpec((nb // steps, 2 * lanes), lambda g, sc: (g, 0)),
        ),
        name="pack",
    )(meta, columns)


def unit_kernel(sc_ref, *refs, n_p, kw, steps, places, fresh):
    n_x = len(places)
    p_refs, x_refs = refs[: 2 * n_p], refs[2 * n_p : 2 * (n_p + n_x)]
    a_refs = refs[2 * (n_p + n_x) : 3 * n_p + 2 * n_x]
    c_in, c_out, y_ref, w_ref, sem = refs[3 * n_p + 2 * n_x :]
    step = pl.program_id(0)
    n_l, _, rows, _ = p_refs[0].shape
    n_chan, n_ch, _ = a_refs[0].shape
    fetch = None if fresh else pltpu.make_async_copy(c_in, w_ref, sem.at[0])

    @pl.when(step == 0)
    def _():
        if fresh:
            w_ref[...] = jnp.zeros_like(w_ref)
        else:
            fetch.start()

    parts = []
    for part in range(2):
        v = jnp.concatenate(
            [
                jnp.concatenate([p_refs[2 * a + t][l, part] for t in range(2)], axis=1)
                for a in range(n_p)
                for l in range(n_l)
            ],
            axis=0,
        )
        h, l = split(v)
        parts += [h, h, l]
    lhs = jnp.concatenate(parts, axis=1)
    rhs = []
    for t in range(n_x):
        x = jnp.concatenate([x_refs[2 * t][...], x_refs[2 * t + 1][...]], axis=0)
        lanes = x.shape[1] // 2
        xh, xl = split(x)
        yh = jnp.concatenate([-xh[:, lanes:], xh[:, :lanes]], axis=1)
        yl = jnp.concatenate([-xl[:, lanes:], xl[:, :lanes]], axis=1)
        rhs.append(jnp.concatenate([xh, xl, xh, yh, yl, yh], axis=0))
    prod = jnp.dot(lhs, jnp.concatenate(rhs, axis=1), preferred_element_type=F32)
    for t in range(n_x):
        piece = prod[:, 2 * lanes * t : 2 * lanes * (t + 1)]

        @pl.when(step == 0)
        def _():
            y_ref[t] = piece

        @pl.when(step > 0)
        def _():
            y_ref[t] += piece

    @pl.when(step == steps - 1)
    def _():
        n = n_p * n_l
        wide = SPAN * lanes
        spread = (
            lane_group((LANES, wide), kw) == lax.broadcasted_iota(jnp.int32, (LANES, wide), 0)
        ).astype(BF16)
        same = (
            lax.broadcasted_iota(jnp.int32, (1, kw, wide), 2) % kw
            == lax.broadcasted_iota(jnp.int32, (1, kw, wide), 1)
        )
        grp = lane_group((n_ch, LANES), n_ch)

        def kron(c):
            t = jnp.dot(c, spread, preferred_element_type=F32)
            t = jnp.where(same, t[:, None, :], 0.0)
            return t.reshape(n * n_ch * kw, wide).astype(BF16)

        if not fresh:
            fetch.wait()

        @pl.loop(0, n_x)
        def _(t):
            s = sc_ref[places[0] + t]
            coef = []
            for a_ref in a_refs:
                v = None
                for d in range(SPAN):
                    at = s + d - R
                    own = a_ref[jnp.clip(at, 0, n_chan - 1)]
                    own = jnp.where((at >= 0) & (at < n_chan), own, 0.0)
                    v = own if v is None else jnp.where(lax.rem(grp, LANES // n_l // n_ch) == d, own, v)
                coef += [pltpu.roll(v, LANES - l * (LANES // n_l), 1) if l else v for l in range(n_l)]
            ch, cl = split(jnp.concatenate(coef, axis=0))
            kh, kl = kron(ch), kron(cl)
            y = y_ref[t]
            z = jnp.concatenate(
                [
                    jnp.concatenate(
                        [y[i * rows : (i + 1) * rows, part * lanes : (part + 1) * lanes] for i in range(n)],
                        axis=1,
                    )
                    for part in range(2)
                ],
                axis=0,
            )
            zh, zl = split(z)
            out = jnp.dot(
                jnp.concatenate([zh, zh, zl], axis=1),
                jnp.concatenate([kh, kl, kh], axis=0),
                preferred_element_type=F32,
            )
            for d in range(SPAN):
                w_ref[s + d] += out[:, d * lanes : (d + 1) * lanes]

        back = pltpu.make_async_copy(w_ref, c_out, sem.at[1])
        back.start()
        back.wait()


def unit(total, shape, panel_sets, coefs, chunks, meta, kw):
    n_l, _, rows, nb = panel_sets[0].shape
    half = nb // 2
    steps = max(1, half // LANES)
    blk = half // steps
    wide = chunks[0][0].shape[1]
    n = len(panel_sets)
    in_specs, args = [], []
    for p in panel_sets:
        in_specs += [
            pl.BlockSpec((n_l, 2, rows, blk), lambda g, sc: (0, 0, 0, g)),
            pl.BlockSpec((n_l, 2, rows, blk), lambda g, sc: (0, 0, 0, steps + g)),
        ]
        args += [p, p]
    for top, bottom, _ in chunks:
        off = steps if bottom.shape[0] == nb else 0
        in_specs += [
            pl.BlockSpec((blk, wide), lambda g, sc: (g, 0)),
            pl.BlockSpec((blk, wide), lambda g, sc, off=off: (off + g, 0)),
        ]
        args += [top, bottom]
    fresh = total is None
    if fresh:
        total = coefs[0]
    in_specs += [pl.BlockSpec(c.shape, lambda g, sc: (0, 0, 0)) for c in coefs]
    in_specs += [pl.BlockSpec(memory_space=pltpu.HBM)]
    args += [*coefs, total]
    flops = 2 * 3 * n * n_l * rows * wide * (2 * nb + SPAN * LANES) * len(chunks)
    return pl.pallas_call(
        functools.partial(
            unit_kernel, n_p=n, kw=kw, steps=steps, places=tuple(c[2] for c in chunks), fresh=fresh
        ),
        out_shape=jax.ShapeDtypeStruct(shape, F32),
        grid_spec=pltpu.PrefetchScalarGridSpec(
            num_scalar_prefetch=1,
            grid=(steps,),
            in_specs=in_specs,
            out_specs=pl.BlockSpec(memory_space=pltpu.HBM),
            scratch_shapes=[
                pltpu.VMEM((len(chunks), n * n_l * rows, wide), F32),
                pltpu.VMEM(shape, F32),
                pltpu.SemaphoreType.DMA((2,)),
            ],
        ),
        input_output_aliases={} if fresh else {len(args): 0},
        cost_estimate=pl.CostEstimate(
            flops=flops, transcendentals=0, bytes_accessed=4 * n * n_l * 2 * rows * nb
        ),
        compiler_params=pltpu.CompilerParams(vmem_limit_bytes=48 << 20),
        name="unit",
    )(meta, *[pltpu.with_memory_space_constraint(a, pltpu.HBM) for a in args])


def finish_kernel(sc_ref, energy_ref, contour_ref, col_ref, *refs, kw, n_mult):
    pieces, out_ref, held = refs[:-2], refs[-2], refs[-1]
    n_ch, _, lanes = col_ref.shape
    n = len(pieces)
    per = n // n_mult
    me = sc_ref[1]
    for s in range(n):
        held[lax.rem(me - s + n, n)] = pieces[s][...]
    rows = pieces[0].shape[0] // 2
    groups = 2 * n_mult
    grp = lane_group((rows, lanes), kw)
    upper = lax.broadcasted_iota(jnp.int32, (rows, lanes), 1) >= lanes // 2
    shift = contour_ref[1]
    for h in range(per):
        vs = [held[u * per + h, part * rows : (part + 1) * rows] for part in range(2) for u in range(n_mult)]
        dist = 1
        while dist < groups:
            odd = (grp // dist) % 2 == 1
            nxt = list(vs)
            for a in range(groups):
                if not a & dist:
                    b = a + dist
                    nxt[a] = jnp.where(odd, pltpu.roll(vs[b], dist * kw, 1), vs[a])
                    nxt[b] = jnp.where(odd, vs[b], pltpu.roll(vs[a], lanes - dist * kw, 1))
            vs = nxt
            dist *= 2
        at = pl.ds(h * rows, rows)
        for i in range(n_ch):
            x = col_ref[i, at]
            turned = pltpu.roll(x, lanes // 2, 1)
            turned = jnp.where(upper, turned, -turned)
            out_ref[i, at] = (contour_ref[0] - energy_ref[i]) * x + shift * turned - vs[i]


def finish(pieces, columns, energies, contour, meta, kw, n_mult):
    n_ch, nb, lanes = columns.shape
    out_rows = nb // n_mult
    smem = pl.BlockSpec(memory_space=pltpu.SMEM)
    return pl.pallas_call(
        functools.partial(finish_kernel, kw=kw, n_mult=n_mult),
        out_shape=jax.ShapeDtypeStruct((n_ch, out_rows, lanes), F32),
        grid_spec=pltpu.PrefetchScalarGridSpec(
            num_scalar_prefetch=1,
            grid=(1,),
            in_specs=[smem, smem, pl.BlockSpec((n_ch, out_rows, lanes), lambda g, sc: (0, sc[0], 0))]
            + [pl.BlockSpec(p.shape, lambda g, sc: (0, 0)) for p in pieces],
            out_specs=pl.BlockSpec((n_ch, out_rows, lanes), lambda g, sc: (0, 0, 0)),
            scratch_shapes=[pltpu.VMEM((len(pieces),) + pieces[0].shape, F32)],
        ),
        name="finish",
    )(meta, energies, contour, columns, *pieces)


def mixing_blocks(coefficients, channel_cols, used_slots, lambda_low, lambda_high, chan_index, mult_index):
    n_ch, slots, lam = coefficients.shape
    n_chan = lax.axis_size("chan")
    local = channel_cols - (chan_index - R) * n_ch
    slot_ids = jnp.arange(slots, dtype=jnp.int32)
    live = slot_ids[None, :] < used_slots[:, None]
    lambda_ids = mult_index * lam + jnp.arange(lam, dtype=jnp.int32)
    inside = (lambda_ids >= lambda_low[:, :, None]) & (lambda_ids < lambda_high[:, :, None])
    weights = jnp.where(live[:, :, None] & inside, coefficients, jnp.zeros_like(coefficients))
    lane = jnp.arange(LANES, dtype=jnp.int32)
    stride = LANES // lam
    order, dist = lane // stride, (lane % stride) // n_ch
    want = (SPAN - 1 - dist)[None, :] * n_ch + jnp.arange(n_ch, dtype=jnp.int32)[:, None]
    want = jnp.where(dist[None, :] < SPAN, want, -1)
    by_lane = jnp.tile(local.T, (1, LANES // n_ch))
    w_lane = jnp.zeros((slots, LANES), F32)
    for l in range(lam):
        w_lane = jnp.where(order[None, :] == l, jnp.tile(weights[:, :, l].T, (1, LANES // n_ch)), w_lane)
    mine = jnp.sum(
        jnp.where(by_lane[:, None, :] == want[None], w_lane[:, None, :], 0.0), axis=0
    )
    return jnp.broadcast_to(mine[None], (n_chan,) + mine.shape)


def steps_of(n_chan):
    full = (n_chan - 1) // 2
    return full, max(1, min(2, full - 1))


def body(
    columns,
    panels,
    coefficients,
    channel_cols,
    used_slots,
    lambda_low,
    lambda_high,
    energies,
    contour,
):
    _, nb, lanes = columns.shape
    n_chan, n_mult = lax.axis_size("chan"), lax.axis_size("mult")
    chan_index, mult_index = lax.axis_index("chan"), lax.axis_index("mult")
    kw = lanes // 2 // n_mult
    rows = panels.shape[2]

    seq = ring_order(n_chan)
    hops = [0]
    for step in range(1, n_chan // 2 + 1):
        hops += [-step, step]
    table = jnp.asarray(
        [[i] + [seq[(seq.index(i) + by) % n_chan] for by in hops] for i in range(n_chan)], jnp.int32
    )
    meta = jnp.concatenate([mult_index[None], table[chan_index]])

    def spot(by):
        return 2 + hops.index(by)

    sent = mixing_blocks(
        coefficients, channel_cols, used_slots, lambda_low, lambda_high, chan_index, mult_index
    )
    sent, meta = lax.optimization_barrier((sent, meta))
    near_coefs = [lax.all_to_all(sent, "chan", 0, 0, tiled=True)]
    near_coefs[0], meta = lax.optimization_barrier((near_coefs[0], meta))
    mine = pack(columns, meta, kw)

    near_sets = [panels]
    bit = n_mult // 4
    while bit:
        near_sets += [flip(p, "mult", bit) for p in near_sets]
        near_coefs += [flip(p, "mult", bit) for p in near_coefs]
        bit //= 2
    far = [flip(panels, "mult", n_mult // 2)]
    far_coefs = [flip(c, "mult", n_mult // 2) for c in near_coefs]

    shape = (n_chan + 2 * R, 2 * rows, LANES)

    def add(total, sets, coefs, chunks):
        return unit(total, shape, sets, coefs, chunks, meta, kw)

    full_steps, switch = steps_of(n_chan)
    total = None
    ahead = behind = mine
    held = [(mine, mine, spot(0))]
    total = add(total, near_sets, near_coefs, held)
    for step in range(1, full_steps + 1):
        ahead = ring_shift(ahead, "chan", 1)
        behind = ring_shift(behind, "chan", -1)
        new = [(ahead, ahead, spot(-step)), (behind, behind, spot(step))]
        if step <= switch:
            total = add(total, near_sets, near_coefs, new)
            held += new
        else:
            total = add(total, near_sets + far, near_coefs + far_coefs, new)
        if step == switch:
            far[0], total = lax.optimization_barrier((far[0], total))
            bit = n_mult // 4
            while bit:
                far += [flip(p, "mult", bit) for p in far]
                bit //= 2
            for at in range(0, len(held), 3):
                total = add(total, far, far_coefs, held[at : at + 3])
    if n_chan % 2 == 0:
        top = ring_shift(ahead[: nb // 2], "chan", 1)
        bottom = ring_shift(behind[nb // 2 :], "chan", -1)
        total = add(total, near_sets + far, near_coefs + far_coefs, [(top, bottom, spot(n_chan // 2))])

    per = n_chan // n_mult
    mine_q = mult_index * per + lax.rem(chan_index, per)
    pieces = []
    for s in range(n_chan):
        pairs = []
        for m in range(n_mult):
            for c in range(n_chan):
                q = m * per + c % per
                pairs.append((m * n_chan + c, (c // per) * n_chan + (q + s) % n_chan))
        piece = lax.dynamic_index_in_dim(total, R + lax.rem(mine_q + s, n_chan), 0, keepdims=False)
        pieces.append(lax.ppermute(piece, ("mult", "chan"), pairs))
    return finish(pieces, columns, energies, contour, meta, kw, n_mult)


def solution(mesh):
    return jax.shard_map(
        body,
        mesh=mesh,
        in_specs=(
            P("chan", None, None),
            P("mult", None, "chan", None),
            P("chan", None, "mult"),
            P("chan", None),
            P("chan"),
            P("chan", None),
            P("chan", None),
            P("chan"),
            P(),
        ),
        out_specs=P("chan", "mult", None),
        check_vma=False,
    )
```

time: 574 us -> 204 us (0.36)
  the two profiles are of different devices: /device:TPU:0 before, /device:TPU:14 now
where the time goes in v1:
time: 204 us; the launch traced here: 203 us
  Pallas kernels  85.9 us (42%)
  waiting for transfers between devices  66.6 us (33%)
  starting transfers between devices  25.2 us (12%)
  local copies, waits for them, and re-layouts  11.7 us (6%)
  blocking collectives  10.4 us (5%)
  other arithmetic  2.99 us (1%)
    pallas_call x7, Pallas kernels, unit(): pl.pallas_call(functools.partial(unit_kernel, n_p=n, kw=kw, steps=steps,...  75.9 us
    ppermute x8, waiting for transfers between devices, ring_shift(): lax.ppermute(value, axis, [(order[i], order[(i + by) % n]) for i in range...  46.4 us
    ppermute x8, waiting for transfers between devices, body(): pieces.append(lax.ppermute(piece, ('mult', 'chan'), pairs))  19 us
    ppermute x8, starting transfers between devices, body(): pieces.append(lax.ppermute(piece, ('mult', 'chan'), pairs))  14.1 us
    all_to_all x1, blocking collectives, body(): near_coefs = [lax.all_to_all(sent, 'chan', 0, 0, tiled=True)]  10.4 us
    ppermute x8, starting transfers between devices, ring_shift(): lax.ppermute(value, axis, [(order[i], order[(i + by) % n]) for i in range...  8.44 us
    unnamed x50, local copies, waits for them, and re-layouts  8.37 us
    pallas_call x1, Pallas kernels, pack(): pl.pallas_call(functools.partial(pack_kernel, kw=kw), out_shape=jax.Shape...  5.6 us
  transfers between devices with their start and end apart: 22, of which 11 were waited for; matrix products, arithmetic and copies ran while one was open for 2% of the time, Pallas kernels for 35%

profile of v1, /device:TPU:14, one launch (start us, length us, event | category | flops | bytes accessed | tf_op | source)
XLA Modules:
  0.0 203.1 jit_solution(4971355625140947185)
XLA Ops:
  3.9 10.4 %all_to_all.5.refs_6_.refs_8_.refs_12_.refs_10_ = f32[8,8,128]{2,1,0:T(8,128)S(1)} all-to-all(f32[8,8,128]{2,1,0:T(8,128)S(1)} %broadcast_in_dim.74), channel_id=1, replica_groups=mesh['mult'=4,'chan'=8] {'chan'}, dimensions={0} | all-to-all | bytes 65536 | tf_op jit(solution)/shard_map/all_to_all | solution.py:355
  14.3 5.6 %pack.1.refs_4_.refs_5_ = f32[1024,256]{1,0:T(8,128)} custom-call(s32[11]{0:T(128)} %pad_add_fusion.sc_ref, f32[8,1024,128]{2,1,0:T(8,128)} %col_ref.3), custom_call_target="tpu_custom_call" | custom-call | tf_op jit(solution)/shard_map/pack/pallas_call | solution.py:64
  19.9 1.3 collective-permute-start.2
  22.4 21.8 %collective-permute-done.2.refs_4_.refs_5_.refs_6_.refs_7_ = f32[1024,256]{1,0:T(8,128)S(1)} collective-permute-done((f32[1024,256]{1,0:T(8,128)}, f32[1024,256]{1,0:T(8,128)S(1)}, u32[]{:S(2)}, u32[]{:S(2)}) %collective-permute-start.2) | collective-permute-done | bytes 1048608 | tf_op jit(solution)/shard_map/ppermute | solution.py:25
  44.2 1.5 collective-permute-start.3
  46.3 1.2 collective-permute-done.6.refs_7_.refs_9_.refs_13_.refs_11_
  48.1 6.5 %unit.7.refs_10_ = f32[12,256,128]{2,1,0:T(8,128)S(1)} custom-call(s32[11]{0:T(128)S(1)} %copy-done.1, f32[2,2,128,1024]{3,2,1,0:T(8,128)} %refs_1_.9, f32[2,2,128,1024]{3,2,1,0:T(8,128)} %refs_1_.9, f32[2,2,128,1024]{3,2,1,0:T(8,128)} %collective-permute-done.refs_2_.refs_3_, f32[2,2,128,1024]{3,2,1,0:T(8,128)} %collective-permute-done.refs_2_.refs_3_, ...), custom_call_target="tpu_custom_call" | custom-call | flops 2113929216 | bytes 4194304 | tf_op jit(solution)/shard_map/unit/pallas_call | solution.py:215
  54.6 1.2 copy-done
  55.8 10.1 %unit.8.refs_10_ = f32[12,256,128]{2,1,0:T(8,128)} custom-call(s32[11]{0:T(128)S(1)} %copy-done.1, f32[2,2,128,1024]{3,2,1,0:T(8,128)} %refs_1_.9, f32[2,2,128,1024]{3,2,1,0:T(8,128)} %refs_1_.9, f32[2,2,128,1024]{3,2,1,0:T(8,128)} %collective-permute-done.refs_2_.refs_3_, ...), custom_call_target="tpu_custom_call", output_to_operand_aliasing={{}: (11, {})} | custom-call | flops 4227858432 | bytes 4194304 | tf_op jit(solution)/shard_map/unit/pallas_call | solution.py:215
  66.0 1.6 collective-permute-done.3.refs_4_.refs_5_
  67.6 1.3 collective-permute-done.5.refs_6_.refs_7_
  70.0 10.2 %unit.9.refs_12_ = f32[12,256,128]{2,1,0:T(8,128)} custom-call(s32[11]{0:T(128)S(1)} %copy-done.1, f32[2,2,128,1024]{3,2,1,0:T(8,128)} %refs_1_.9, f32[2,2,128,1024]{3,2,1,0:T(8,128)} %refs_1_.9, f32[2,2,128,1024]{3,2,1,0:T(8,128)} %collective-permute-done.refs_2_.refs_3_, ...), custom_call_target="tpu_custom_call", output_to_operand_aliasing={{}: (11, {})} | custom-call | flops 4227858432 | bytes 4194304 | tf_op jit(solution)/shard_map/unit/pallas_call | solution.py:215
  81.0 1.4 collective-permute-start.8
  82.9 1.5 collective-permute-start.13
  84.4 21.7 %collective-permute-done.10.refs_10_.refs_11_ = f32[1024,256]{1,0:T(8,128)S(1)} collective-permute-done((f32[1024,256]{1,0:T(8,128)}, f32[1024,256]{1,0:T(8,128)S(1)}, u32[]{:S(2)}, u32[]{:S(2)}) %collective-permute-start.10) | collective-permute-done | bytes 1048608 | tf_op jit(solution)/shard_map/ppermute | solution.py:25
  108.8 1.6 collective-permute-start.9
  111.1 1.4 copy-done.3
  112.5 12.9 %unit.10.refs_10_ = f32[12,256,128]{2,1,0:T(8,128)} custom-call(s32[11]{0:T(128)S(1)} %copy-done.1, f32[2,2,128,1024]{3,2,1,0:T(8,128)} %collective-permute-done.1.refs_0_.refs_1_.refs_4_.refs_5_, f32[2,2,128,1024]{3,2,1,0:T(8,128)} %collective-permute-done.1.refs_0_.refs_1_.refs_4_.refs_5_, ...), custom_call_target="tpu_custom_call", output_to_operand_aliasing={{}: (13, {})} | custom-call | flops 6341787648 | bytes 4194304 | tf_op jit(solution)/shard_map/unit/pallas_call | solution.py:215
  125.4 10.1 %unit.11.refs_16_ = f32[12,256,128]{2,1,0:T(8,128)} custom-call(s32[11]{0:T(128)S(1)} %copy-done.1, f32[2,2,128,1024]{3,2,1,0:T(8,128)} %collective-permute-done.1.refs_0_.refs_1_.refs_4_.refs_5_, f32[2,2,128,1024]{3,2,1,0:T(8,128)} %collective-permute-done.1.refs_0_.refs_1_.refs_4_.refs_5_, ...), custom_call_target="tpu_custom_call", output_to_operand_aliasing={{}: (11, {})} | custom-call | flops 4227858432 | bytes 4194304 | tf_op jit(solution)/shard_map/unit/pallas_call | solution.py:215
  135.5 15.5 %unit.12.refs_14_ = f32[12,256,128]{2,1,0:T(8,128)} custom-call(s32[11]{0:T(128)S(1)} %copy-done.1, f32[2,2,128,1024]{3,2,1,0:T(8,128)} %refs_1_.9, f32[2,2,128,1024]{3,2,1,0:T(8,128)} %refs_1_.9, f32[2,2,128,1024]{3,2,1,0:T(8,128)} %collective-permute-done.refs_2_.refs_3_, ...), custom_call_target="tpu_custom_call", output_to_operand_aliasing={{}: (17, {})} | custom-call | flops 8455716864 | bytes 8388608 | tf_op jit(solution)/shard_map/unit/pallas_call | solution.py:215
  152.7 10.5 %unit.13 = f32[12,256,128]{2,1,0:T(8,128)} custom-call(s32[11]{0:T(128)S(1)} %copy-done.1, f32[2,2,128,1024]{3,2,1,0:T(8,128)} %refs_1_.9, f32[2,2,128,1024]{3,2,1,0:T(8,128)} %refs_1_.9, f32[2,2,128,1024]{3,2,1,0:T(8,128)} %collective-permute-done.refs_2_.refs_3_, ...), custom_call_target="tpu_custom_call", output_to_operand_aliasing={{}: (15, {})} | custom-call | flops 4227858432 | bytes 8388608 | tf_op jit(solution)/shard_map/unit/pallas_call | solution.py:215
  163.2 1.4 dynamic-slice_bitcast_fusion
  164.6 1.9 collective-permute-start.14
  166.5 2.7 %collective-permute-start.15 = (f32[256,128]{1,0:T(8,128)S(1)}, f32[256,128]{1,0:T(8,128)S(1)}, u32[]{:S(2)}, u32[]{:S(2)}) collective-permute-start(f32[256,128]{1,0:T(8,128)S(1)} %get-tuple-element.23), channel_id=1, source_target_pairs={{0,1},{1,2},{2,9},{3,10},{4,17},{5,18},{6,25},{7,26},{8,3},{9,4},{... | collective-permute-start | bytes 393224 | tf_op jit(solution)/shard_map/ppermute | solution.py:410
  170.3 2.7 %collective-permute-start.17 = (f32[256,128]{1,0:T(8,128)S(1)}, f32[256,128]{1,0:T(8,128)S(1)}, u32[]{:S(2)}, u32[]{:S(2)}) collective-permute-start(f32[256,128]{1,0:T(8,128)S(1)} %get-tuple-element.21), channel_id=1, source_target_pairs={{0,3},{1,4},{2,11},{3,12},{4,19},{5,20},{6,27},{7,28},{8,5},{9,6},... | collective-permute-start | bytes 393224 | tf_op jit(solution)/shard_map/ppermute | solution.py:410
  173.1 1.4 collective-permute-start.18
  174.5 2.5 %collective-permute-done.14.refs_0_ = f32[256,128]{1,0:T(8,128)S(1)} collective-permute-done((f32[256,128]{1,0:T(8,128)S(1)}, f32[256,128]{1,0:T(8,128)S(1)}, u32[]{:S(2)}, u32[]{:S(2)}) %collective-permute-start.14) | collective-permute-done | bytes 131104 | tf_op jit(solution)/shard_map/ppermute | solution.py:410
  177.0 8.7 %collective-permute-done.15.refs_1_ = f32[256,128]{1,0:T(8,128)S(1)} collective-permute-done((f32[256,128]{1,0:T(8,128)S(1)}, f32[256,128]{1,0:T(8,128)S(1)}, u32[]{:S(2)}, u32[]{:S(2)}) %collective-permute-start.15) | collective-permute-done | bytes 131104 | tf_op jit(solution)/shard_map/ppermute | solution.py:410
  185.7 4.2 %collective-permute-start.21 = (f32[256,128]{1,0:T(8,128)S(1)}, f32[256,128]{1,0:T(8,128)S(1)}, u32[]{:S(2)}, u32[]{:S(2)}) collective-permute-start(f32[256,128]{1,0:T(8,128)S(1)} %get-tuple-element.17), channel_id=1, source_target_pairs={{0,7},{1,0},{2,15},{3,8},{4,23},{5,16},{6,31},{7,24},{8,1},{9,2},{... | collective-permute-start | bytes 393224 | tf_op jit(solution)/shard_map/ppermute | solution.py:410
  190.0 4.5 %collective-permute-done.18.refs_4_ = f32[256,128]{1,0:T(8,128)S(1)} collective-permute-done((f32[256,128]{1,0:T(8,128)S(1)}, f32[256,128]{1,0:T(8,128)S(1)}, u32[]{:S(2)}, u32[]{:S(2)}) %collective-permute-start.18) | collective-permute-done | bytes 131104 | tf_op jit(solution)/shard_map/ppermute | solution.py:410
  194.6 2.8 %collective-permute-done.19.refs_5_ = f32[256,128]{1,0:T(8,128)S(1)} collective-permute-done((f32[256,128]{1,0:T(8,128)S(1)}, f32[256,128]{1,0:T(8,128)S(1)}, u32[]{:S(2)}, u32[]{:S(2)}) %collective-permute-start.19) | collective-permute-done | bytes 131104 | tf_op jit(solution)/shard_map/ppermute | solution.py:410
  198.7 4.4 %finish.1 = f32[8,256,128]{2,1,0:T(8,128)} custom-call(s32[11]{0:T(128)} %pad_add_fusion.sc_ref, f32[8]{0:T(128)} %energy_ref.1, f32[2]{0:T(128)} %contour_ref.1, f32[8,1024,128]{2,1,0:T(8,128)} %col_ref.3, f32[256,128]{1,0:T(8,128)} %copy-done.17, f32[256,128]{1,0:T(8,128)} %copy-done.18, f32[256,128]{1,0:T(8,128)} %copy-done.19, f32[256,128]{1,0:T(8,128)} %copy-done.20, ...), custom_call_target="tpu_custom_call" | custom-call | tf_op jit(solution)/shard_map/finish/pallas_call | solution.py:278
  (92 shorter events, 16.2 us)
Async XLA Ops:
  0.0 47.5 %collective-permute-start = (f32[2,2,128,1024]{3,2,1,0:T(8,128)}, f32[2,2,128,1024]{3,2,1,0:T(8,128)}, u32[]{:S(2)}, u32[]{:S(2)}) collective-permute-start(f32[2,2,128,1024]{3,2,1,0:T(8,128)} %refs_1_.9), channel_id=1, source_target_pairs={{0,8},{8,0},{16,24},{24,16},{1,9},{9,1},{17,25},{25,17},{2,10},{10... | collective-permute-start | bytes 6291464 | tf_op jit(solution)/shard_map/ppermute | solution.py:29
  14.3 32.0 %copy-start.8 = (f32[8,8,128]{2,1,0:T(8,128)}, f32[8,8,128]{2,1,0:T(8,128)S(1)}, u32[]{:S(2)}) copy-start(f32[8,8,128]{2,1,0:T(8,128)S(1)} %all_to_all.5.refs_6_.refs_8_.refs_12_.refs_10_) | copy-start | bytes 98308
  14.3 33.8 %copy-start.1 = (s32[11]{0:T(128)S(1)}, s32[11]{0:T(128)}, u32[]{:S(2)}) copy-start(s32[11]{0:T(128)} %pad_add_fusion.sc_ref) | copy-start | bytes 136
  19.9 24.4 %collective-permute-start.2 = (f32[1024,256]{1,0:T(8,128)}, f32[1024,256]{1,0:T(8,128)S(1)}, u32[]{:S(2)}, u32[]{:S(2)}) collective-permute-start(f32[1024,256]{1,0:T(8,128)} %pack.1.refs_4_.refs_5_), channel_id=1, source_target_pairs={{0,2},{2,4},{4,6},{6,7},{7,5},{5,3},{3,1},{1,0},{8,10},{10,12},{12... | collective-permute-start | bytes 3145736 | tf_op jit(solution)/shard_map/ppermute | solution.py:25
  21.2 24.5 %collective-permute-start.4 = (f32[1024,256]{1,0:T(8,128)}, f32[1024,256]{1,0:T(8,128)S(1)}, u32[]{:S(2)}, u32[]{:S(2)}) collective-permute-start(f32[1024,256]{1,0:T(8,128)} %pack.1.refs_4_.refs_5_), channel_id=1, source_target_pairs={{0,1},{2,0},{4,2},{6,4},{7,6},{5,7},{3,5},{1,3},{8,9},{10,8},{12,1... | collective-permute-start | bytes 3145736 | tf_op jit(solution)/shard_map/ppermute | solution.py:25
  21.9 58.3 %collective-permute-start.1 = (f32[2,2,128,1024]{3,2,1,0:T(8,128)S(1)}, f32[2,2,128,1024]{3,2,1,0:T(8,128)}, u32[]{:S(2)}, u32[]{:S(2)}) collective-permute-start(f32[2,2,128,1024]{3,2,1,0:T(8,128)S(1)} %copy-done.2), channel_id=1, source_target_pairs={{0,16},{8,24},{16,0},{24,8},{1,17},{9,25},{17,1},{25,9},{2,18},{10... | collective-permute-start | bytes 6291464 | tf_op jit(solution)/shard_map/ppermute | solution.py:29
  44.2 10.4 %copy-start.6 = (f32[1024,256]{1,0:T(8,128)}, f32[1024,256]{1,0:T(8,128)S(1)}, u32[]{:S(2)}) copy-start(f32[1024,256]{1,0:T(8,128)S(1)} %collective-permute-done.2.refs_4_.refs_5_.refs_6_.refs_7_) | copy-start | bytes 3145732
  44.2 23.4 %collective-permute-start.3 = (f32[1024,256]{1,0:T(8,128)S(1)}, f32[1024,256]{1,0:T(8,128)S(1)}, u32[]{:S(2)}, u32[]{:S(2)}) collective-permute-start(f32[1024,256]{1,0:T(8,128)S(1)} %collective-permute-done.2.refs_4_.refs_5_.refs_6_.refs_7_), channel_id=1, source_target_pairs={{0,2},{2,4},{4,6},{6,7},{7,5},{5,3},{3,1},{1,0},{8,10},{10,12},{12... | collective-permute-start | bytes 3145736 | tf_op jit(solution)/shard_map/ppermute | solution.py:25
  45.7 8.9 %copy-start.7 = (f32[1024,256]{1,0:T(8,128)}, f32[1024,256]{1,0:T(8,128)S(1)}, u32[]{:S(2)}) copy-start(f32[1024,256]{1,0:T(8,128)S(1)} %collective-permute-done.4.refs_6_.refs_7_.refs_8_.refs_9_) | copy-start | bytes 3145732
  45.7 23.2 %collective-permute-start.5 = (f32[1024,256]{1,0:T(8,128)S(1)}, f32[1024,256]{1,0:T(8,128)S(1)}, u32[]{:S(2)}, u32[]{:S(2)}) collective-permute-start(f32[1024,256]{1,0:T(8,128)S(1)} %collective-permute-done.4.refs_6_.refs_7_.refs_8_.refs_9_), channel_id=1, source_target_pairs={{0,1},{2,0},{4,2},{6,4},{7,6},{5,7},{3,5},{1,3},{8,9},{10,8},{12,1... | collective-permute-start | bytes 3145736 | tf_op jit(solution)/shard_map/ppermute | solution.py:25
  46.3 1.2 collective-permute-start.6
  66.0 16.4 %copy-start.9 = (f32[8,8,128]{2,1,0:T(8,128)S(1)}, f32[8,8,128]{2,1,0:T(8,128)}, u32[]{:S(2)}) copy-start(f32[8,8,128]{2,1,0:T(8,128)} %copy-done.8) | copy-start | bytes 98308
  66.0 16.9 %copy-start.11 = (f32[8,8,128]{2,1,0:T(8,128)S(1)}, f32[8,8,128]{2,1,0:T(8,128)}, u32[]{:S(2)}) copy-start(f32[8,8,128]{2,1,0:T(8,128)} %copy-done.10) | copy-start | bytes 98308
  80.2 30.3 %collective-permute-start.7 = (f32[2,2,128,1024]{3,2,1,0:T(8,128)}, f32[2,2,128,1024]{3,2,1,0:T(8,128)S(1)}, u32[]{:S(2)}, u32[]{:S(2)}) collective-permute-start(f32[2,2,128,1024]{3,2,1,0:T(8,128)} %collective-permute-done.1.refs_0_.refs_1_.refs_4_.refs_5_), channel_id=1, source_target_pairs={{0,8},{8,0},{16,24},{24,16},{1,9},{9,1},{17,25},{25,17},{2,10},{10... | collective-permute-start | bytes 6291464 | tf_op jit(solution)/shard_map/ppermute | solution.py:29
  80.3 25.8 %collective-permute-start.10 = (f32[1024,256]{1,0:T(8,128)}, f32[1024,256]{1,0:T(8,128)S(1)}, u32[]{:S(2)}, u32[]{:S(2)}) collective-permute-start(f32[1024,256]{1,0:T(8,128)} %copy-done.5), channel_id=1, source_target_pairs={{0,1},{2,0},{4,2},{6,4},{7,6},{5,7},{3,5},{1,3},{8,9},{10,8},{12,1... | collective-permute-start | bytes 3145736 | tf_op jit(solution)/shard_map/ppermute | solution.py:25
  81.0 26.8 %collective-permute-start.8 = (f32[1024,256]{1,0:T(8,128)}, f32[1024,256]{1,0:T(8,128)}, u32[]{:S(2)}, u32[]{:S(2)}) collective-permute-start(f32[1024,256]{1,0:T(8,128)} %copy-done.4), channel_id=1, source_target_pairs={{0,2},{2,4},{4,6},{6,7},{7,5},{5,3},{3,1},{1,0},{8,10},{10,12},{12... | collective-permute-start | bytes 3145736 | tf_op jit(solution)/shard_map/ppermute | solution.py:25
  82.4 28.1 %collective-permute-start.12 = (f32[8,8,128]{2,1,0:T(8,128)S(1)}, f32[8,8,128]{2,1,0:T(8,128)S(1)}, u32[]{:S(2)}, u32[]{:S(2)}) collective-permute-start(f32[8,8,128]{2,1,0:T(8,128)S(1)} %copy-done.9), channel_id=1, source_target_pairs={{0,16},{8,24},{16,0},{24,8},{1,17},{9,25},{17,1},{25,9},{2,18},{10... | collective-permute-start | bytes 98312 | tf_op jit(solution)/shard_map/ppermute | solution.py:29
  82.9 27.6 %collective-permute-start.13 = (f32[8,8,128]{2,1,0:T(8,128)S(1)}, f32[8,8,128]{2,1,0:T(8,128)S(1)}, u32[]{:S(2)}, u32[]{:S(2)}) collective-permute-start(f32[8,8,128]{2,1,0:T(8,128)S(1)} %copy-done.11), channel_id=1, source_target_pairs={{0,16},{8,24},{16,0},{24,8},{1,17},{9,25},{17,1},{25,9},{2,18},{10... | collective-permute-start | bytes 98312 | tf_op jit(solution)/shard_map/ppermute | solution.py:29
  107.1 44.0 %collective-permute-start.11 = (f32[512,256]{1,0:T(8,128)S(1)}, f32[512,256]{1,0:T(8,128)S(1)}, u32[]{:S(2)}, u32[]{:S(2)}) collective-permute-start(f32[512,256]{1,0:T(8,128)S(1)} %slice.19), channel_id=1, source_target_pairs={{0,1},{2,0},{4,2},{6,4},{7,6},{5,7},{3,5},{1,3},{8,9},{10,8},{12,1... | collective-permute-start | bytes 1572872 | tf_op jit(solution)/shard_map/ppermute | solution.py:25
  108.8 42.2 %collective-permute-start.9 = (f32[512,256]{1,0:T(8,128)S(1)}, f32[512,256]{1,0:T(8,128)S(1)}, u32[]{:S(2)}, u32[]{:S(2)}) collective-permute-start(f32[512,256]{1,0:T(8,128)S(1)} %slice.18), channel_id=1, source_target_pairs={{0,2},{2,4},{4,6},{6,7},{7,5},{5,3},{3,1},{1,0},{8,10},{10,12},{12... | collective-permute-start | bytes 1572872 | tf_op jit(solution)/shard_map/ppermute | solution.py:25
  164.6 12.4 %collective-permute-start.14 = (f32[256,128]{1,0:T(8,128)S(1)}, f32[256,128]{1,0:T(8,128)S(1)}, u32[]{:S(2)}, u32[]{:S(2)}) collective-permute-start(f32[256,128]{1,0:T(8,128)S(1)} %get-tuple-element.24), channel_id=1, source_target_pairs={{0,0},{1,1},{2,8},{3,9},{4,16},{5,17},{6,24},{7,25},{8,2},{9,3},{1... | collective-permute-start | bytes 393224 | tf_op jit(solution)/shard_map/ppermute | solution.py:410
  166.5 19.2 %collective-permute-start.15 = (f32[256,128]{1,0:T(8,128)S(1)}, f32[256,128]{1,0:T(8,128)S(1)}, u32[]{:S(2)}, u32[]{:S(2)}) collective-permute-start(f32[256,128]{1,0:T(8,128)S(1)} %get-tuple-element.23), channel_id=1, source_target_pairs={{0,1},{1,2},{2,9},{3,10},{4,17},{5,18},{6,25},{7,26},{8,3},{9,4},{... | collective-permute-start | bytes 393224 | tf_op jit(solution)/shard_map/ppermute | solution.py:410
  169.2 16.5 %collective-permute-start.16 = (f32[256,128]{1,0:T(8,128)S(1)}, f32[256,128]{1,0:T(8,128)S(1)}, u32[]{:S(2)}, u32[]{:S(2)}) collective-permute-start(f32[256,128]{1,0:T(8,128)S(1)} %get-tuple-element.22), channel_id=1, source_target_pairs={{0,2},{1,3},{2,10},{3,11},{4,18},{5,19},{6,26},{7,27},{8,4},{9,5},... | collective-permute-start | bytes 393224 | tf_op jit(solution)/shard_map/ppermute | solution.py:410
  170.3 19.7 %collective-permute-start.17 = (f32[256,128]{1,0:T(8,128)S(1)}, f32[256,128]{1,0:T(8,128)S(1)}, u32[]{:S(2)}, u32[]{:S(2)}) collective-permute-start(f32[256,128]{1,0:T(8,128)S(1)} %get-tuple-element.21), channel_id=1, source_target_pairs={{0,3},{1,4},{2,11},{3,12},{4,19},{5,20},{6,27},{7,28},{8,5},{9,6},... | collective-permute-start | bytes 393224 | tf_op jit(solution)/shard_map/ppermute | solution.py:410
  173.1 21.5 %collective-permute-start.18 = (f32[256,128]{1,0:T(8,128)S(1)}, f32[256,128]{1,0:T(8,128)S(1)}, u32[]{:S(2)}, u32[]{:S(2)}) collective-permute-start(f32[256,128]{1,0:T(8,128)S(1)} %get-tuple-element.20), channel_id=1, source_target_pairs={{0,4},{1,5},{2,12},{3,13},{4,20},{5,21},{6,28},{7,29},{8,6},{9,7},... | collective-permute-start | bytes 393224 | tf_op jit(solution)/shard_map/ppermute | solution.py:410
  177.0 20.7 %copy-start.17 = (f32[256,128]{1,0:T(8,128)}, f32[256,128]{1,0:T(8,128)S(1)}, u32[]{:S(2)}) copy-start(f32[256,128]{1,0:T(8,128)S(1)} %collective-permute-done.14.refs_0_) | copy-start | bytes 393220
  177.0 20.3 %collective-permute-start.19 = (f32[256,128]{1,0:T(8,128)S(1)}, f32[256,128]{1,0:T(8,128)S(1)}, u32[]{:S(2)}, u32[]{:S(2)}) collective-permute-start(f32[256,128]{1,0:T(8,128)S(1)} %get-tuple-element.19), channel_id=1, source_target_pairs={{0,5},{1,6},{2,13},{3,14},{4,21},{5,22},{6,29},{7,30},{8,7},{9,0},... | collective-permute-start | bytes 393224 | tf_op jit(solution)/shard_map/ppermute | solution.py:410
  185.7 12.0 %copy-start.18 = (f32[256,128]{1,0:T(8,128)}, f32[256,128]{1,0:T(8,128)S(1)}, u32[]{:S(2)}) copy-start(f32[256,128]{1,0:T(8,128)S(1)} %collective-permute-done.15.refs_1_) | copy-start | bytes 393220
  185.7 11.6 %collective-permute-start.20 = (f32[256,128]{1,0:T(8,128)S(1)}, f32[256,128]{1,0:T(8,128)S(1)}, u32[]{:S(2)}, u32[]{:S(2)}) collective-permute-start(f32[256,128]{1,0:T(8,128)S(1)} %get-tuple-element.18), channel_id=1, source_target_pairs={{0,6},{1,7},{2,14},{3,15},{4,22},{5,23},{6,30},{7,31},{8,0},{9,1},... | collective-permute-start | bytes 393224 | tf_op jit(solution)/shard_map/ppermute | solution.py:410
  185.7 12.0 %copy-start.19 = (f32[256,128]{1,0:T(8,128)}, f32[256,128]{1,0:T(8,128)S(1)}, u32[]{:S(2)}) copy-start(f32[256,128]{1,0:T(8,128)S(1)} %collective-permute-done.16.refs_2_) | copy-start | bytes 393220
  185.7 12.0 %collective-permute-start.21 = (f32[256,128]{1,0:T(8,128)S(1)}, f32[256,128]{1,0:T(8,128)S(1)}, u32[]{:S(2)}, u32[]{:S(2)}) collective-permute-start(f32[256,128]{1,0:T(8,128)S(1)} %get-tuple-element.17), channel_id=1, source_target_pairs={{0,7},{1,0},{2,15},{3,8},{4,23},{5,16},{6,31},{7,24},{8,1},{9,2},{... | collective-permute-start | bytes 393224 | tf_op jit(solution)/shard_map/ppermute | solution.py:410
  190.0 7.7 %copy-start.20 = (f32[256,128]{1,0:T(8,128)}, f32[256,128]{1,0:T(8,128)S(1)}, u32[]{:S(2)}) copy-start(f32[256,128]{1,0:T(8,128)S(1)} %collective-permute-done.17.refs_3_) | copy-start | bytes 393220
  (15 other events, 22.1 us)

commit v2 on v1

--- a/solution.py
+++ b/solution.py
@@ -39,35 +39,40 @@
 
 
 def pack_kernel(sc_ref, col_ref, out_ref, *, kw):
-    m = sc_ref[0]
     n_ch, rows, lanes = col_ref.shape
     groups = lanes // kw
     half = groups // 2
-    grp = lane_group((rows, lanes), kw)
-    re = im = None
-    for j in range(n_ch):
-        v = col_ref[j]
-        if j:
-            v = pltpu.roll(v, j * kw, 1)
-        if re is None:
-            re = im = v
-        else:
-            re = jnp.where(grp == lax.rem(m + j, groups), v, re)
-            im = jnp.where(grp == lax.rem(m + half + j, groups), v, im)
-    out_ref[:, :lanes] = pltpu.roll(re, lax.rem((groups - m) * kw, lanes), 1)
-    out_ref[:, lanes:] = pltpu.roll(im, lax.rem((groups + half - m) * kw, lanes), 1)
-
-
-def pack(columns, meta, kw):
+    sub = min(rows, 64)
+    grp = lane_group((sub, lanes), kw)
+
+    def share(m):
+        @pl.loop(0, rows // sub)
+        def _(t):
+            at = pl.ds(pl.multiple_of(t * sub, sub), sub)
+            re = im = None
+            for j in range(n_ch):
+                v = col_ref[j, at]
+                if j:
+                    v = pltpu.roll(v, j * kw, 1)
+                re = v if re is None else jnp.where(grp == (m + j) % groups, v, re)
+                im = v if im is None else jnp.where(grp == (m + half + j) % groups, v, im)
+            out_ref[at, :lanes] = pltpu.roll(re, (groups - m) * kw, 1) if m else re
+            out_ref[at, lanes:] = pltpu.roll(im, (half - m) * kw, 1)
+
+    for m in range(half):
+        pl.when(sc_ref[0] == m)(functools.partial(share, m))
+
+
+def pack(columns, meta, kw, part):
     n_ch, nb, lanes = columns.shape
-    steps = 4
+    nb, steps = nb // 2, 2
     return pl.pallas_call(
         functools.partial(pack_kernel, kw=kw),
         out_shape=jax.ShapeDtypeStruct((nb, 2 * lanes), F32),
         grid_spec=pltpu.PrefetchScalarGridSpec(
             num_scalar_prefetch=1,
             grid=(steps,),
-            in_specs=[pl.BlockSpec((n_ch, nb // steps, lanes), lambda g, sc: (0, g, 0))],
+            in_specs=[pl.BlockSpec((n_ch, nb // steps, lanes), lambda g, sc: (0, part * steps + g, 0))],
             out_specs=pl.BlockSpec((nb // steps, 2 * lanes), lambda g, sc: (g, 0)),
         ),
         name="pack",
@@ -82,7 +87,13 @@
     step = pl.program_id(0)
     n_l, _, rows, _ = p_refs[0].shape
     n_chan, n_ch, _ = a_refs[0].shape
-    fetch = None if fresh else pltpu.make_async_copy(c_in, w_ref, sem.at[0])
+    if fresh:
+        fetch = None
+    elif n_x == 1:
+        near = pl.ds(sc_ref[places[0]], SPAN)
+        fetch = pltpu.make_async_copy(c_in.at[near], w_ref, sem.at[0])
+    else:
+        fetch = pltpu.make_async_copy(c_in, w_ref, sem.at[0])
 
     @pl.when(step == 0)
     def _():
@@ -102,8 +113,8 @@
             axis=0,
         )
         h, l = split(v)
-        parts += [h, h, l]
-    lhs = jnp.concatenate(parts, axis=1)
+        parts.append((h, l))
+    (rh, rl), (ih, il) = parts
     rhs = []
     for t in range(n_x):
         x = jnp.concatenate([x_refs[2 * t][...], x_refs[2 * t + 1][...]], axis=0)
@@ -111,8 +122,19 @@
         xh, xl = split(x)
         yh = jnp.concatenate([-xh[:, lanes:], xh[:, :lanes]], axis=1)
         yl = jnp.concatenate([-xl[:, lanes:], xl[:, :lanes]], axis=1)
-        rhs.append(jnp.concatenate([xh, xl, xh, yh, yl, yh], axis=0))
-    prod = jnp.dot(lhs, jnp.concatenate(rhs, axis=1), preferred_element_type=F32)
+        rhs.append((jnp.concatenate([xh, yh], axis=0), jnp.concatenate([xl, yl], axis=0)))
+    hi = jnp.concatenate([rh, ih], axis=1)
+    lo = jnp.concatenate([rl, il], axis=1)
+    if n_x == 1:
+        both = jnp.dot(hi, jnp.concatenate(rhs[0], axis=1), preferred_element_type=F32)
+        prod = both[:, : 2 * lanes] + both[:, 2 * lanes :]
+        prod += jnp.dot(lo, rhs[0][0], preferred_element_type=F32)
+    else:
+        prod = jnp.dot(
+            jnp.concatenate([hi, hi, lo], axis=1),
+            jnp.concatenate([jnp.concatenate([h, l, h], axis=0) for h, l in rhs], axis=1),
+            preferred_element_type=F32,
+        )
     for t in range(n_x):
         piece = prod[:, 2 * lanes * t : 2 * lanes * (t + 1)]
 
@@ -148,12 +170,13 @@
         @pl.loop(0, n_x)
         def _(t):
             s = sc_ref[places[0] + t]
+            me = sc_ref[1]
             coef = []
             for a_ref in a_refs:
                 v = None
                 for d in range(SPAN):
                     at = s + d - R
-                    own = a_ref[jnp.clip(at, 0, n_chan - 1)]
+                    own = a_ref[lax.rem(me - at + 2 * n_chan, n_chan)]
                     own = jnp.where((at >= 0) & (at < n_chan), own, 0.0)
                     v = own if v is None else jnp.where(lax.rem(grp, LANES // n_l // n_ch) == d, own, v)
                 coef += [pltpu.roll(v, LANES - l * (LANES // n_l), 1) if l else v for l in range(n_l)]
@@ -177,9 +200,12 @@
                 preferred_element_type=F32,
             )
             for d in range(SPAN):
-                w_ref[s + d] += out[:, d * lanes : (d + 1) * lanes]
-
-        back = pltpu.make_async_copy(w_ref, c_out, sem.at[1])
+                w_ref[d if n_x == 1 and not fresh else s + d] += out[:, d * lanes : (d + 1) * lanes]
+
+        if n_x == 1 and not fresh:
+            back = pltpu.make_async_copy(w_ref, c_out.at[near], sem.at[1])
+        else:
+            back = pltpu.make_async_copy(w_ref, c_out, sem.at[1])
         back.start()
         back.wait()
 
@@ -224,7 +250,7 @@
             out_specs=pl.BlockSpec(memory_space=pltpu.HBM),
             scratch_shapes=[
                 pltpu.VMEM((len(chunks), n * n_l * rows, wide), F32),
-                pltpu.VMEM(shape, F32),
+                pltpu.VMEM((SPAN,) + shape[1:] if len(chunks) == 1 and not fresh else shape, F32),
                 pltpu.SemaphoreType.DMA((2,)),
             ],
         ),
@@ -232,67 +258,94 @@
         cost_estimate=pl.CostEstimate(
             flops=flops, transcendentals=0, bytes_accessed=4 * n * n_l * 2 * rows * nb
         ),
-        compiler_params=pltpu.CompilerParams(vmem_limit_bytes=48 << 20),
+        compiler_params=pltpu.CompilerParams(vmem_limit_bytes=26 << 20),
         name="unit",
-    )(meta, *[pltpu.with_memory_space_constraint(a, pltpu.HBM) for a in args])
-
-
-def finish_kernel(sc_ref, energy_ref, contour_ref, col_ref, *refs, kw, n_mult):
+    )(
+        meta,
+        *args[: 2 * n],
+        *[pltpu.with_memory_space_constraint(a, pltpu.HBM) for a in args[2 * n :]],
+    )
+
+
+def shift_kernel(sc_ref, energy_ref, contour_ref, col_ref, out_ref):
+    n_ch, rows, lanes = col_ref.shape
+    upper = lax.broadcasted_iota(jnp.int32, (rows, lanes), 1) >= lanes // 2
+    shift = jnp.where(upper, contour_ref[1], -contour_ref[1])
+    for i in range(n_ch):
+        x = col_ref[i]
+        out_ref[i] = (contour_ref[0] - energy_ref[i]) * x + shift * pltpu.roll(x, lanes // 2, 1)
+
+
+def shifted_columns(columns, energies, contour, meta, n_mult):
+    n_ch, nb, lanes = columns.shape
+    rows = nb // n_mult
+    steps = max(1, rows // 64)
+    sub = rows // steps
+    smem = pl.BlockSpec(memory_space=pltpu.SMEM)
+    return pl.pallas_call(
+        shift_kernel,
+        out_shape=jax.ShapeDtypeStruct((n_ch, rows, lanes), F32),
+        grid_spec=pltpu.PrefetchScalarGridSpec(
+            num_scalar_prefetch=1,
+            grid=(steps,),
+            in_specs=[smem, smem, pl.BlockSpec((n_ch, sub, lanes), lambda g, sc: (0, sc[0] * steps + g, 0))],
+            out_specs=pl.BlockSpec((n_ch, sub, lanes), lambda g, sc: (0, g, 0)),
+        ),
+        name="shifted",
+    )(meta, energies, contour, columns)
+
+
+def finish_kernel(sc_ref, base_ref, *refs, kw, n_mult):
     pieces, out_ref, held = refs[:-2], refs[-2], refs[-1]
-    n_ch, _, lanes = col_ref.shape
+    n_ch, per, sub, lanes = base_ref.shape
     n = len(pieces)
-    per = n // n_mult
     me = sc_ref[1]
     for s in range(n):
         held[lax.rem(me - s + n, n)] = pieces[s][...]
+    groups = 2 * n_mult
+    v = jnp.concatenate(
+        [
+            jnp.concatenate([held[u * per + h, part] for part in range(2) for u in range(n_mult)], axis=1)
+            for h in range(per)
+        ],
+        axis=0,
+    )
+    vh, vl = split(v)
+    both = jnp.concatenate([vh, vl], axis=0)
+    row = lax.broadcasted_iota(jnp.int32, (groups * lanes, lanes), 0)
+    col = lax.broadcasted_iota(jnp.int32, (groups * lanes, lanes), 1)
+    start = (col // kw) * lanes + col % kw
+    picks = jnp.concatenate([(row == start + i * kw).astype(BF16) for i in range(n_ch)], axis=1)
+    out = jnp.dot(both, picks, preferred_element_type=F32)
+    out = out[: per * sub] + out[per * sub :]
+    for h in range(per):
+        for i in range(n_ch):
+            out_ref[i, h] = base_ref[i, h] - out[h * sub : (h + 1) * sub, i * lanes : (i + 1) * lanes]
+
+
+def finish(pieces, base, meta, kw, n_mult):
+    n_ch, out_rows, lanes = base.shape
     rows = pieces[0].shape[0] // 2
-    groups = 2 * n_mult
-    grp = lane_group((rows, lanes), kw)
-    upper = lax.broadcasted_iota(jnp.int32, (rows, lanes), 1) >= lanes // 2
-    shift = contour_ref[1]
-    for h in range(per):
-        vs = [held[u * per + h, part * rows : (part + 1) * rows] for part in range(2) for u in range(n_mult)]
-        dist = 1
-        while dist < groups:
-            odd = (grp // dist) % 2 == 1
-            nxt = list(vs)
-            for a in range(groups):
-                if not a & dist:
-                    b = a + dist
-                    nxt[a] = jnp.where(odd, pltpu.roll(vs[b], dist * kw, 1), vs[a])
-                    nxt[b] = jnp.where(odd, vs[b], pltpu.roll(vs[a], lanes - dist * kw, 1))
-            vs = nxt
-            dist *= 2
-        at = pl.ds(h * rows, rows)
-        for i in range(n_ch):
-            x = col_ref[i, at]
-            turned = pltpu.roll(x, lanes // 2, 1)
-            turned = jnp.where(upper, turned, -turned)
-            out_ref[i, at] = (contour_ref[0] - energy_ref[i]) * x + shift * turned - vs[i]
-
-
-def finish(pieces, columns, energies, contour, meta, kw, n_mult):
-    n_ch, nb, lanes = columns.shape
-    out_rows = nb // n_mult
-    smem = pl.BlockSpec(memory_space=pltpu.SMEM)
-    return pl.pallas_call(
+    per = out_rows // rows
+    sub = min(rows, 64)
+    out = pl.pallas_call(
         functools.partial(finish_kernel, kw=kw, n_mult=n_mult),
-        out_shape=jax.ShapeDtypeStruct((n_ch, out_rows, lanes), F32),
+        out_shape=jax.ShapeDtypeStruct((n_ch, per, rows, lanes), F32),
         grid_spec=pltpu.PrefetchScalarGridSpec(
             num_scalar_prefetch=1,
-            grid=(1,),
-            in_specs=[smem, smem, pl.BlockSpec((n_ch, out_rows, lanes), lambda g, sc: (0, sc[0], 0))]
-            + [pl.BlockSpec(p.shape, lambda g, sc: (0, 0)) for p in pieces],
-            out_specs=pl.BlockSpec((n_ch, out_rows, lanes), lambda g, sc: (0, 0, 0)),
-            scratch_shapes=[pltpu.VMEM((len(pieces),) + pieces[0].shape, F32)],
+            grid=(rows // sub,),
+            in_specs=[pl.BlockSpec((n_ch, per, sub, lanes), lambda g, sc: (0, 0, g, 0))]
+            + [pl.BlockSpec((2, sub, lanes), lambda g, sc: (0, g, 0)) for _ in pieces],
+            out_specs=pl.BlockSpec((n_ch, per, sub, lanes), lambda g, sc: (0, 0, g, 0)),
+            scratch_shapes=[pltpu.VMEM((len(pieces), 2, sub, lanes), F32)],
         ),
         name="finish",
-    )(meta, energies, contour, columns, *pieces)
+    )(meta, base.reshape(n_ch, per, rows, lanes), *[p.reshape(2, rows, lanes) for p in pieces])
+    return out.reshape(n_ch, out_rows, lanes)
 
 
 def mixing_blocks(coefficients, channel_cols, used_slots, lambda_low, lambda_high, chan_index, mult_index):
     n_ch, slots, lam = coefficients.shape
-    n_chan = lax.axis_size("chan")
     local = channel_cols - (chan_index - R) * n_ch
     slot_ids = jnp.arange(slots, dtype=jnp.int32)
     live = slot_ids[None, :] < used_slots[:, None]
@@ -311,12 +364,12 @@
     mine = jnp.sum(
         jnp.where(by_lane[:, None, :] == want[None], w_lane[:, None, :], 0.0), axis=0
     )
-    return jnp.broadcast_to(mine[None], (n_chan,) + mine.shape)
+    return mine
 
 
 def steps_of(n_chan):
     full = (n_chan - 1) // 2
-    return full, max(1, min(2, full - 1))
+    return full, min(2, full)
 
 
 def body(
@@ -330,7 +383,7 @@
     energies,
     contour,
 ):
-    _, nb, lanes = columns.shape
+    _, _, lanes = columns.shape
     n_chan, n_mult = lax.axis_size("chan"), lax.axis_size("mult")
     chan_index, mult_index = lax.axis_index("chan"), lax.axis_index("mult")
     kw = lanes // 2 // n_mult
@@ -348,13 +401,19 @@
     def spot(by):
         return 2 + hops.index(by)
 
+    mine = []
+    for part in range(2):
+        mine.append(pack(columns, meta, kw, part))
+    mine[1], coefficients = lax.optimization_barrier((mine[1], coefficients))
     sent = mixing_blocks(
         coefficients, channel_cols, used_slots, lambda_low, lambda_high, chan_index, mult_index
     )
-    sent, meta = lax.optimization_barrier((sent, meta))
-    near_coefs = [lax.all_to_all(sent, "chan", 0, 0, tiled=True)]
-    near_coefs[0], meta = lax.optimization_barrier((near_coefs[0], meta))
-    mine = pack(columns, meta, kw)
+    near_coefs = [sent]
+    for by in range(1, n_chan):
+        near_coefs.append(
+            lax.ppermute(sent, "chan", [(i, (i + by) % n_chan) for i in range(n_chan)])
+        )
+    near_coefs = [jnp.stack(near_coefs)]
 
     near_sets = [panels]
     bit = n_mult // 4
@@ -372,29 +431,30 @@
 
     full_steps, switch = steps_of(n_chan)
     total = None
-    ahead = behind = mine
-    held = [(mine, mine, spot(0))]
-    total = add(total, near_sets, near_coefs, held)
+    ahead, behind = list(mine), list(mine)
+    held, late = [(*mine, spot(0))], []
     for step in range(1, full_steps + 1):
-        ahead = ring_shift(ahead, "chan", 1)
-        behind = ring_shift(behind, "chan", -1)
-        new = [(ahead, ahead, spot(-step)), (behind, behind, spot(step))]
+        for part in range(2):
+            ahead[part] = ring_shift(ahead[part], "chan", 1)
+            behind[part] = ring_shift(behind[part], "chan", -1)
+        held += [(*ahead, spot(-step)), (*behind, spot(step))]
         if step <= switch:
-            total = add(total, near_sets, near_coefs, new)
-            held += new
+            total = add(total, near_sets, near_coefs, held)
+            late += held
         else:
-            total = add(total, near_sets + far, near_coefs + far_coefs, new)
-        if step == switch:
+            total = add(total, near_sets + far, near_coefs + far_coefs, held)
+        held = []
+        if step == 1:
             far[0], total = lax.optimization_barrier((far[0], total))
             bit = n_mult // 4
             while bit:
                 far += [flip(p, "mult", bit) for p in far]
                 bit //= 2
-            for at in range(0, len(held), 3):
-                total = add(total, far, far_coefs, held[at : at + 3])
+        if step == switch:
+            total = add(total, far, far_coefs, late)
     if n_chan % 2 == 0:
-        top = ring_shift(ahead[: nb // 2], "chan", 1)
-        bottom = ring_shift(behind[nb // 2 :], "chan", -1)
+        top = ring_shift(ahead[0], "chan", 1)
+        bottom = ring_shift(behind[1], "chan", -1)
         total = add(total, near_sets + far, near_coefs + far_coefs, [(top, bottom, spot(n_chan // 2))])
 
     per = n_chan // n_mult
@@ -408,7 +468,8 @@
                 pairs.append((m * n_chan + c, (c // per) * n_chan + (q + s) % n_chan))
         piece = lax.dynamic_index_in_dim(total, R + lax.rem(mine_q + s, n_chan), 0, keepdims=False)
         pieces.append(lax.ppermute(piece, ("mult", "chan"), pairs))
-    return finish(pieces, columns, energies, contour, meta, kw, n_mult)
+    base = shifted_columns(columns, energies, contour, meta, n_mult)
+    return finish(pieces, base, meta, kw, n_mult)
 
 
 def solution(mesh):

time: 204 us -> 193 us (0.946)
  the two profiles are of different devices: /device:TPU:14 before, /device:TPU:2 now
where the time goes in v2:
time: 193 us; the launch traced here: 192 us
  Pallas kernels  82.5 us (43%)
  waiting for transfers between devices  62.9 us (33%)
  starting transfers between devices  37.5 us (19%)
  local copies, waits for them, and re-layouts  8.12 us (4%)
    pallas_call x5, Pallas kernels, unit(): pl.pallas_call(functools.partial(unit_kernel, n_p=n, kw=kw, steps=steps,...  65.2 us
    ppermute x14, waiting for transfers between devices, ring_shift(): lax.ppermute(value, axis, [(order[i], order[(i + by) % n]) for i in range...  39.7 us
    ppermute x8, waiting for transfers between devices, body(): pieces.append(lax.ppermute(piece, ('mult', 'chan'), pairs))  17.7 us
    ppermute x14, starting transfers between devices, ring_shift(): lax.ppermute(value, axis, [(order[i], order[(i + by) % n]) for i in range...  13.6 us
    ppermute x7, starting transfers between devices, body(): lax.ppermute(sent, 'chan', [(i, (i + by) % n_chan) for i in range(n_chan)])  12.4 us
    ppermute x8, starting transfers between devices, body(): pieces.append(lax.ppermute(piece, ('mult', 'chan'), pairs))  8.97 us
    pallas_call x2, Pallas kernels, pack(): pl.pallas_call(functools.partial(pack_kernel, kw=kw), out_shape=jax.Shape...  8.62 us
    unnamed x69, local copies, waits for them, and re-layouts  5.92 us
  transfers between devices with their start and end apart: 35, of which 12 were waited for; matrix products, arithmetic and copies ran while one was open for 0% of the time, Pallas kernels for 33%

profile of v2, /device:TPU:2, one launch (start us, length us, event | category | flops | bytes accessed | tf_op | source)
XLA Modules:
  0.0 192.4 jit_solution(3986825020460816110)
XLA Ops:
  1.4 4.4 %pack.3.refs_5_ = f32[512,256]{1,0:T(8,128)} custom-call(s32[11]{0:T(128)} %pad_add_fusion.sc_ref, f32[8,1024,128]{2,1,0:T(8,128)} %col_ref.5), custom_call_target="tpu_custom_call" | custom-call | tf_op jit(solution)/shard_map/pack/pallas_call | solution.py:69
  6.2 1.6 collective-permute-start.6
  7.8 1.6 collective-permute-start.7
  9.4 2.5 %collective-permute-start.8 = (f32[8,128]{1,0:T(8,128)S(1)}, f32[8,128]{1,0:T(8,128)S(1)}, u32[]{:S(2)}, u32[]{:S(2)}) collective-permute-start(f32[8,128]{1,0:T(8,128)S(1)} %select_reduce_fusion), channel_id=1, source_target_pairs={{0,3},{1,4},{2,5},{3,6},{4,7},{5,0},{6,1},{7,2},{8,11},{9,12},{10,... | collective-permute-start | bytes 12296 | tf_op jit(solution)/shard_map/ppermute | solution.py:414
  13.1 2.6 %collective-permute-start.10 = (f32[8,128]{1,0:T(8,128)S(1)}, f32[8,128]{1,0:T(8,128)S(1)}, u32[]{:S(2)}, u32[]{:S(2)}) collective-permute-start(f32[8,128]{1,0:T(8,128)S(1)} %select_reduce_fusion), channel_id=1, source_target_pairs={{0,5},{1,6},{2,7},{3,0},{4,1},{5,2},{6,3},{7,4},{8,13},{9,14},{10,... | collective-permute-start | bytes 12296 | tf_op jit(solution)/shard_map/ppermute | solution.py:414
  19.8 1.5 collective-permute-done.12
  21.4 1.6 collective-permute-start.5
  22.9 4.2 %pack.2.refs_4_ = f32[512,256]{1,0:T(8,128)} custom-call(s32[11]{0:T(128)} %pad_add_fusion.sc_ref, f32[8,1024,128]{2,1,0:T(8,128)} %col_ref.5), custom_call_target="tpu_custom_call" | custom-call | tf_op jit(solution)/shard_map/pack/pallas_call | solution.py:69
  27.8 6.4 %collective-permute-done.3.refs_7_ = f32[512,256]{1,0:T(8,128)S(1)} collective-permute-done((f32[512,256]{1,0:T(8,128)}, f32[512,256]{1,0:T(8,128)S(1)}, u32[]{:S(2)}, u32[]{:S(2)}) %collective-permute-start.3) | collective-permute-done | bytes 524320 | tf_op jit(solution)/shard_map/ppermute | solution.py:25
  34.8 1.6 collective-permute-done.5.refs_9_
  36.4 7.6 %collective-permute-done.2.refs_6_ = f32[512,256]{1,0:T(8,128)S(1)} collective-permute-done((f32[512,256]{1,0:T(8,128)}, f32[512,256]{1,0:T(8,128)S(1)}, u32[]{:S(2)}, u32[]{:S(2)}) %collective-permute-start.2) | collective-permute-done | bytes 524320 | tf_op jit(solution)/shard_map/ppermute | solution.py:25
  44.0 3.1 %collective-permute-done.4.refs_8_ = f32[512,256]{1,0:T(8,128)S(1)} collective-permute-done((f32[512,256]{1,0:T(8,128)}, f32[512,256]{1,0:T(8,128)S(1)}, u32[]{:S(2)}, u32[]{:S(2)}) %collective-permute-start.4) | collective-permute-done | bytes 524320 | tf_op jit(solution)/shard_map/ppermute | solution.py:25
  48.0 11.9 %unit.5.refs_10_ = f32[12,256,128]{2,1,0:T(8,128)S(1)} custom-call(s32[11]{0:T(128)S(1)} %copy-done.2, f32[2,2,128,1024]{3,2,1,0:T(8,128)S(1)} %copy-done, f32[2,2,128,1024]{3,2,1,0:T(8,128)S(1)} %copy-done, f32[2,2,128,1024]{3,2,1,0:T(8,128)} %collective-permute-done.refs_2_.refs_3_, f32[2,2,128,1024]{3,2,1,0:T(8,128)} %collective-permute-done.refs_2_.refs_3_, ...), custom_call_target="tpu_custom_call" | custom-call | flops 6341787648 | bytes 4194304 | tf_op jit(solution)/shard_map/unit/pallas_call | solution.py:241
  61.1 4.0 %collective-permute-done.1.refs_0_.refs_1_.refs_4_.refs_5_ = f32[2,2,128,1024]{3,2,1,0:T(8,128)} collective-permute-done((f32[2,2,128,1024]{3,2,1,0:T(8,128)S(1)}, f32[2,2,128,1024]{3,2,1,0:T(8,128)}, u32[]{:S(2)}, u32[]{:S(2)}) %collective-permute-start.1) | collective-permute-done | bytes 2097184 | tf_op jit(solution)/shard_map/ppermute | solution.py:29
  69.1 11.0 %collective-permute-done.18.refs_7_.refs_13_ = f32[512,256]{1,0:T(8,128)S(1)} collective-permute-done((f32[512,256]{1,0:T(8,128)}, f32[512,256]{1,0:T(8,128)S(1)}, u32[]{:S(2)}, u32[]{:S(2)}) %collective-permute-start.18) | collective-permute-done | bytes 524320 | tf_op jit(solution)/shard_map/ppermute | solution.py:25
  82.1 9.9 %collective-permute-done.23.refs_5_.refs_11_ = f32[512,256]{1,0:T(8,128)} collective-permute-done((f32[512,256]{1,0:T(8,128)}, f32[512,256]{1,0:T(8,128)}, u32[]{:S(2)}, u32[]{:S(2)}) %collective-permute-start.23) | collective-permute-done | bytes 524320 | tf_op jit(solution)/shard_map/ppermute | solution.py:25
  92.5 1.6 collective-permute-start.22
  94.1 9.9 %unit.6.refs_16_ = f32[12,256,128]{2,1,0:T(8,128)} custom-call(s32[11]{0:T(128)S(1)} %copy-done.2, f32[2,2,128,1024]{3,2,1,0:T(8,128)S(1)} %copy-done, f32[2,2,128,1024]{3,2,1,0:T(8,128)S(1)} %copy-done, f32[2,2,128,1024]{3,2,1,0:T(8,128)} %collective-permute-done.refs_2_.refs_3_, ...), custom_call_target="tpu_custom_call", output_to_operand_aliasing={{}: (11, {})} | custom-call | flops 4227858432 | bytes 4194304 | tf_op jit(solution)/shard_map/unit/pallas_call | solution.py:241
  104.0 1.5 collective-permute-start.24
  106.3 1.8 collective-permute-start.17
  108.1 18.7 %unit.7.refs_16_ = f32[12,256,128]{2,1,0:T(8,128)} custom-call(s32[11]{0:T(128)S(1)} %copy-done.2, f32[2,2,128,1024]{3,2,1,0:T(8,128)} %collective-permute-done.1.refs_0_.refs_1_.refs_4_.refs_5_, f32[2,2,128,1024]{3,2,1,0:T(8,128)} %collective-permute-done.1.refs_0_.refs_1_.refs_4_.refs_5_, ...), custom_call_target="tpu_custom_call", output_to_operand_aliasing={{}: (17, {})} | custom-call | flops 10569646080 | bytes 4194304 | tf_op jit(solution)/shard_map/unit/pallas_call | solution.py:241
  128.4 15.1 %unit.8.refs_14_ = f32[12,256,128]{2,1,0:T(8,128)} custom-call(s32[11]{0:T(128)S(1)} %copy-done.2, f32[2,2,128,1024]{3,2,1,0:T(8,128)S(1)} %copy-done, f32[2,2,128,1024]{3,2,1,0:T(8,128)S(1)} %copy-done, f32[2,2,128,1024]{3,2,1,0:T(8,128)} %collective-permute-done.refs_2_.refs_3_, ...), custom_call_target="tpu_custom_call", output_to_operand_aliasing={{}: (17, {})} | custom-call | flops 8455716864 | bytes 8388608 | tf_op jit(solution)/shard_map/unit/pallas_call | solution.py:241
  145.1 9.7 %unit.9 = f32[12,256,128]{2,1,0:T(8,128)} custom-call(s32[11]{0:T(128)S(1)} %copy-done.2, f32[2,2,128,1024]{3,2,1,0:T(8,128)S(1)} %copy-done, f32[2,2,128,1024]{3,2,1,0:T(8,128)S(1)} %copy-done, f32[2,2,128,1024]{3,2,1,0:T(8,128)} %collective-permute-done.refs_2_.refs_3_, ...), custom_call_target="tpu_custom_call", output_to_operand_aliasing={{}: (15, {})} | custom-call | flops 4227858432 | bytes 8388608 | tf_op jit(solution)/shard_map/unit/pallas_call | solution.py:241
  156.2 3.3 %collective-permute-start.27 = (f32[256,128]{1,0:T(8,128)S(1)}, f32[256,128]{1,0:T(8,128)S(1)}, u32[]{:S(2)}, u32[]{:S(2)}) collective-permute-start(f32[256,128]{1,0:T(8,128)S(1)} %get-tuple-element.20), channel_id=1, source_target_pairs={{0,0},{1,1},{2,8},{3,9},{4,16},{5,17},{6,24},{7,25},{8,2},{9,3},{1... | collective-permute-start | bytes 393224 | tf_op jit(solution)/shard_map/ppermute | solution.py:470
  159.5 2.2 %collective-permute-start.28 = (f32[256,128]{1,0:T(8,128)S(1)}, f32[256,128]{1,0:T(8,128)S(1)}, u32[]{:S(2)}, u32[]{:S(2)}) collective-permute-start(f32[256,128]{1,0:T(8,128)S(1)} %get-tuple-element.19), channel_id=1, source_target_pairs={{0,1},{1,2},{2,9},{3,10},{4,17},{5,18},{6,25},{7,26},{8,3},{9,4},{... | collective-permute-start | bytes 393224 | tf_op jit(solution)/shard_map/ppermute | solution.py:470
  161.7 2.1 %collective-permute-start.29 = (f32[256,128]{1,0:T(8,128)S(1)}, f32[256,128]{1,0:T(8,128)S(1)}, u32[]{:S(2)}, u32[]{:S(2)}) collective-permute-start(f32[256,128]{1,0:T(8,128)S(1)} %get-tuple-element.18), channel_id=1, source_target_pairs={{0,2},{1,3},{2,10},{3,11},{4,18},{5,19},{6,26},{7,27},{8,4},{9,5},... | collective-permute-start | bytes 393224 | tf_op jit(solution)/shard_map/ppermute | solution.py:470
  165.1 4.3 %collective-permute-done.27 = f32[256,128]{1,0:T(8,128)S(1)} collective-permute-done((f32[256,128]{1,0:T(8,128)S(1)}, f32[256,128]{1,0:T(8,128)S(1)}, u32[]{:S(2)}, u32[]{:S(2)}) %collective-permute-start.27) | collective-permute-done | bytes 131104 | tf_op jit(solution)/shard_map/ppermute | solution.py:470
  169.4 9.3 %collective-permute-done.28 = f32[256,128]{1,0:T(8,128)S(1)} collective-permute-done((f32[256,128]{1,0:T(8,128)S(1)}, f32[256,128]{1,0:T(8,128)S(1)}, u32[]{:S(2)}, u32[]{:S(2)}) %collective-permute-start.28) | collective-permute-done | bytes 131104 | tf_op jit(solution)/shard_map/ppermute | solution.py:470
  178.8 4.4 %shifted.1 = f32[8,256,128]{2,1,0:T(8,128)} custom-call(s32[11]{0:T(128)} %pad_add_fusion.sc_ref, f32[8]{0:T(128)} %energy_ref.1, f32[2]{0:T(128)} %contour_ref.1, f32[8,1024,128]{2,1,0:T(8,128)} %col_ref.5), custom_call_target="tpu_custom_call" | custom-call | tf_op jit(solution)/shard_map/shifted/pallas_call | solution.py:285
  183.3 1.7 collective-permute-done.33
  184.9 2.5 %collective-permute-done.34 = f32[256,128]{1,0:T(8,128)S(1)} collective-permute-done((f32[256,128]{1,0:T(8,128)S(1)}, f32[256,128]{1,0:T(8,128)S(1)}, u32[]{:S(2)}, u32[]{:S(2)}) %collective-permute-start.34) | collective-permute-done | bytes 131104 | tf_op jit(solution)/shard_map/ppermute | solution.py:470
  188.1 4.3 %finish.1 = f32[8,2,128,128]{3,2,1,0:T(8,128)} custom-call(s32[11]{0:T(128)} %pad_add_fusion.sc_ref, f32[8,2,128,128]{3,2,1,0:T(8,128)} %bitcast.63, f32[2,128,128]{2,1,0:T(8,128)} %bitcast.64, f32[2,128,128]{2,1,0:T(8,128)} %bitcast.65, f32[2,128,128]{2,1,0:T(8,128)} %bitcast.66, f32[2,128,128]{2,1,0:T(8,128)} %bitcast.67, f32[2,128,128]{2,1,0:T(8,128)} %bitcast.68, ...), custom_call_target="tpu_custom_call" | custom-call | tf_op jit(solution)/shard_map/finish/pallas_call | solution.py:331
  (134 shorter events, 24.3 us)
Async XLA Ops:
  6.2 9.6 %collective-permute-start.6 = (f32[8,128]{1,0:T(8,128)S(1)}, f32[8,128]{1,0:T(8,128)S(1)}, u32[]{:S(2)}, u32[]{:S(2)}) collective-permute-start(f32[8,128]{1,0:T(8,128)S(1)} %select_reduce_fusion), channel_id=1, source_target_pairs={{0,1},{1,2},{2,3},{3,4},{4,5},{5,6},{6,7},{7,0},{8,9},{9,10},{10,1... | collective-permute-start | bytes 12296 | tf_op jit(solution)/shard_map/ppermute | solution.py:414
  7.8 8.1 %collective-permute-start.7 = (f32[8,128]{1,0:T(8,128)S(1)}, f32[8,128]{1,0:T(8,128)S(1)}, u32[]{:S(2)}, u32[]{:S(2)}) collective-permute-start(f32[8,128]{1,0:T(8,128)S(1)} %select_reduce_fusion), channel_id=1, source_target_pairs={{0,2},{1,3},{2,4},{3,5},{4,6},{5,7},{6,0},{7,1},{8,10},{9,11},{10,... | collective-permute-start | bytes 12296 | tf_op jit(solution)/shard_map/ppermute | solution.py:414
  9.4 7.9 %collective-permute-start.8 = (f32[8,128]{1,0:T(8,128)S(1)}, f32[8,128]{1,0:T(8,128)S(1)}, u32[]{:S(2)}, u32[]{:S(2)}) collective-permute-start(f32[8,128]{1,0:T(8,128)S(1)} %select_reduce_fusion), channel_id=1, source_target_pairs={{0,3},{1,4},{2,5},{3,6},{4,7},{5,0},{6,1},{7,2},{8,11},{9,12},{10,... | collective-permute-start | bytes 12296 | tf_op jit(solution)/shard_map/ppermute | solution.py:414
  11.9 5.9 %collective-permute-start.9 = (f32[8,128]{1,0:T(8,128)S(1)}, f32[8,128]{1,0:T(8,128)S(1)}, u32[]{:S(2)}, u32[]{:S(2)}) collective-permute-start(f32[8,128]{1,0:T(8,128)S(1)} %select_reduce_fusion), channel_id=1, source_target_pairs={{0,4},{1,5},{2,6},{3,7},{4,0},{5,1},{6,2},{7,3},{8,12},{9,13},{10,... | collective-permute-start | bytes 12296 | tf_op jit(solution)/shard_map/ppermute | solution.py:414
  13.1 6.0 %collective-permute-start.10 = (f32[8,128]{1,0:T(8,128)S(1)}, f32[8,128]{1,0:T(8,128)S(1)}, u32[]{:S(2)}, u32[]{:S(2)}) collective-permute-start(f32[8,128]{1,0:T(8,128)S(1)} %select_reduce_fusion), channel_id=1, source_target_pairs={{0,5},{1,6},{2,7},{3,0},{4,1},{5,2},{6,3},{7,4},{8,13},{9,14},{10,... | collective-permute-start | bytes 12296 | tf_op jit(solution)/shard_map/ppermute | solution.py:414
  15.8 31.4 %collective-permute-start = (f32[2,2,128,1024]{3,2,1,0:T(8,128)S(1)}, f32[2,2,128,1024]{3,2,1,0:T(8,128)}, u32[]{:S(2)}, u32[]{:S(2)}) collective-permute-start(f32[2,2,128,1024]{3,2,1,0:T(8,128)S(1)} %copy-done), channel_id=1, source_target_pairs={{0,8},{8,0},{16,24},{24,16},{1,9},{9,1},{17,25},{25,17},{2,10},{10... | collective-permute-start | bytes 6291464 | tf_op jit(solution)/shard_map/ppermute | solution.py:29
  17.3 47.8 %collective-permute-start.1 = (f32[2,2,128,1024]{3,2,1,0:T(8,128)S(1)}, f32[2,2,128,1024]{3,2,1,0:T(8,128)}, u32[]{:S(2)}, u32[]{:S(2)}) collective-permute-start(f32[2,2,128,1024]{3,2,1,0:T(8,128)S(1)} %copy-done), channel_id=1, source_target_pairs={{0,16},{8,24},{16,0},{24,8},{1,17},{9,25},{17,1},{25,9},{2,18},{10... | collective-permute-start | bytes 6291464 | tf_op jit(solution)/shard_map/ppermute | solution.py:29
  19.2 15.0 %collective-permute-start.3 = (f32[512,256]{1,0:T(8,128)}, f32[512,256]{1,0:T(8,128)S(1)}, u32[]{:S(2)}, u32[]{:S(2)}) collective-permute-start(f32[512,256]{1,0:T(8,128)} %pack.3.refs_5_), channel_id=1, source_target_pairs={{0,2},{2,4},{4,6},{6,7},{7,5},{5,3},{3,1},{1,0},{8,10},{10,12},{12... | collective-permute-start | bytes 1572872 | tf_op jit(solution)/shard_map/ppermute | solution.py:25
  21.4 15.1 %collective-permute-start.5 = (f32[512,256]{1,0:T(8,128)}, f32[512,256]{1,0:T(8,128)S(1)}, u32[]{:S(2)}, u32[]{:S(2)}) collective-permute-start(f32[512,256]{1,0:T(8,128)} %pack.3.refs_5_), channel_id=1, source_target_pairs={{0,1},{2,0},{4,2},{6,4},{7,6},{5,7},{3,5},{1,3},{8,9},{10,8},{12,1... | collective-permute-start | bytes 1572872 | tf_op jit(solution)/shard_map/ppermute | solution.py:25
  27.2 16.8 %collective-permute-start.2 = (f32[512,256]{1,0:T(8,128)}, f32[512,256]{1,0:T(8,128)S(1)}, u32[]{:S(2)}, u32[]{:S(2)}) collective-permute-start(f32[512,256]{1,0:T(8,128)} %pack.2.refs_4_), channel_id=1, source_target_pairs={{0,2},{2,4},{4,6},{6,7},{7,5},{5,3},{3,1},{1,0},{8,10},{10,12},{12... | collective-permute-start | bytes 1572872 | tf_op jit(solution)/shard_map/ppermute | solution.py:25
  34.2 13.0 %collective-permute-start.4 = (f32[512,256]{1,0:T(8,128)}, f32[512,256]{1,0:T(8,128)S(1)}, u32[]{:S(2)}, u32[]{:S(2)}) collective-permute-start(f32[512,256]{1,0:T(8,128)} %pack.2.refs_4_), channel_id=1, source_target_pairs={{0,1},{2,0},{4,2},{6,4},{7,6},{5,7},{3,5},{1,3},{8,9},{10,8},{12,1... | collective-permute-start | bytes 1572872 | tf_op jit(solution)/shard_map/ppermute | solution.py:25
  65.1 43.0 %collective-permute-start.14 = (f32[2,2,128,1024]{3,2,1,0:T(8,128)}, f32[2,2,128,1024]{3,2,1,0:T(8,128)}, u32[]{:S(2)}, u32[]{:S(2)}) collective-permute-start(f32[2,2,128,1024]{3,2,1,0:T(8,128)} %collective-permute-done.1.refs_0_.refs_1_.refs_4_.refs_5_), channel_id=1, source_target_pairs={{0,8},{8,0},{16,24},{24,16},{1,9},{9,1},{17,25},{25,17},{2,10},{10... | collective-permute-start | bytes 6291464 | tf_op jit(solution)/shard_map/ppermute | solution.py:29
  65.1 15.0 %collective-permute-start.18 = (f32[512,256]{1,0:T(8,128)}, f32[512,256]{1,0:T(8,128)S(1)}, u32[]{:S(2)}, u32[]{:S(2)}) collective-permute-start(f32[512,256]{1,0:T(8,128)} %copy-done.23), channel_id=1, source_target_pairs={{0,1},{2,0},{4,2},{6,4},{7,6},{5,7},{3,5},{1,3},{8,9},{10,8},{12,1... | collective-permute-start | bytes 1572872 | tf_op jit(solution)/shard_map/ppermute | solution.py:25
  65.7 15.0 %collective-permute-start.15 = (f32[512,256]{1,0:T(8,128)}, f32[512,256]{1,0:T(8,128)S(1)}, u32[]{:S(2)}, u32[]{:S(2)}) collective-permute-start(f32[512,256]{1,0:T(8,128)} %copy-done.24), channel_id=1, source_target_pairs={{0,2},{2,4},{4,6},{6,7},{7,5},{5,3},{3,1},{1,0},{8,10},{10,12},{12... | collective-permute-start | bytes 1572872 | tf_op jit(solution)/shard_map/ppermute | solution.py:25
  67.1 24.9 %collective-permute-start.23 = (f32[512,256]{1,0:T(8,128)}, f32[512,256]{1,0:T(8,128)}, u32[]{:S(2)}, u32[]{:S(2)}) collective-permute-start(f32[512,256]{1,0:T(8,128)} %copy-done.22), channel_id=1, source_target_pairs={{0,2},{2,4},{4,6},{6,7},{7,5},{5,3},{3,1},{1,0},{8,10},{10,12},{12... | collective-permute-start | bytes 1572872 | tf_op jit(solution)/shard_map/ppermute | solution.py:25
  67.8 24.7 %collective-permute-start.25 = (f32[512,256]{1,0:T(8,128)}, f32[512,256]{1,0:T(8,128)}, u32[]{:S(2)}, u32[]{:S(2)}) collective-permute-start(f32[512,256]{1,0:T(8,128)} %copy-done.25), channel_id=1, source_target_pairs={{0,1},{2,0},{4,2},{6,4},{7,6},{5,7},{3,5},{1,3},{8,9},{10,8},{12,1... | collective-permute-start | bytes 1572872 | tf_op jit(solution)/shard_map/ppermute | solution.py:25
  80.1 26.0 %collective-permute-start.19 = (f32[512,256]{1,0:T(8,128)S(1)}, f32[512,256]{1,0:T(8,128)}, u32[]{:S(2)}, u32[]{:S(2)}) collective-permute-start(f32[512,256]{1,0:T(8,128)S(1)} %collective-permute-done.18.refs_7_.refs_13_), channel_id=1, source_target_pairs={{0,1},{2,0},{4,2},{6,4},{7,6},{5,7},{3,5},{1,3},{8,9},{10,8},{12,1... | collective-permute-start | bytes 1572872 | tf_op jit(solution)/shard_map/ppermute | solution.py:25
  80.7 25.6 %collective-permute-start.16 = (f32[512,256]{1,0:T(8,128)S(1)}, f32[512,256]{1,0:T(8,128)}, u32[]{:S(2)}, u32[]{:S(2)}) collective-permute-start(f32[512,256]{1,0:T(8,128)S(1)} %collective-permute-done.15.refs_4_.refs_10_), channel_id=1, source_target_pairs={{0,2},{2,4},{4,6},{6,7},{7,5},{5,3},{3,1},{1,0},{8,10},{10,12},{12... | collective-permute-start | bytes 1572872 | tf_op jit(solution)/shard_map/ppermute | solution.py:25
  92.0 11.9 %collective-permute-start.21 = (f32[8,8,128]{2,1,0:T(8,128)S(1)}, f32[8,8,128]{2,1,0:T(8,128)S(1)}, u32[]{:S(2)}, u32[]{:S(2)}) collective-permute-start(f32[8,8,128]{2,1,0:T(8,128)S(1)} %copy-done.14), channel_id=1, source_target_pairs={{0,16},{8,24},{16,0},{24,8},{1,17},{9,25},{17,1},{25,9},{2,18},{10... | collective-permute-start | bytes 98312 | tf_op jit(solution)/shard_map/ppermute | solution.py:29
  92.5 12.9 %collective-permute-start.22 = (f32[8,8,128]{2,1,0:T(8,128)}, f32[8,8,128]{2,1,0:T(8,128)S(1)}, u32[]{:S(2)}, u32[]{:S(2)}) collective-permute-start(f32[8,8,128]{2,1,0:T(8,128)} %copy-done.15), channel_id=1, source_target_pairs={{0,16},{8,24},{16,0},{24,8},{1,17},{9,25},{17,1},{25,9},{2,18},{10... | collective-permute-start | bytes 98312 | tf_op jit(solution)/shard_map/ppermute | solution.py:29
  104.0 22.8 %collective-permute-start.24 = (f32[512,256]{1,0:T(8,128)}, f32[512,256]{1,0:T(8,128)S(1)}, u32[]{:S(2)}, u32[]{:S(2)}) collective-permute-start(f32[512,256]{1,0:T(8,128)} %collective-permute-done.23.refs_5_.refs_11_), channel_id=1, source_target_pairs={{0,2},{2,4},{4,6},{6,7},{7,5},{5,3},{3,1},{1,0},{8,10},{10,12},{12... | collective-permute-start | bytes 1572872 | tf_op jit(solution)/shard_map/ppermute | solution.py:25
  105.4 21.4 %collective-permute-start.26 = (f32[512,256]{1,0:T(8,128)}, f32[512,256]{1,0:T(8,128)S(1)}, u32[]{:S(2)}, u32[]{:S(2)}) collective-permute-start(f32[512,256]{1,0:T(8,128)} %collective-permute-done.25.refs_6_.refs_12_), channel_id=1, source_target_pairs={{0,1},{2,0},{4,2},{6,4},{7,6},{5,7},{3,5},{1,3},{8,9},{10,8},{12,1... | collective-permute-start | bytes 1572872 | tf_op jit(solution)/shard_map/ppermute | solution.py:25
  106.1 37.5 %collective-permute-start.20 = (f32[512,256]{1,0:T(8,128)}, f32[512,256]{1,0:T(8,128)S(1)}, u32[]{:S(2)}, u32[]{:S(2)}) collective-permute-start(f32[512,256]{1,0:T(8,128)} %collective-permute-done.19.refs_11_), channel_id=1, source_target_pairs={{0,1},{2,0},{4,2},{6,4},{7,6},{5,7},{3,5},{1,3},{8,9},{10,8},{12,1... | collective-permute-start | bytes 1572872 | tf_op jit(solution)/shard_map/ppermute | solution.py:25
  106.3 37.3 %collective-permute-start.17 = (f32[512,256]{1,0:T(8,128)}, f32[512,256]{1,0:T(8,128)S(1)}, u32[]{:S(2)}, u32[]{:S(2)}) collective-permute-start(f32[512,256]{1,0:T(8,128)} %collective-permute-done.16.refs_8_), channel_id=1, source_target_pairs={{0,2},{2,4},{4,6},{6,7},{7,5},{5,3},{3,1},{1,0},{8,10},{10,12},{12... | collective-permute-start | bytes 1572872 | tf_op jit(solution)/shard_map/ppermute | solution.py:25
  156.2 13.2 %collective-permute-start.27 = (f32[256,128]{1,0:T(8,128)S(1)}, f32[256,128]{1,0:T(8,128)S(1)}, u32[]{:S(2)}, u32[]{:S(2)}) collective-permute-start(f32[256,128]{1,0:T(8,128)S(1)} %get-tuple-element.20), channel_id=1, source_target_pairs={{0,0},{1,1},{2,8},{3,9},{4,16},{5,17},{6,24},{7,25},{8,2},{9,3},{1... | collective-permute-start | bytes 393224 | tf_op jit(solution)/shard_map/ppermute | solution.py:470
  159.5 19.2 %collective-permute-start.28 = (f32[256,128]{1,0:T(8,128)S(1)}, f32[256,128]{1,0:T(8,128)S(1)}, u32[]{:S(2)}, u32[]{:S(2)}) collective-permute-start(f32[256,128]{1,0:T(8,128)S(1)} %get-tuple-element.19), channel_id=1, source_target_pairs={{0,1},{1,2},{2,9},{3,10},{4,17},{5,18},{6,25},{7,26},{8,3},{9,4},{... | collective-permute-start | bytes 393224 | tf_op jit(solution)/shard_map/ppermute | solution.py:470
  161.7 17.0 %collective-permute-start.29 = (f32[256,128]{1,0:T(8,128)S(1)}, f32[256,128]{1,0:T(8,128)S(1)}, u32[]{:S(2)}, u32[]{:S(2)}) collective-permute-start(f32[256,128]{1,0:T(8,128)S(1)} %get-tuple-element.18), channel_id=1, source_target_pairs={{0,2},{1,3},{2,10},{3,11},{4,18},{5,19},{6,26},{7,27},{8,4},{9,5},... | collective-permute-start | bytes 393224 | tf_op jit(solution)/shard_map/ppermute | solution.py:470
  163.8 19.4 %collective-permute-start.30 = (f32[256,128]{1,0:T(8,128)S(1)}, f32[256,128]{1,0:T(8,128)S(1)}, u32[]{:S(2)}, u32[]{:S(2)}) collective-permute-start(f32[256,128]{1,0:T(8,128)S(1)} %get-tuple-element.17), channel_id=1, source_target_pairs={{0,3},{1,4},{2,11},{3,12},{4,19},{5,20},{6,27},{7,28},{8,5},{9,6},... | collective-permute-start | bytes 393224 | tf_op jit(solution)/shard_map/ppermute | solution.py:470
  165.1 18.1 %collective-permute-start.31 = (f32[256,128]{1,0:T(8,128)S(1)}, f32[256,128]{1,0:T(8,128)S(1)}, u32[]{:S(2)}, u32[]{:S(2)}) collective-permute-start(f32[256,128]{1,0:T(8,128)S(1)} %get-tuple-element.16), channel_id=1, source_target_pairs={{0,4},{1,5},{2,12},{3,13},{4,20},{5,21},{6,28},{7,29},{8,6},{9,7},... | collective-permute-start | bytes 393224 | tf_op jit(solution)/shard_map/ppermute | solution.py:470
  169.4 13.8 %collective-permute-start.32 = (f32[256,128]{1,0:T(8,128)S(1)}, f32[256,128]{1,0:T(8,128)S(1)}, u32[]{:S(2)}, u32[]{:S(2)}) collective-permute-start(f32[256,128]{1,0:T(8,128)S(1)} %get-tuple-element.15), channel_id=1, source_target_pairs={{0,5},{1,6},{2,13},{3,14},{4,21},{5,22},{6,29},{7,30},{8,7},{9,0},... | collective-permute-start | bytes 393224 | tf_op jit(solution)/shard_map/ppermute | solution.py:470
  178.7 6.2 %collective-permute-start.33 = (f32[256,128]{1,0:T(8,128)S(1)}, f32[256,128]{1,0:T(8,128)S(1)}, u32[]{:S(2)}, u32[]{:S(2)}) collective-permute-start(f32[256,128]{1,0:T(8,128)S(1)} %get-tuple-element.14), channel_id=1, source_target_pairs={{0,6},{1,7},{2,14},{3,15},{4,22},{5,23},{6,30},{7,31},{8,0},{9,1},... | collective-permute-start | bytes 393224 | tf_op jit(solution)/shard_map/ppermute | solution.py:470
  178.8 8.6 %collective-permute-start.34 = (f32[256,128]{1,0:T(8,128)S(1)}, f32[256,128]{1,0:T(8,128)S(1)}, u32[]{:S(2)}, u32[]{:S(2)}) collective-permute-start(f32[256,128]{1,0:T(8,128)S(1)} %get-tuple-element.13), channel_id=1, source_target_pairs={{0,7},{1,0},{2,15},{3,8},{4,23},{5,16},{6,31},{7,24},{8,1},{9,2},{... | collective-permute-start | bytes 393224 | tf_op jit(solution)/shard_map/ppermute | solution.py:470
  (34 other events, 272.4 us)

commit v3 on v2

--- a/solution.py
+++ b/solution.py
@@ -38,7 +38,7 @@
     return lax.broadcasted_iota(jnp.int32, shape, len(shape) - 1) // width
 
 
-def pack_kernel(sc_ref, col_ref, out_ref, *, kw):
+def pack_kernel(col_ref, out_ref, *, kw):
     n_ch, rows, lanes = col_ref.shape
     groups = lanes // kw
     half = groups // 2
@@ -60,38 +60,32 @@
             out_ref[at, lanes:] = pltpu.roll(im, (half - m) * kw, 1)
 
     for m in range(half):
-        pl.when(sc_ref[0] == m)(functools.partial(share, m))
-
-
-def pack(columns, meta, kw, part):
+        pl.when(lax.axis_index("mult") == m)(functools.partial(share, m))
+
+
+def pack(columns, kw, part):
     n_ch, nb, lanes = columns.shape
     nb, steps = nb // 2, 2
     return pl.pallas_call(
         functools.partial(pack_kernel, kw=kw),
         out_shape=jax.ShapeDtypeStruct((nb, 2 * lanes), F32),
-        grid_spec=pltpu.PrefetchScalarGridSpec(
-            num_scalar_prefetch=1,
-            grid=(steps,),
-            in_specs=[pl.BlockSpec((n_ch, nb // steps, lanes), lambda g, sc: (0, part * steps + g, 0))],
-            out_specs=pl.BlockSpec((nb // steps, 2 * lanes), lambda g, sc: (g, 0)),
-        ),
+        grid=(steps,),
+        in_specs=[pl.BlockSpec((n_ch, nb // steps, lanes), lambda g: (0, part * steps + g, 0))],
+        out_specs=pl.BlockSpec((nb // steps, 2 * lanes), lambda g: (g, 0)),
         name="pack",
-    )(meta, columns)
-
-
-def unit_kernel(sc_ref, *refs, n_p, kw, steps, places, fresh):
+    )(columns)
+
+
+def unit_kernel(sc_ref, *refs, n_p, kw, steps, places, fresh, emit):
     n_x = len(places)
     p_refs, x_refs = refs[: 2 * n_p], refs[2 * n_p : 2 * (n_p + n_x)]
     a_refs = refs[2 * (n_p + n_x) : 3 * n_p + 2 * n_x]
-    c_in, c_out, y_ref, w_ref, sem = refs[3 * n_p + 2 * n_x :]
+    c_in, *c_outs, y_ref, w_ref, sem = refs[3 * n_p + 2 * n_x :]
     step = pl.program_id(0)
     n_l, _, rows, _ = p_refs[0].shape
     n_chan, n_ch, _ = a_refs[0].shape
     if fresh:
         fetch = None
-    elif n_x == 1:
-        near = pl.ds(sc_ref[places[0]], SPAN)
-        fetch = pltpu.make_async_copy(c_in.at[near], w_ref, sem.at[0])
     else:
         fetch = pltpu.make_async_copy(c_in, w_ref, sem.at[0])
 
@@ -161,8 +155,8 @@
 
         def kron(c):
             t = jnp.dot(c, spread, preferred_element_type=F32)
-            t = jnp.where(same, t[:, None, :], 0.0)
-            return t.reshape(n * n_ch * kw, wide).astype(BF16)
+            t = jnp.broadcast_to(t.astype(BF16)[:, None, :], (n * n_ch, kw, wide))
+            return jnp.where(same, t, jnp.zeros_like(t)).reshape(n * n_ch * kw, wide)
 
         if not fresh:
             fetch.wait()
@@ -200,20 +194,24 @@
                 preferred_element_type=F32,
             )
             for d in range(SPAN):
-                w_ref[d if n_x == 1 and not fresh else s + d] += out[:, d * lanes : (d + 1) * lanes]
-
-        if n_x == 1 and not fresh:
-            back = pltpu.make_async_copy(w_ref, c_out.at[near], sem.at[1])
-        else:
-            back = pltpu.make_async_copy(w_ref, c_out, sem.at[1])
-        back.start()
-        back.wait()
-
-
-def unit(total, shape, panel_sets, coefs, chunks, meta, kw):
+                w_ref[s + d] += out[:, d * lanes : (d + 1) * lanes]
+
+        backs = []
+        for t, c_out in enumerate(c_outs):
+            block = w_ref
+            if emit:
+                per = n_chan // emit
+                block = w_ref.at[R + lax.rem(sc_ref[0] * per + lax.rem(sc_ref[1], per) + t, n_chan)]
+            backs.append(pltpu.make_async_copy(block, c_out, sem.at[1 + t]))
+            backs[-1].start()
+        for back in backs:
+            back.wait()
+
+
+def unit(total, shape, panel_sets, coefs, chunks, meta, kw, emit=0):
     n_l, _, rows, nb = panel_sets[0].shape
     half = nb // 2
-    steps = max(1, half // LANES)
+    steps = max(1, half // (2 * LANES))
     blk = half // steps
     wide = chunks[0][0].shape[1]
     n = len(panel_sets)
@@ -238,33 +236,36 @@
     in_specs += [pl.BlockSpec(memory_space=pltpu.HBM)]
     args += [*coefs, total]
     flops = 2 * 3 * n * n_l * rows * wide * (2 * nb + SPAN * LANES) * len(chunks)
-    return pl.pallas_call(
+    n_chan = shape[0] - 2 * R
+    outs = [jax.ShapeDtypeStruct(shape[1:], F32)] * n_chan if emit else [jax.ShapeDtypeStruct(shape, F32)]
+    result = pl.pallas_call(
         functools.partial(
-            unit_kernel, n_p=n, kw=kw, steps=steps, places=tuple(c[2] for c in chunks), fresh=fresh
+            unit_kernel, n_p=n, kw=kw, steps=steps, places=tuple(c[2] for c in chunks), fresh=fresh, emit=emit
         ),
-        out_shape=jax.ShapeDtypeStruct(shape, F32),
+        out_shape=outs,
         grid_spec=pltpu.PrefetchScalarGridSpec(
             num_scalar_prefetch=1,
             grid=(steps,),
             in_specs=in_specs,
-            out_specs=pl.BlockSpec(memory_space=pltpu.HBM),
+            out_specs=[pl.BlockSpec(memory_space=pltpu.HBM) for _ in outs],
             scratch_shapes=[
                 pltpu.VMEM((len(chunks), n * n_l * rows, wide), F32),
-                pltpu.VMEM((SPAN,) + shape[1:] if len(chunks) == 1 and not fresh else shape, F32),
-                pltpu.SemaphoreType.DMA((2,)),
+                pltpu.VMEM(shape, F32),
+                pltpu.SemaphoreType.DMA((1 + len(outs),)),
             ],
         ),
-        input_output_aliases={} if fresh else {len(args): 0},
+        input_output_aliases={} if fresh or emit else {len(args): 0},
         cost_estimate=pl.CostEstimate(
             flops=flops, transcendentals=0, bytes_accessed=4 * n * n_l * 2 * rows * nb
         ),
-        compiler_params=pltpu.CompilerParams(vmem_limit_bytes=26 << 20),
+        compiler_params=pltpu.CompilerParams(vmem_limit_bytes=40 << 20),
         name="unit",
     )(
         meta,
         *args[: 2 * n],
         *[pltpu.with_memory_space_constraint(a, pltpu.HBM) for a in args[2 * n :]],
     )
+    return result if emit else result[0]
 
 
 def shift_kernel(sc_ref, energy_ref, contour_ref, col_ref, out_ref):
@@ -296,7 +297,7 @@
 
 
 def finish_kernel(sc_ref, base_ref, *refs, kw, n_mult):
-    pieces, out_ref, held = refs[:-2], refs[-2], refs[-1]
+    pieces, (out_ref, held, pick_ref) = refs[:-3], refs[-3:]
     n_ch, per, sub, lanes = base_ref.shape
     n = len(pieces)
     me = sc_ref[1]
@@ -312,11 +313,16 @@
     )
     vh, vl = split(v)
     both = jnp.concatenate([vh, vl], axis=0)
-    row = lax.broadcasted_iota(jnp.int32, (groups * lanes, lanes), 0)
-    col = lax.broadcasted_iota(jnp.int32, (groups * lanes, lanes), 1)
-    start = (col // kw) * lanes + col % kw
-    picks = jnp.concatenate([(row == start + i * kw).astype(BF16) for i in range(n_ch)], axis=1)
-    out = jnp.dot(both, picks, preferred_element_type=F32)
+
+    @pl.when(pl.program_id(0) == 0)
+    def _():
+        row = lax.broadcasted_iota(jnp.int32, (groups * lanes, lanes), 0)
+        col = lax.broadcasted_iota(jnp.int32, (groups * lanes, lanes), 1)
+        start = (col // kw) * lanes + col % kw
+        for i in range(n_ch):
+            pick_ref[:, i * lanes : (i + 1) * lanes] = (row == start + i * kw).astype(BF16)
+
+    out = jnp.dot(both, pick_ref[...], preferred_element_type=F32)
     out = out[: per * sub] + out[per * sub :]
     for h in range(per):
         for i in range(n_ch):
@@ -337,10 +343,17 @@
             in_specs=[pl.BlockSpec((n_ch, per, sub, lanes), lambda g, sc: (0, 0, g, 0))]
             + [pl.BlockSpec((2, sub, lanes), lambda g, sc: (0, g, 0)) for _ in pieces],
             out_specs=pl.BlockSpec((n_ch, per, sub, lanes), lambda g, sc: (0, 0, g, 0)),
-            scratch_shapes=[pltpu.VMEM((len(pieces), 2, sub, lanes), F32)],
+            scratch_shapes=[
+                pltpu.VMEM((len(pieces), 2, sub, lanes), F32),
+                pltpu.VMEM((2 * n_mult * lanes, n_ch * lanes), BF16),
+            ],
         ),
         name="finish",
-    )(meta, base.reshape(n_ch, per, rows, lanes), *[p.reshape(2, rows, lanes) for p in pieces])
+    )(
+        meta,
+        base.reshape(n_ch, per, rows, lanes),
+        *[pltpu.with_memory_space_constraint(p.reshape(2, rows, lanes), pltpu.HBM) for p in pieces],
+    )
     return out.reshape(n_ch, out_rows, lanes)
 
 
@@ -403,7 +416,7 @@
 
     mine = []
     for part in range(2):
-        mine.append(pack(columns, meta, kw, part))
+        mine.append(pack(columns, kw, part))
     mine[1], coefficients = lax.optimization_barrier((mine[1], coefficients))
     sent = mixing_blocks(
         coefficients, channel_cols, used_slots, lambda_low, lambda_high, chan_index, mult_index
@@ -426,8 +439,8 @@
 
     shape = (n_chan + 2 * R, 2 * rows, LANES)
 
-    def add(total, sets, coefs, chunks):
-        return unit(total, shape, sets, coefs, chunks, meta, kw)
+    def add(total, sets, coefs, chunks, emit=0):
+        return unit(total, shape, sets, coefs, chunks, meta, kw, emit)
 
     full_steps, switch = steps_of(n_chan)
     total = None
@@ -452,13 +465,13 @@
                 bit //= 2
         if step == switch:
             total = add(total, far, far_coefs, late)
-    if n_chan % 2 == 0:
-        top = ring_shift(ahead[0], "chan", 1)
-        bottom = ring_shift(behind[1], "chan", -1)
-        total = add(total, near_sets + far, near_coefs + far_coefs, [(top, bottom, spot(n_chan // 2))])
+    top = ring_shift(ahead[0], "chan", 1)
+    bottom = ring_shift(behind[1], "chan", -1)
+    sends = add(
+        total, near_sets + far, near_coefs + far_coefs, [(top, bottom, spot(n_chan // 2))], n_mult
+    )
 
     per = n_chan // n_mult
-    mine_q = mult_index * per + lax.rem(chan_index, per)
     pieces = []
     for s in range(n_chan):
         pairs = []
@@ -466,8 +479,7 @@
             for c in range(n_chan):
                 q = m * per + c % per
                 pairs.append((m * n_chan + c, (c // per) * n_chan + (q + s) % n_chan))
-        piece = lax.dynamic_index_in_dim(total, R + lax.rem(mine_q + s, n_chan), 0, keepdims=False)
-        pieces.append(lax.ppermute(piece, ("mult", "chan"), pairs))
+        pieces.append(lax.ppermute(sends[s], ("mult", "chan"), pairs))
     base = shifted_columns(columns, energies, contour, meta, n_mult)
     return finish(pieces, base, meta, kw, n_mult)
 

time: 193 us -> 188 us (0.974)
  the two profiles are of different devices: /device:TPU:2 before, /device:TPU:6 now
where the time goes in v3:
time: 188 us
  Pallas kernels  79.5 us (42%)
  waiting for transfers between devices  64 us (34%)
  starting transfers between devices  37.8 us (20%)
  local copies, waits for them, and re-layouts  5.95 us (3%)
    pallas_call x5, Pallas kernels, unit(): pl.pallas_call(functools.partial(unit_kernel, n_p=n, kw=kw, steps=steps,...  62.9 us
    ppermute x14, waiting for transfers between devices, ring_shift(): lax.ppermute(value, axis, [(order[i], order[(i + by) % n]) for i in range...  38.9 us
    ppermute x8, waiting for transfers between devices, body(): pieces.append(lax.ppermute(sends[s], ('mult', 'chan'), pairs))  19.1 us
    ppermute x14, starting transfers between devices, ring_shift(): lax.ppermute(value, axis, [(order[i], order[(i + by) % n]) for i in range...  14.7 us
    ppermute x7, starting transfers between devices, body(): lax.ppermute(sent, 'chan', [(i, (i + by) % n_chan) for i in range(n_chan)])  11.5 us
    ppermute x8, starting transfers between devices, body(): pieces.append(lax.ppermute(sends[s], ('mult', 'chan'), pairs))  9.11 us
    pallas_call x2, Pallas kernels, pack(): pl.pallas_call(functools.partial(pack_kernel, kw=kw), out_shape=jax.Shape...  7.31 us
    unnamed x73, local copies, waits for them, and re-layouts  5.13 us
  transfers between devices with their start and end apart: 35, of which 12 were waited for; matrix products, arithmetic and copies ran while one was open for 0% of the time, Pallas kernels for 32%

profile of v3, /device:TPU:6, one launch (start us, length us, event | category | flops | bytes accessed | tf_op | source)
XLA Modules:
  0.0 188.1 jit_solution(5466323006827073859)
XLA Ops:
  0.1 3.7 %pack.3.refs_5_ = f32[512,256]{1,0:T(8,128)} custom-call(f32[8,1024,128]{2,1,0:T(8,128)} %col_ref.5), custom_call_target="tpu_custom_call" | custom-call | tf_op jit(solution)/shard_map/pack/pallas_call | solution.py:69
  4.3 1.6 collective-permute-start.6
  5.9 1.6 collective-permute-start.7
  7.5 2.5 %collective-permute-start.8 = (f32[8,128]{1,0:T(8,128)S(1)}, f32[8,128]{1,0:T(8,128)S(1)}, u32[]{:S(2)}, u32[]{:S(2)}) collective-permute-start(f32[8,128]{1,0:T(8,128)S(1)} %select_reduce_fusion), channel_id=1, source_target_pairs={{0,3},{1,4},{2,5},{3,6},{4,7},{5,0},{6,1},{7,2},{8,11},{9,12},{10,... | collective-permute-start | bytes 12296 | tf_op jit(solution)/shard_map/ppermute | solution.py:427
  10.4 2.2 %collective-permute-start.10 = (f32[8,128]{1,0:T(8,128)S(1)}, f32[8,128]{1,0:T(8,128)S(1)}, u32[]{:S(2)}, u32[]{:S(2)}) collective-permute-start(f32[8,128]{1,0:T(8,128)S(1)} %select_reduce_fusion), channel_id=1, source_target_pairs={{0,5},{1,6},{2,7},{3,0},{4,1},{5,2},{6,3},{7,4},{8,13},{9,14},{10,... | collective-permute-start | bytes 12296 | tf_op jit(solution)/shard_map/ppermute | solution.py:427
  12.6 1.9 collective-permute-start.11
  17.8 1.7 collective-permute-done.12
  19.7 3.6 %pack.2.refs_4_ = f32[512,256]{1,0:T(8,128)} custom-call(f32[8,1024,128]{2,1,0:T(8,128)} %col_ref.5), custom_call_target="tpu_custom_call" | custom-call | tf_op jit(solution)/shard_map/pack/pallas_call | solution.py:69
  23.2 2.0 %collective-permute-start.2 = (f32[512,256]{1,0:T(8,128)}, f32[512,256]{1,0:T(8,128)}, u32[]{:S(2)}, u32[]{:S(2)}) collective-permute-start(f32[512,256]{1,0:T(8,128)} %pack.2.refs_4_), channel_id=1, source_target_pairs={{0,2},{2,4},{4,6},{6,7},{7,5},{5,3},{3,1},{1,0},{8,10},{10,12},{12... | collective-permute-start | bytes 1572872 | tf_op jit(solution)/shard_map/ppermute | solution.py:25
  25.2 6.2 %collective-permute-done.3.refs_7_ = f32[512,256]{1,0:T(8,128)S(1)} collective-permute-done((f32[512,256]{1,0:T(8,128)}, f32[512,256]{1,0:T(8,128)S(1)}, u32[]{:S(2)}, u32[]{:S(2)}) %collective-permute-start.3) | collective-permute-done | bytes 524320 | tf_op jit(solution)/shard_map/ppermute | solution.py:25
  34.5 6.8 %collective-permute-done.2.refs_6_ = f32[512,256]{1,0:T(8,128)} collective-permute-done((f32[512,256]{1,0:T(8,128)}, f32[512,256]{1,0:T(8,128)}, u32[]{:S(2)}, u32[]{:S(2)}) %collective-permute-start.2) | collective-permute-done | bytes 524320 | tf_op jit(solution)/shard_map/ppermute | solution.py:25
  41.4 4.0 %collective-permute-done.4.refs_8_ = f32[512,256]{1,0:T(8,128)} collective-permute-done((f32[512,256]{1,0:T(8,128)}, f32[512,256]{1,0:T(8,128)}, u32[]{:S(2)}, u32[]{:S(2)}) %collective-permute-start.4) | collective-permute-done | bytes 524320 | tf_op jit(solution)/shard_map/ppermute | solution.py:25
  45.4 11.3 %unit.5.refs_10_ = f32[12,256,128]{2,1,0:T(8,128)S(1)} custom-call(s32[11]{0:T(128)S(1)} %pad_add_fusion.sc_ref, f32[2,2,128,1024]{3,2,1,0:T(8,128)S(1)} %copy-done, f32[2,2,128,1024]{3,2,1,0:T(8,128)S(1)} %copy-done, f32[2,2,128,1024]{3,2,1,0:T(8,128)} %collective-permute-done.refs_2_.refs_3_, f32[2,2,128,1024]{3,2,1,0:T(8,128)} %collective-permute-done.refs_2_.refs_3_, ...), custom_call_target="tpu_custom_call" | custom-call | flops 6341787648 | bytes 4194304 | tf_op jit(solution)/shard_map/unit/pallas_call | solution.py:241
  57.9 4.4 %collective-permute-done.1.refs_0_.refs_1_.refs_4_.refs_5_ = f32[2,2,128,1024]{3,2,1,0:T(8,128)} collective-permute-done((f32[2,2,128,1024]{3,2,1,0:T(8,128)S(1)}, f32[2,2,128,1024]{3,2,1,0:T(8,128)}, u32[]{:S(2)}, u32[]{:S(2)}) %collective-permute-start.1) | collective-permute-done | bytes 2097184 | tf_op jit(solution)/shard_map/ppermute | solution.py:29
  62.5 1.8 collective-permute-start.15
  66.4 11.0 %collective-permute-done.18.refs_7_.refs_13_ = f32[512,256]{1,0:T(8,128)S(1)} collective-permute-done((f32[512,256]{1,0:T(8,128)}, f32[512,256]{1,0:T(8,128)S(1)}, u32[]{:S(2)}, u32[]{:S(2)}) %collective-permute-start.18) | collective-permute-done | bytes 524320 | tf_op jit(solution)/shard_map/ppermute | solution.py:25
  77.5 1.8 collective-permute-start.16
  79.3 9.4 %collective-permute-done.23.refs_5_.refs_11_ = f32[512,256]{1,0:T(8,128)S(1)} collective-permute-done((f32[512,256]{1,0:T(8,128)}, f32[512,256]{1,0:T(8,128)S(1)}, u32[]{:S(2)}, u32[]{:S(2)}) %collective-permute-start.23) | collective-permute-done | bytes 524320 | tf_op jit(solution)/shard_map/ppermute | solution.py:25
  89.1 1.7 collective-permute-start.22
  90.8 9.3 %unit.6.refs_16_ = f32[12,256,128]{2,1,0:T(8,128)} custom-call(s32[11]{0:T(128)S(1)} %pad_add_fusion.sc_ref, f32[2,2,128,1024]{3,2,1,0:T(8,128)S(1)} %copy-done, f32[2,2,128,1024]{3,2,1,0:T(8,128)S(1)} %copy-done, f32[2,2,128,1024]{3,2,1,0:T(8,128)} %collective-permute-done.refs_2_.refs_3_, ...), custom_call_target="tpu_custom_call", output_to_operand_aliasing={{}: (11, {})} | custom-call | flops 4227858432 | bytes 4194304 | tf_op jit(solution)/shard_map/unit/pallas_call | solution.py:241
  100.2 1.9 collective-permute-start.24
  104.3 18.1 %unit.7.refs_16_ = f32[12,256,128]{2,1,0:T(8,128)} custom-call(s32[11]{0:T(128)S(1)} %pad_add_fusion.sc_ref, f32[2,2,128,1024]{3,2,1,0:T(8,128)} %collective-permute-done.1.refs_0_.refs_1_.refs_4_.refs_5_, f32[2,2,128,1024]{3,2,1,0:T(8,128)} %collective-permute-done.1.refs_0_.refs_1_.refs_4_.refs_5_, ...), custom_call_target="tpu_custom_call", output_to_operand_aliasing={{}: (17, {})} | custom-call | flops 10569646080 | bytes 4194304 | tf_op jit(solution)/shard_map/unit/pallas_call | solution.py:241
  124.0 14.4 %unit.8.refs_14_ = f32[12,256,128]{2,1,0:T(8,128)} custom-call(s32[11]{0:T(128)S(1)} %pad_add_fusion.sc_ref, f32[2,2,128,1024]{3,2,1,0:T(8,128)S(1)} %copy-done, f32[2,2,128,1024]{3,2,1,0:T(8,128)S(1)} %copy-done, f32[2,2,128,1024]{3,2,1,0:T(8,128)} %collective-permute-done.refs_2_.refs_3_, ...), custom_call_target="tpu_custom_call", output_to_operand_aliasing={{}: (17, {})} | custom-call | flops 8455716864 | bytes 8388608 | tf_op jit(solution)/shard_map/unit/pallas_call | solution.py:241
  140.0 9.9 %unit.9 = (f32[256,128]{1,0:T(8,128)S(1)}, f32[256,128]{1,0:T(8,128)S(1)}, f32[256,128]{1,0:T(8,128)S(1)}, f32[256,128]{1,0:T(8,128)S(1)}, f32[256,128]{1,0:T(8,...) custom-call(s32[11]{0:T(128)S(1)} %pad_add_fusion.sc_ref, ...), custom_call_target="tpu_custom_call" | custom-call | flops 4227858432 | bytes 8388608 | tf_op jit(solution)/shard_map/unit/pallas_call | solution.py:241
  149.9 3.7 %collective-permute-start.27 = (f32[256,128]{1,0:T(8,128)S(1)}, f32[256,128]{1,0:T(8,128)S(1)}, u32[]{:S(2)}, u32[]{:S(2)}) collective-permute-start(f32[256,128]{1,0:T(8,128)S(1)} %get-tuple-element.21), channel_id=1, source_target_pairs={{0,0},{1,1},{2,8},{3,9},{4,16},{5,17},{6,24},{7,25},{8,2},{9,3},{1... | collective-permute-start | bytes 393224 | tf_op jit(solution)/shard_map/ppermute | solution.py:482
  156.0 3.1 %collective-permute-start.31 = (f32[256,128]{1,0:T(8,128)S(1)}, f32[256,128]{1,0:T(8,128)S(1)}, u32[]{:S(2)}, u32[]{:S(2)}) collective-permute-start(f32[256,128]{1,0:T(8,128)S(1)} %get-tuple-element.25), channel_id=1, source_target_pairs={{0,4},{1,5},{2,12},{3,13},{4,20},{5,21},{6,28},{7,29},{8,6},{9,7},... | collective-permute-start | bytes 393224 | tf_op jit(solution)/shard_map/ppermute | solution.py:482
  159.0 1.8 collective-permute-done.27
  160.8 9.9 %collective-permute-done.28 = f32[256,128]{1,0:T(8,128)S(1)} collective-permute-done((f32[256,128]{1,0:T(8,128)S(1)}, f32[256,128]{1,0:T(8,128)S(1)}, u32[]{:S(2)}, u32[]{:S(2)}) %collective-permute-start.28) | collective-permute-done | bytes 131104 | tf_op jit(solution)/shard_map/ppermute | solution.py:482
  170.7 4.8 %collective-permute-done.29 = f32[256,128]{1,0:T(8,128)S(1)} collective-permute-done((f32[256,128]{1,0:T(8,128)S(1)}, f32[256,128]{1,0:T(8,128)S(1)}, u32[]{:S(2)}, u32[]{:S(2)}) %collective-permute-start.29) | collective-permute-done | bytes 131104 | tf_op jit(solution)/shard_map/ppermute | solution.py:482
  175.4 4.4 %shifted.1 = f32[8,256,128]{2,1,0:T(8,128)} custom-call(s32[11]{0:T(128)} %copy-done.2, f32[8]{0:T(128)} %energy_ref.1, f32[2]{0:T(128)} %contour_ref.1, f32[8,1024,128]{2,1,0:T(8,128)} %col_ref.5), custom_call_target="tpu_custom_call" | custom-call | tf_op jit(solution)/shard_map/shifted/pallas_call | solution.py:286
  179.9 2.6 %collective-permute-done.34 = f32[256,128]{1,0:T(8,128)S(1)} collective-permute-done((f32[256,128]{1,0:T(8,128)S(1)}, f32[256,128]{1,0:T(8,128)S(1)}, u32[]{:S(2)}, u32[]{:S(2)}) %collective-permute-start.34) | collective-permute-done | bytes 131104 | tf_op jit(solution)/shard_map/ppermute | solution.py:482
  183.2 4.9 %finish.1 = f32[8,2,128,128]{3,2,1,0:T(8,128)} custom-call(s32[11]{0:T(128)} %copy-done.2, f32[8,2,128,128]{3,2,1,0:T(8,128)} %bitcast.47, f32[2,128,128]{2,1,0:T(8,128)} %bitcast.48, f32[2,128,128]{2,1,0:T(8,128)} %bitcast.49, f32[2,128,128]{2,1,0:T(8,128)} %bitcast.50, f32[2,128,128]{2,1,0:T(8,128)} %bitcast.51, f32[2,128,128]{2,1,0:T(8,128)} %bitcast.52, ...), custom_call_target="tpu_custom_call" | custom-call | tf_op jit(solution)/shard_map/finish/pallas_call | solution.py:337
  (137 shorter events, 20.1 us)
Async XLA Ops:
  4.3 8.2 %collective-permute-start.6 = (f32[8,128]{1,0:T(8,128)S(1)}, f32[8,128]{1,0:T(8,128)S(1)}, u32[]{:S(2)}, u32[]{:S(2)}) collective-permute-start(f32[8,128]{1,0:T(8,128)S(1)} %select_reduce_fusion), channel_id=1, source_target_pairs={{0,1},{1,2},{2,3},{3,4},{4,5},{5,6},{6,7},{7,0},{8,9},{9,10},{10,1... | collective-permute-start | bytes 12296 | tf_op jit(solution)/shard_map/ppermute | solution.py:427
  5.9 6.7 %collective-permute-start.7 = (f32[8,128]{1,0:T(8,128)S(1)}, f32[8,128]{1,0:T(8,128)S(1)}, u32[]{:S(2)}, u32[]{:S(2)}) collective-permute-start(f32[8,128]{1,0:T(8,128)S(1)} %select_reduce_fusion), channel_id=1, source_target_pairs={{0,2},{1,3},{2,4},{3,5},{4,6},{5,7},{6,0},{7,1},{8,10},{9,11},{10,... | collective-permute-start | bytes 12296 | tf_op jit(solution)/shard_map/ppermute | solution.py:427
  7.5 7.0 %collective-permute-start.8 = (f32[8,128]{1,0:T(8,128)S(1)}, f32[8,128]{1,0:T(8,128)S(1)}, u32[]{:S(2)}, u32[]{:S(2)}) collective-permute-start(f32[8,128]{1,0:T(8,128)S(1)} %select_reduce_fusion), channel_id=1, source_target_pairs={{0,3},{1,4},{2,5},{3,6},{4,7},{5,0},{6,1},{7,2},{8,11},{9,12},{10,... | collective-permute-start | bytes 12296 | tf_op jit(solution)/shard_map/ppermute | solution.py:427
  10.4 6.0 %collective-permute-start.10 = (f32[8,128]{1,0:T(8,128)S(1)}, f32[8,128]{1,0:T(8,128)S(1)}, u32[]{:S(2)}, u32[]{:S(2)}) collective-permute-start(f32[8,128]{1,0:T(8,128)S(1)} %select_reduce_fusion), channel_id=1, source_target_pairs={{0,5},{1,6},{2,7},{3,0},{4,1},{5,2},{6,3},{7,4},{8,13},{9,14},{10,... | collective-permute-start | bytes 12296 | tf_op jit(solution)/shard_map/ppermute | solution.py:427
  12.6 32.8 %collective-permute-start = (f32[2,2,128,1024]{3,2,1,0:T(8,128)S(1)}, f32[2,2,128,1024]{3,2,1,0:T(8,128)}, u32[]{:S(2)}, u32[]{:S(2)}) collective-permute-start(f32[2,2,128,1024]{3,2,1,0:T(8,128)S(1)} %copy-done), channel_id=1, source_target_pairs={{0,8},{8,0},{16,24},{24,16},{1,9},{9,1},{17,25},{25,17},{2,10},{10... | collective-permute-start | bytes 6291464 | tf_op jit(solution)/shard_map/ppermute | solution.py:29
  12.6 5.2 %collective-permute-start.11 = (f32[8,128]{1,0:T(8,128)S(1)}, f32[8,128]{1,0:T(8,128)S(1)}, u32[]{:S(2)}, u32[]{:S(2)}) collective-permute-start(f32[8,128]{1,0:T(8,128)S(1)} %select_reduce_fusion), channel_id=1, source_target_pairs={{0,6},{1,7},{2,0},{3,1},{4,2},{5,3},{6,4},{7,5},{8,14},{9,15},{10,... | collective-permute-start | bytes 12296 | tf_op jit(solution)/shard_map/ppermute | solution.py:427
  14.5 47.8 %collective-permute-start.1 = (f32[2,2,128,1024]{3,2,1,0:T(8,128)S(1)}, f32[2,2,128,1024]{3,2,1,0:T(8,128)}, u32[]{:S(2)}, u32[]{:S(2)}) collective-permute-start(f32[2,2,128,1024]{3,2,1,0:T(8,128)S(1)} %copy-done), channel_id=1, source_target_pairs={{0,16},{8,24},{16,0},{24,8},{1,17},{9,25},{17,1},{25,9},{2,18},{10... | collective-permute-start | bytes 6291464 | tf_op jit(solution)/shard_map/ppermute | solution.py:29
  16.4 15.0 %collective-permute-start.3 = (f32[512,256]{1,0:T(8,128)}, f32[512,256]{1,0:T(8,128)S(1)}, u32[]{:S(2)}, u32[]{:S(2)}) collective-permute-start(f32[512,256]{1,0:T(8,128)} %pack.3.refs_5_), channel_id=1, source_target_pairs={{0,2},{2,4},{4,6},{6,7},{7,5},{5,3},{3,1},{1,0},{8,10},{10,12},{12... | collective-permute-start | bytes 1572872 | tf_op jit(solution)/shard_map/ppermute | solution.py:25
  19.5 15.1 %collective-permute-start.5 = (f32[512,256]{1,0:T(8,128)}, f32[512,256]{1,0:T(8,128)S(1)}, u32[]{:S(2)}, u32[]{:S(2)}) collective-permute-start(f32[512,256]{1,0:T(8,128)} %pack.3.refs_5_), channel_id=1, source_target_pairs={{0,1},{2,0},{4,2},{6,4},{7,6},{5,7},{3,5},{1,3},{8,9},{10,8},{12,1... | collective-permute-start | bytes 1572872 | tf_op jit(solution)/shard_map/ppermute | solution.py:25
  23.2 18.1 %collective-permute-start.2 = (f32[512,256]{1,0:T(8,128)}, f32[512,256]{1,0:T(8,128)}, u32[]{:S(2)}, u32[]{:S(2)}) collective-permute-start(f32[512,256]{1,0:T(8,128)} %pack.2.refs_4_), channel_id=1, source_target_pairs={{0,2},{2,4},{4,6},{6,7},{7,5},{5,3},{3,1},{1,0},{8,10},{10,12},{12... | collective-permute-start | bytes 1572872 | tf_op jit(solution)/shard_map/ppermute | solution.py:25
  31.4 14.0 %collective-permute-start.4 = (f32[512,256]{1,0:T(8,128)}, f32[512,256]{1,0:T(8,128)}, u32[]{:S(2)}, u32[]{:S(2)}) collective-permute-start(f32[512,256]{1,0:T(8,128)} %pack.2.refs_4_), channel_id=1, source_target_pairs={{0,1},{2,0},{4,2},{6,4},{7,6},{5,7},{3,5},{1,3},{8,9},{10,8},{12,1... | collective-permute-start | bytes 1572872 | tf_op jit(solution)/shard_map/ppermute | solution.py:25
  62.3 42.0 %collective-permute-start.14 = (f32[2,2,128,1024]{3,2,1,0:T(8,128)}, f32[2,2,128,1024]{3,2,1,0:T(8,128)S(1)}, u32[]{:S(2)}, u32[]{:S(2)}) collective-permute-start(f32[2,2,128,1024]{3,2,1,0:T(8,128)} %collective-permute-done.1.refs_0_.refs_1_.refs_4_.refs_5_), channel_id=1, source_target_pairs={{0,8},{8,0},{16,24},{24,16},{1,9},{9,1},{17,25},{25,17},{2,10},{10... | collective-permute-start | bytes 6291464 | tf_op jit(solution)/shard_map/ppermute | solution.py:29
  62.3 15.0 %collective-permute-start.18 = (f32[512,256]{1,0:T(8,128)}, f32[512,256]{1,0:T(8,128)S(1)}, u32[]{:S(2)}, u32[]{:S(2)}) collective-permute-start(f32[512,256]{1,0:T(8,128)} %copy-done.23), channel_id=1, source_target_pairs={{0,1},{2,0},{4,2},{6,4},{7,6},{5,7},{3,5},{1,3},{8,9},{10,8},{12,1... | collective-permute-start | bytes 1572872 | tf_op jit(solution)/shard_map/ppermute | solution.py:25
  62.5 15.0 %collective-permute-start.15 = (f32[512,256]{1,0:T(8,128)}, f32[512,256]{1,0:T(8,128)S(1)}, u32[]{:S(2)}, u32[]{:S(2)}) collective-permute-start(f32[512,256]{1,0:T(8,128)} %collective-permute-done.2.refs_6_), channel_id=1, source_target_pairs={{0,2},{2,4},{4,6},{6,7},{7,5},{5,3},{3,1},{1,0},{8,10},{10,12},{12... | collective-permute-start | bytes 1572872 | tf_op jit(solution)/shard_map/ppermute | solution.py:25
  64.3 24.4 %collective-permute-start.23 = (f32[512,256]{1,0:T(8,128)}, f32[512,256]{1,0:T(8,128)S(1)}, u32[]{:S(2)}, u32[]{:S(2)}) collective-permute-start(f32[512,256]{1,0:T(8,128)} %copy-done.22), channel_id=1, source_target_pairs={{0,2},{2,4},{4,6},{6,7},{7,5},{5,3},{3,1},{1,0},{8,10},{10,12},{12... | collective-permute-start | bytes 1572872 | tf_op jit(solution)/shard_map/ppermute | solution.py:25
  65.7 23.4 %collective-permute-start.25 = (f32[512,256]{1,0:T(8,128)}, f32[512,256]{1,0:T(8,128)S(1)}, u32[]{:S(2)}, u32[]{:S(2)}) collective-permute-start(f32[512,256]{1,0:T(8,128)} %collective-permute-done.4.refs_8_), channel_id=1, source_target_pairs={{0,1},{2,0},{4,2},{6,4},{7,6},{5,7},{3,5},{1,3},{8,9},{10,8},{12,1... | collective-permute-start | bytes 1572872 | tf_op jit(solution)/shard_map/ppermute | solution.py:25
  77.3 24.9 %collective-permute-start.19 = (f32[512,256]{1,0:T(8,128)S(1)}, f32[512,256]{1,0:T(8,128)S(1)}, u32[]{:S(2)}, u32[]{:S(2)}) collective-permute-start(f32[512,256]{1,0:T(8,128)S(1)} %collective-permute-done.18.refs_7_.refs_13_), channel_id=1, source_target_pairs={{0,1},{2,0},{4,2},{6,4},{7,6},{5,7},{3,5},{1,3},{8,9},{10,8},{12,1... | collective-permute-start | bytes 1572872 | tf_op jit(solution)/shard_map/ppermute | solution.py:25
  77.5 25.4 %collective-permute-start.16 = (f32[512,256]{1,0:T(8,128)S(1)}, f32[512,256]{1,0:T(8,128)S(1)}, u32[]{:S(2)}, u32[]{:S(2)}) collective-permute-start(f32[512,256]{1,0:T(8,128)S(1)} %collective-permute-done.15.refs_4_.refs_10_), channel_id=1, source_target_pairs={{0,2},{2,4},{4,6},{6,7},{7,5},{5,3},{3,1},{1,0},{8,10},{10,12},{12... | collective-permute-start | bytes 1572872 | tf_op jit(solution)/shard_map/ppermute | solution.py:25
  88.8 11.4 %collective-permute-start.21 = (f32[8,8,128]{2,1,0:T(8,128)S(1)}, f32[8,8,128]{2,1,0:T(8,128)S(1)}, u32[]{:S(2)}, u32[]{:S(2)}) collective-permute-start(f32[8,8,128]{2,1,0:T(8,128)S(1)} %copy-done.14), channel_id=1, source_target_pairs={{0,16},{8,24},{16,0},{24,8},{1,17},{9,25},{17,1},{25,9},{2,18},{10... | collective-permute-start | bytes 98312 | tf_op jit(solution)/shard_map/ppermute | solution.py:29
  89.1 12.9 %collective-permute-start.22 = (f32[8,8,128]{2,1,0:T(8,128)}, f32[8,8,128]{2,1,0:T(8,128)S(1)}, u32[]{:S(2)}, u32[]{:S(2)}) collective-permute-start(f32[8,8,128]{2,1,0:T(8,128)} %copy-done.15), channel_id=1, source_target_pairs={{0,16},{8,24},{16,0},{24,8},{1,17},{9,25},{17,1},{25,9},{2,18},{10... | collective-permute-start | bytes 98312 | tf_op jit(solution)/shard_map/ppermute | solution.py:29
  100.2 22.3 %collective-permute-start.24 = (f32[512,256]{1,0:T(8,128)}, f32[512,256]{1,0:T(8,128)S(1)}, u32[]{:S(2)}, u32[]{:S(2)}) collective-permute-start(f32[512,256]{1,0:T(8,128)} %copy-done.27), channel_id=1, source_target_pairs={{0,2},{2,4},{4,6},{6,7},{7,5},{5,3},{3,1},{1,0},{8,10},{10,12},{12... | collective-permute-start | bytes 1572872 | tf_op jit(solution)/shard_map/ppermute | solution.py:25
  102.0 20.4 %collective-permute-start.26 = (f32[512,256]{1,0:T(8,128)}, f32[512,256]{1,0:T(8,128)S(1)}, u32[]{:S(2)}, u32[]{:S(2)}) collective-permute-start(f32[512,256]{1,0:T(8,128)} %copy-done.28), channel_id=1, source_target_pairs={{0,1},{2,0},{4,2},{6,4},{7,6},{5,7},{3,5},{1,3},{8,9},{10,8},{12,1... | collective-permute-start | bytes 1572872 | tf_op jit(solution)/shard_map/ppermute | solution.py:25
  102.3 36.2 %collective-permute-start.20 = (f32[512,256]{1,0:T(8,128)S(1)}, f32[512,256]{1,0:T(8,128)S(1)}, u32[]{:S(2)}, u32[]{:S(2)}) collective-permute-start(f32[512,256]{1,0:T(8,128)S(1)} %collective-permute-done.19.refs_11_), channel_id=1, source_target_pairs={{0,1},{2,0},{4,2},{6,4},{7,6},{5,7},{3,5},{1,3},{8,9},{10,8},{12,1... | collective-permute-start | bytes 1572872 | tf_op jit(solution)/shard_map/ppermute | solution.py:25
  102.9 35.5 %collective-permute-start.17 = (f32[512,256]{1,0:T(8,128)S(1)}, f32[512,256]{1,0:T(8,128)S(1)}, u32[]{:S(2)}, u32[]{:S(2)}) collective-permute-start(f32[512,256]{1,0:T(8,128)S(1)} %collective-permute-done.16.refs_8_), channel_id=1, source_target_pairs={{0,2},{2,4},{4,6},{6,7},{7,5},{5,3},{3,1},{1,0},{8,10},{10,12},{12... | collective-permute-start | bytes 1572872 | tf_op jit(solution)/shard_map/ppermute | solution.py:25
  149.9 10.9 %collective-permute-start.27 = (f32[256,128]{1,0:T(8,128)S(1)}, f32[256,128]{1,0:T(8,128)S(1)}, u32[]{:S(2)}, u32[]{:S(2)}) collective-permute-start(f32[256,128]{1,0:T(8,128)S(1)} %get-tuple-element.21), channel_id=1, source_target_pairs={{0,0},{1,1},{2,8},{3,9},{4,16},{5,17},{6,24},{7,25},{8,2},{9,3},{1... | collective-permute-start | bytes 393224 | tf_op jit(solution)/shard_map/ppermute | solution.py:482
  153.7 17.0 %collective-permute-start.28 = (f32[256,128]{1,0:T(8,128)S(1)}, f32[256,128]{1,0:T(8,128)S(1)}, u32[]{:S(2)}, u32[]{:S(2)}) collective-permute-start(f32[256,128]{1,0:T(8,128)S(1)} %get-tuple-element.22), channel_id=1, source_target_pairs={{0,1},{1,2},{2,9},{3,10},{4,17},{5,18},{6,25},{7,26},{8,3},{9,4},{... | collective-permute-start | bytes 393224 | tf_op jit(solution)/shard_map/ppermute | solution.py:482
  154.5 20.9 %collective-permute-start.29 = (f32[256,128]{1,0:T(8,128)S(1)}, f32[256,128]{1,0:T(8,128)S(1)}, u32[]{:S(2)}, u32[]{:S(2)}) collective-permute-start(f32[256,128]{1,0:T(8,128)S(1)} %get-tuple-element.23), channel_id=1, source_target_pairs={{0,2},{1,3},{2,10},{3,11},{4,18},{5,19},{6,26},{7,27},{8,4},{9,5},... | collective-permute-start | bytes 393224 | tf_op jit(solution)/shard_map/ppermute | solution.py:482
  155.0 24.8 %collective-permute-start.30 = (f32[256,128]{1,0:T(8,128)S(1)}, f32[256,128]{1,0:T(8,128)S(1)}, u32[]{:S(2)}, u32[]{:S(2)}) collective-permute-start(f32[256,128]{1,0:T(8,128)S(1)} %get-tuple-element.24), channel_id=1, source_target_pairs={{0,3},{1,4},{2,11},{3,12},{4,19},{5,20},{6,27},{7,28},{8,5},{9,6},... | collective-permute-start | bytes 393224 | tf_op jit(solution)/shard_map/ppermute | solution.py:482
  156.0 23.9 %collective-permute-start.31 = (f32[256,128]{1,0:T(8,128)S(1)}, f32[256,128]{1,0:T(8,128)S(1)}, u32[]{:S(2)}, u32[]{:S(2)}) collective-permute-start(f32[256,128]{1,0:T(8,128)S(1)} %get-tuple-element.25), channel_id=1, source_target_pairs={{0,4},{1,5},{2,12},{3,13},{4,20},{5,21},{6,28},{7,29},{8,6},{9,7},... | collective-permute-start | bytes 393224 | tf_op jit(solution)/shard_map/ppermute | solution.py:482
  160.8 19.1 %collective-permute-start.32 = (f32[256,128]{1,0:T(8,128)S(1)}, f32[256,128]{1,0:T(8,128)S(1)}, u32[]{:S(2)}, u32[]{:S(2)}) collective-permute-start(f32[256,128]{1,0:T(8,128)S(1)} %get-tuple-element.26), channel_id=1, source_target_pairs={{0,5},{1,6},{2,13},{3,14},{4,21},{5,22},{6,29},{7,30},{8,7},{9,0},... | collective-permute-start | bytes 393224 | tf_op jit(solution)/shard_map/ppermute | solution.py:482
  170.7 9.2 %collective-permute-start.33 = (f32[256,128]{1,0:T(8,128)S(1)}, f32[256,128]{1,0:T(8,128)S(1)}, u32[]{:S(2)}, u32[]{:S(2)}) collective-permute-start(f32[256,128]{1,0:T(8,128)S(1)} %get-tuple-element.27), channel_id=1, source_target_pairs={{0,6},{1,7},{2,14},{3,15},{4,22},{5,23},{6,30},{7,31},{8,0},{9,1},... | collective-permute-start | bytes 393224 | tf_op jit(solution)/shard_map/ppermute | solution.py:482
  175.4 7.1 %collective-permute-start.34 = (f32[256,128]{1,0:T(8,128)S(1)}, f32[256,128]{1,0:T(8,128)S(1)}, u32[]{:S(2)}, u32[]{:S(2)}) collective-permute-start(f32[256,128]{1,0:T(8,128)S(1)} %get-tuple-element.28), channel_id=1, source_target_pairs={{0,7},{1,0},{2,15},{3,8},{4,23},{5,16},{6,31},{7,24},{8,1},{9,2},{... | collective-permute-start | bytes 393224 | tf_op jit(solution)/shard_map/ppermute | solution.py:482
  (36 other events, 381.9 us)

commit v4 on v3

--- a/solution.py
+++ b/solution.py
@@ -208,7 +208,7 @@
             back.wait()
 
 
-def unit(total, shape, panel_sets, coefs, chunks, meta, kw, emit=0):
+def unit(total, shape, panel_sets, coefs, chunks, meta, kw, emit=0, kept=False):
     n_l, _, rows, nb = panel_sets[0].shape
     half = nb // 2
     steps = max(1, half // (2 * LANES))
@@ -233,7 +233,7 @@
     if fresh:
         total = coefs[0]
     in_specs += [pl.BlockSpec(c.shape, lambda g, sc: (0, 0, 0)) for c in coefs]
-    in_specs += [pl.BlockSpec(memory_space=pltpu.HBM)]
+    in_specs += [pl.BlockSpec(memory_space=pl.ANY)]
     args += [*coefs, total]
     flops = 2 * 3 * n * n_l * rows * wide * (2 * nb + SPAN * LANES) * len(chunks)
     n_chan = shape[0] - 2 * R
@@ -247,7 +247,7 @@
             num_scalar_prefetch=1,
             grid=(steps,),
             in_specs=in_specs,
-            out_specs=[pl.BlockSpec(memory_space=pltpu.HBM) for _ in outs],
+            out_specs=[pl.BlockSpec(memory_space=pl.ANY) for _ in outs],
             scratch_shapes=[
                 pltpu.VMEM((len(chunks), n * n_l * rows, wide), F32),
                 pltpu.VMEM(shape, F32),
@@ -258,12 +258,13 @@
         cost_estimate=pl.CostEstimate(
             flops=flops, transcendentals=0, bytes_accessed=4 * n * n_l * 2 * rows * nb
         ),
-        compiler_params=pltpu.CompilerParams(vmem_limit_bytes=40 << 20),
+        compiler_params=pltpu.CompilerParams(vmem_limit_bytes=30 << 20),
         name="unit",
     )(
         meta,
         *args[: 2 * n],
-        *[pltpu.with_memory_space_constraint(a, pltpu.HBM) for a in args[2 * n :]],
+        *[pltpu.with_memory_space_constraint(a, pltpu.HBM) if kept else a for a in args[2 * n : -n - 1]],
+        *args[-n - 1 :],
     )
     return result if emit else result[0]
 
@@ -297,7 +298,7 @@
 
 
 def finish_kernel(sc_ref, base_ref, *refs, kw, n_mult):
-    pieces, (out_ref, held, pick_ref) = refs[:-3], refs[-3:]
+    pieces, out_ref, held = refs[:-2], refs[-2], refs[-1]
     n_ch, per, sub, lanes = base_ref.shape
     n = len(pieces)
     me = sc_ref[1]
@@ -314,15 +315,11 @@
     vh, vl = split(v)
     both = jnp.concatenate([vh, vl], axis=0)
 
-    @pl.when(pl.program_id(0) == 0)
-    def _():
-        row = lax.broadcasted_iota(jnp.int32, (groups * lanes, lanes), 0)
-        col = lax.broadcasted_iota(jnp.int32, (groups * lanes, lanes), 1)
-        start = (col // kw) * lanes + col % kw
-        for i in range(n_ch):
-            pick_ref[:, i * lanes : (i + 1) * lanes] = (row == start + i * kw).astype(BF16)
-
-    out = jnp.dot(both, pick_ref[...], preferred_element_type=F32)
+    row = lax.broadcasted_iota(jnp.int32, (groups * lanes, lanes), 0)
+    col = lax.broadcasted_iota(jnp.int32, (groups * lanes, lanes), 1)
+    start = (col // kw) * lanes + col % kw
+    picks = jnp.concatenate([(row == start + i * kw).astype(BF16) for i in range(n_ch)], axis=1)
+    out = jnp.dot(both, picks, preferred_element_type=F32)
     out = out[: per * sub] + out[per * sub :]
     for h in range(per):
         for i in range(n_ch):
@@ -343,16 +340,13 @@
             in_specs=[pl.BlockSpec((n_ch, per, sub, lanes), lambda g, sc: (0, 0, g, 0))]
             + [pl.BlockSpec((2, sub, lanes), lambda g, sc: (0, g, 0)) for _ in pieces],
             out_specs=pl.BlockSpec((n_ch, per, sub, lanes), lambda g, sc: (0, 0, g, 0)),
-            scratch_shapes=[
-                pltpu.VMEM((len(pieces), 2, sub, lanes), F32),
-                pltpu.VMEM((2 * n_mult * lanes, n_ch * lanes), BF16),
-            ],
+            scratch_shapes=[pltpu.VMEM((len(pieces), 2, sub, lanes), F32)],
         ),
         name="finish",
     )(
         meta,
         base.reshape(n_ch, per, rows, lanes),
-        *[pltpu.with_memory_space_constraint(p.reshape(2, rows, lanes), pltpu.HBM) for p in pieces],
+        *[p.reshape(2, rows, lanes) for p in pieces],
     )
     return out.reshape(n_ch, out_rows, lanes)
 
@@ -439,8 +433,8 @@
 
     shape = (n_chan + 2 * R, 2 * rows, LANES)
 
-    def add(total, sets, coefs, chunks, emit=0):
-        return unit(total, shape, sets, coefs, chunks, meta, kw, emit)
+    def add(total, sets, coefs, chunks, emit=0, kept=False):
+        return unit(total, shape, sets, coefs, chunks, meta, kw, emit, kept)
 
     full_steps, switch = steps_of(n_chan)
     total = None

time: 188 us -> 180 us (0.957)
  the two profiles are of different devices: /device:TPU:6 before, /device:TPU:2 now
where the time goes in v4:
time: 180 us
  Pallas kernels  74.5 us (41%)
  waiting for transfers between devices  64.7 us (36%)
  starting transfers between devices  37.5 us (21%)
  local copies, waits for them, and re-layouts  2.57 us (1%)
    pallas_call x5, Pallas kernels, unit(): pl.pallas_call(functools.partial(unit_kernel, n_p=n, kw=kw, steps=steps,...  58.5 us
    ppermute x14, waiting for transfers between devices, ring_shift(): lax.ppermute(value, axis, [(order[i], order[(i + by) % n]) for i in range...  39.6 us
    ppermute x8, waiting for transfers between devices, body(): pieces.append(lax.ppermute(sends[s], ('mult', 'chan'), pairs))  17.7 us
    ppermute x14, starting transfers between devices, ring_shift(): lax.ppermute(value, axis, [(order[i], order[(i + by) % n]) for i in range...  13.6 us
    ppermute x7, starting transfers between devices, body(): lax.ppermute(sent, 'chan', [(i, (i + by) % n_chan) for i in range(n_chan)])  12.4 us
    ppermute x8, starting transfers between devices, body(): pieces.append(lax.ppermute(sends[s], ('mult', 'chan'), pairs))  8.97 us
    pallas_call x2, Pallas kernels, pack(): pl.pallas_call(functools.partial(pack_kernel, kw=kw), out_shape=jax.Shape...  7.29 us
    ppermute x6, waiting for transfers between devices, flip(): lax.ppermute(value, axis, [(i, i ^ bit) for i in range(lax.axis_size(axis...  5.75 us
  transfers between devices with their start and end apart: 35, of which 12 were waited for; matrix products, arithmetic and copies ran while one was open for 0% of the time, Pallas kernels for 32%

profile of v4, /device:TPU:2, one launch (start us, length us, event | category | flops | bytes accessed | tf_op | source)
XLA Modules:
  0.0 179.9 jit_solution(18286728239117382335)
XLA Ops:
  0.1 3.7 %pack.3.refs_5_ = f32[512,256]{1,0:T(8,128)} custom-call(f32[8,1024,128]{2,1,0:T(8,128)} %col_ref.5), custom_call_target="tpu_custom_call" | custom-call | tf_op jit(solution)/shard_map/pack/pallas_call | solution.py:69
  4.3 1.6 collective-permute-start.6
  5.9 1.6 collective-permute-start.7
  7.5 2.5 %collective-permute-start.8 = (f32[8,128]{1,0:T(8,128)S(1)}, f32[8,128]{1,0:T(8,128)S(1)}, u32[]{:S(2)}, u32[]{:S(2)}) collective-permute-start(f32[8,128]{1,0:T(8,128)S(1)} %select_reduce_fusion), channel_id=1, source_target_pairs={{0,3},{1,4},{2,5},{3,6},{4,7},{5,0},{6,1},{7,2},{8,11},{9,12},{10,... | collective-permute-start | bytes 12296 | tf_op jit(solution)/shard_map/ppermute | solution.py:421
  11.2 2.6 %collective-permute-start.10 = (f32[8,128]{1,0:T(8,128)S(1)}, f32[8,128]{1,0:T(8,128)S(1)}, u32[]{:S(2)}, u32[]{:S(2)}) collective-permute-start(f32[8,128]{1,0:T(8,128)S(1)} %select_reduce_fusion), channel_id=1, source_target_pairs={{0,5},{1,6},{2,7},{3,0},{4,1},{5,2},{6,3},{7,4},{8,13},{9,14},{10,... | collective-permute-start | bytes 12296 | tf_op jit(solution)/shard_map/ppermute | solution.py:421
  15.9 1.4 collective-permute-start.12
  17.9 1.5 collective-permute-done.12
  19.5 1.6 collective-permute-start.5
  21.0 3.6 %pack.2.refs_4_ = f32[512,256]{1,0:T(8,128)} custom-call(f32[8,1024,128]{2,1,0:T(8,128)} %col_ref.5), custom_call_target="tpu_custom_call" | custom-call | tf_op jit(solution)/shard_map/pack/pallas_call | solution.py:69
  25.1 7.2 %collective-permute-done.3.refs_7_ = f32[512,256]{1,0:T(8,128)S(1)} collective-permute-done((f32[512,256]{1,0:T(8,128)}, f32[512,256]{1,0:T(8,128)S(1)}, u32[]{:S(2)}, u32[]{:S(2)}) %collective-permute-start.3) | collective-permute-done | bytes 524320 | tf_op jit(solution)/shard_map/ppermute | solution.py:25
  34.6 7.6 %collective-permute-done.2.refs_6_ = f32[512,256]{1,0:T(8,128)} collective-permute-done((f32[512,256]{1,0:T(8,128)}, f32[512,256]{1,0:T(8,128)}, u32[]{:S(2)}, u32[]{:S(2)}) %collective-permute-start.2) | collective-permute-done | bytes 524320 | tf_op jit(solution)/shard_map/ppermute | solution.py:25
  42.2 3.1 %collective-permute-done.4.refs_8_ = f32[512,256]{1,0:T(8,128)} collective-permute-done((f32[512,256]{1,0:T(8,128)}, f32[512,256]{1,0:T(8,128)}, u32[]{:S(2)}, u32[]{:S(2)}) %collective-permute-start.4) | collective-permute-done | bytes 524320 | tf_op jit(solution)/shard_map/ppermute | solution.py:25
  46.4 11.0 %unit.5.refs_10_ = f32[12,256,128]{2,1,0:T(8,128)S(1)} custom-call(s32[11]{0:T(128)S(1)} %pad_add_fusion.sc_ref, f32[2,2,128,1024]{3,2,1,0:T(8,128)S(1)} %copy-done, f32[2,2,128,1024]{3,2,1,0:T(8,128)S(1)} %copy-done, f32[2,2,128,1024]{3,2,1,0:T(8,128)} %collective-permute-done.refs_2_.refs_3_, f32[2,2,128,1024]{3,2,1,0:T(8,128)} %collective-permute-done.refs_2_.refs_3_, ...), custom_call_target="tpu_custom_call" | custom-call | flops 6341787648 | bytes 4194304 | tf_op jit(solution)/shard_map/unit/pallas_call | solution.py:241
  57.4 5.7 %collective-permute-done.1.refs_0_.refs_1_.refs_4_.refs_5_ = f32[2,2,128,1024]{3,2,1,0:T(8,128)} collective-permute-done((f32[2,2,128,1024]{3,2,1,0:T(8,128)S(1)}, f32[2,2,128,1024]{3,2,1,0:T(8,128)}, u32[]{:S(2)}, u32[]{:S(2)}) %collective-permute-start.1) | collective-permute-done | bytes 2097184 | tf_op jit(solution)/shard_map/ppermute | solution.py:29
  67.2 11.0 %collective-permute-done.18.refs_7_.refs_13_ = f32[512,256]{1,0:T(8,128)S(1)} collective-permute-done((f32[512,256]{1,0:T(8,128)}, f32[512,256]{1,0:T(8,128)S(1)}, u32[]{:S(2)}, u32[]{:S(2)}) %collective-permute-start.18) | collective-permute-done | bytes 524320 | tf_op jit(solution)/shard_map/ppermute | solution.py:25
  80.2 9.8 %collective-permute-done.23.refs_5_.refs_11_ = f32[512,256]{1,0:T(8,128)S(1)} collective-permute-done((f32[512,256]{1,0:T(8,128)S(1)}, f32[512,256]{1,0:T(8,128)S(1)}, u32[]{:S(2)}, u32[]{:S(2)}) %collective-permute-start.23) | collective-permute-done | bytes 524320 | tf_op jit(solution)/shard_map/ppermute | solution.py:25
  90.5 1.6 collective-permute-start.22
  92.1 8.0 %unit.6.refs_16_ = f32[12,256,128]{2,1,0:T(8,128)S(1)} custom-call(s32[11]{0:T(128)S(1)} %pad_add_fusion.sc_ref, f32[2,2,128,1024]{3,2,1,0:T(8,128)S(1)} %copy-done, f32[2,2,128,1024]{3,2,1,0:T(8,128)S(1)} %copy-done, f32[2,2,128,1024]{3,2,1,0:T(8,128)} %collective-permute-done.refs_2_.refs_3_, ...), custom_call_target="tpu_custom_call", output_to_operand_aliasing={{}: (11, {})} | custom-call | flops 4227858432 | bytes 4194304 | tf_op jit(solution)/shard_map/unit/pallas_call | solution.py:241
  100.1 1.5 collective-permute-start.24
  102.4 1.8 %collective-permute-start.17 = (f32[512,256]{1,0:T(8,128)S(1)}, f32[512,256]{1,0:T(8,128)S(1)}, u32[]{:S(2)}, u32[]{:S(2)}) collective-permute-start(f32[512,256]{1,0:T(8,128)S(1)} %collective-permute-done.16.refs_8_), channel_id=1, source_target_pairs={{0,2},{2,4},{4,6},{6,7},{7,5},{5,3},{3,1},{1,0},{8,10},{10,12},{12... | collective-permute-start | bytes 1572872 | tf_op jit(solution)/shard_map/ppermute | solution.py:25
  104.2 16.5 %unit.7.refs_16_ = f32[12,256,128]{2,1,0:T(8,128)S(1)} custom-call(s32[11]{0:T(128)S(1)} %pad_add_fusion.sc_ref, f32[2,2,128,1024]{3,2,1,0:T(8,128)} %collective-permute-done.1.refs_0_.refs_1_.refs_4_.refs_5_, f32[2,2,128,1024]{3,2,1,0:T(8,128)} %collective-permute-done.1.refs_0_.refs_1_.refs_4_.refs_5_, ...), custom_call_target="tpu_custom_call", output_to_operand_aliasing={{}: (17, {})} | custom-call | flops 10569646080 | bytes 4194304 | tf_op jit(solution)/shard_map/unit/pallas_call | solution.py:241
  120.8 13.1 %unit.8.refs_14_ = f32[12,256,128]{2,1,0:T(8,128)S(1)} custom-call(s32[11]{0:T(128)S(1)} %pad_add_fusion.sc_ref, f32[2,2,128,1024]{3,2,1,0:T(8,128)S(1)} %copy-done, f32[2,2,128,1024]{3,2,1,0:T(8,128)S(1)} %copy-done, f32[2,2,128,1024]{3,2,1,0:T(8,128)} %collective-permute-done.refs_2_.refs_3_, ...), custom_call_target="tpu_custom_call", output_to_operand_aliasing={{}: (17, {})} | custom-call | flops 8455716864 | bytes 8388608 | tf_op jit(solution)/shard_map/unit/pallas_call | solution.py:241
  134.0 9.8 %unit.9 = (f32[256,128]{1,0:T(8,128)S(1)}, f32[256,128]{1,0:T(8,128)S(1)}, f32[256,128]{1,0:T(8,128)S(1)}, f32[256,128]{1,0:T(8,128)S(1)}, f32[256,128]{1,0:T(8,...) custom-call(s32[11]{0:T(128)S(1)} %pad_add_fusion.sc_ref, ...), custom_call_target="tpu_custom_call" | custom-call | flops 4227858432 | bytes 8388608 | tf_op jit(solution)/shard_map/unit/pallas_call | solution.py:241
  143.8 3.3 %collective-permute-start.27 = (f32[256,128]{1,0:T(8,128)S(1)}, f32[256,128]{1,0:T(8,128)S(1)}, u32[]{:S(2)}, u32[]{:S(2)}) collective-permute-start(f32[256,128]{1,0:T(8,128)S(1)} %get-tuple-element.21), channel_id=1, source_target_pairs={{0,0},{1,1},{2,8},{3,9},{4,16},{5,17},{6,24},{7,25},{8,2},{9,3},{1... | collective-permute-start | bytes 393224 | tf_op jit(solution)/shard_map/ppermute | solution.py:476
  147.1 2.1 %collective-permute-start.28 = (f32[256,128]{1,0:T(8,128)S(1)}, f32[256,128]{1,0:T(8,128)S(1)}, u32[]{:S(2)}, u32[]{:S(2)}) collective-permute-start(f32[256,128]{1,0:T(8,128)S(1)} %get-tuple-element.22), channel_id=1, source_target_pairs={{0,1},{1,2},{2,9},{3,10},{4,17},{5,18},{6,25},{7,26},{8,3},{9,4},{... | collective-permute-start | bytes 393224 | tf_op jit(solution)/shard_map/ppermute | solution.py:476
  149.3 2.1 %collective-permute-start.29 = (f32[256,128]{1,0:T(8,128)S(1)}, f32[256,128]{1,0:T(8,128)S(1)}, u32[]{:S(2)}, u32[]{:S(2)}) collective-permute-start(f32[256,128]{1,0:T(8,128)S(1)} %get-tuple-element.23), channel_id=1, source_target_pairs={{0,2},{1,3},{2,10},{3,11},{4,18},{5,19},{6,26},{7,27},{8,4},{9,5},... | collective-permute-start | bytes 393224 | tf_op jit(solution)/shard_map/ppermute | solution.py:476
  152.7 4.2 %collective-permute-done.27 = f32[256,128]{1,0:T(8,128)S(1)} collective-permute-done((f32[256,128]{1,0:T(8,128)S(1)}, f32[256,128]{1,0:T(8,128)S(1)}, u32[]{:S(2)}, u32[]{:S(2)}) %collective-permute-start.27) | collective-permute-done | bytes 131104 | tf_op jit(solution)/shard_map/ppermute | solution.py:476
  157.0 9.3 %collective-permute-done.28 = f32[256,128]{1,0:T(8,128)S(1)} collective-permute-done((f32[256,128]{1,0:T(8,128)S(1)}, f32[256,128]{1,0:T(8,128)S(1)}, u32[]{:S(2)}, u32[]{:S(2)}) %collective-permute-start.28) | collective-permute-done | bytes 131104 | tf_op jit(solution)/shard_map/ppermute | solution.py:476
  166.3 4.4 %shifted.1 = f32[8,256,128]{2,1,0:T(8,128)} custom-call(s32[11]{0:T(128)} %copy-done.3, f32[8]{0:T(128)} %energy_ref.1, f32[2]{0:T(128)} %contour_ref.1, f32[8,1024,128]{2,1,0:T(8,128)} %col_ref.5), custom_call_target="tpu_custom_call" | custom-call | tf_op jit(solution)/shard_map/shifted/pallas_call | solution.py:287
  170.7 1.7 collective-permute-done.33
  172.4 2.6 %collective-permute-done.34 = f32[256,128]{1,0:T(8,128)S(1)} collective-permute-done((f32[256,128]{1,0:T(8,128)S(1)}, f32[256,128]{1,0:T(8,128)S(1)}, u32[]{:S(2)}, u32[]{:S(2)}) %collective-permute-start.34) | collective-permute-done | bytes 131104 | tf_op jit(solution)/shard_map/ppermute | solution.py:476
  175.6 4.3 %finish.1 = f32[8,2,128,128]{3,2,1,0:T(8,128)} custom-call(s32[11]{0:T(128)} %copy-done.3, f32[8,2,128,128]{3,2,1,0:T(8,128)} %bitcast.47, f32[2,128,128]{2,1,0:T(8,128)} %bitcast.48, f32[2,128,128]{2,1,0:T(8,128)} %bitcast.49, f32[2,128,128]{2,1,0:T(8,128)} %bitcast.50, f32[2,128,128]{2,1,0:T(8,128)} %bitcast.51, f32[2,128,128]{2,1,0:T(8,128)} %bitcast.52, ...), custom_call_target="tpu_custom_call" | custom-call | tf_op jit(solution)/shard_map/finish/pallas_call | solution.py:334
  (105 shorter events, 17.7 us)
Async XLA Ops:
  4.3 9.6 %collective-permute-start.6 = (f32[8,128]{1,0:T(8,128)S(1)}, f32[8,128]{1,0:T(8,128)S(1)}, u32[]{:S(2)}, u32[]{:S(2)}) collective-permute-start(f32[8,128]{1,0:T(8,128)S(1)} %select_reduce_fusion), channel_id=1, source_target_pairs={{0,1},{1,2},{2,3},{3,4},{4,5},{5,6},{6,7},{7,0},{8,9},{9,10},{10,1... | collective-permute-start | bytes 12296 | tf_op jit(solution)/shard_map/ppermute | solution.py:421
  5.9 8.1 %collective-permute-start.7 = (f32[8,128]{1,0:T(8,128)S(1)}, f32[8,128]{1,0:T(8,128)S(1)}, u32[]{:S(2)}, u32[]{:S(2)}) collective-permute-start(f32[8,128]{1,0:T(8,128)S(1)} %select_reduce_fusion), channel_id=1, source_target_pairs={{0,2},{1,3},{2,4},{3,5},{4,6},{5,7},{6,0},{7,1},{8,10},{9,11},{10,... | collective-permute-start | bytes 12296 | tf_op jit(solution)/shard_map/ppermute | solution.py:421
  7.5 7.9 %collective-permute-start.8 = (f32[8,128]{1,0:T(8,128)S(1)}, f32[8,128]{1,0:T(8,128)S(1)}, u32[]{:S(2)}, u32[]{:S(2)}) collective-permute-start(f32[8,128]{1,0:T(8,128)S(1)} %select_reduce_fusion), channel_id=1, source_target_pairs={{0,3},{1,4},{2,5},{3,6},{4,7},{5,0},{6,1},{7,2},{8,11},{9,12},{10,... | collective-permute-start | bytes 12296 | tf_op jit(solution)/shard_map/ppermute | solution.py:421
  10.0 5.9 %collective-permute-start.9 = (f32[8,128]{1,0:T(8,128)S(1)}, f32[8,128]{1,0:T(8,128)S(1)}, u32[]{:S(2)}, u32[]{:S(2)}) collective-permute-start(f32[8,128]{1,0:T(8,128)S(1)} %select_reduce_fusion), channel_id=1, source_target_pairs={{0,4},{1,5},{2,6},{3,7},{4,0},{5,1},{6,2},{7,3},{8,12},{9,13},{10,... | collective-permute-start | bytes 12296 | tf_op jit(solution)/shard_map/ppermute | solution.py:421
  11.2 6.0 %collective-permute-start.10 = (f32[8,128]{1,0:T(8,128)S(1)}, f32[8,128]{1,0:T(8,128)S(1)}, u32[]{:S(2)}, u32[]{:S(2)}) collective-permute-start(f32[8,128]{1,0:T(8,128)S(1)} %select_reduce_fusion), channel_id=1, source_target_pairs={{0,5},{1,6},{2,7},{3,0},{4,1},{5,2},{6,3},{7,4},{8,13},{9,14},{10,... | collective-permute-start | bytes 12296 | tf_op jit(solution)/shard_map/ppermute | solution.py:421
  13.9 31.5 %collective-permute-start = (f32[2,2,128,1024]{3,2,1,0:T(8,128)S(1)}, f32[2,2,128,1024]{3,2,1,0:T(8,128)}, u32[]{:S(2)}, u32[]{:S(2)}) collective-permute-start(f32[2,2,128,1024]{3,2,1,0:T(8,128)S(1)} %copy-done), channel_id=1, source_target_pairs={{0,8},{8,0},{16,24},{24,16},{1,9},{9,1},{17,25},{25,17},{2,10},{10... | collective-permute-start | bytes 6291464 | tf_op jit(solution)/shard_map/ppermute | solution.py:29
  15.4 47.8 %collective-permute-start.1 = (f32[2,2,128,1024]{3,2,1,0:T(8,128)S(1)}, f32[2,2,128,1024]{3,2,1,0:T(8,128)}, u32[]{:S(2)}, u32[]{:S(2)}) collective-permute-start(f32[2,2,128,1024]{3,2,1,0:T(8,128)S(1)} %copy-done), channel_id=1, source_target_pairs={{0,16},{8,24},{16,0},{24,8},{1,17},{9,25},{17,1},{25,9},{2,18},{10... | collective-permute-start | bytes 6291464 | tf_op jit(solution)/shard_map/ppermute | solution.py:29
  17.3 15.0 %collective-permute-start.3 = (f32[512,256]{1,0:T(8,128)}, f32[512,256]{1,0:T(8,128)S(1)}, u32[]{:S(2)}, u32[]{:S(2)}) collective-permute-start(f32[512,256]{1,0:T(8,128)} %pack.3.refs_5_), channel_id=1, source_target_pairs={{0,2},{2,4},{4,6},{6,7},{7,5},{5,3},{3,1},{1,0},{8,10},{10,12},{12... | collective-permute-start | bytes 1572872 | tf_op jit(solution)/shard_map/ppermute | solution.py:25
  19.5 15.2 %collective-permute-start.5 = (f32[512,256]{1,0:T(8,128)}, f32[512,256]{1,0:T(8,128)}, u32[]{:S(2)}, u32[]{:S(2)}) collective-permute-start(f32[512,256]{1,0:T(8,128)} %pack.3.refs_5_), channel_id=1, source_target_pairs={{0,1},{2,0},{4,2},{6,4},{7,6},{5,7},{3,5},{1,3},{8,9},{10,8},{12,1... | collective-permute-start | bytes 1572872 | tf_op jit(solution)/shard_map/ppermute | solution.py:25
  24.6 17.6 %collective-permute-start.2 = (f32[512,256]{1,0:T(8,128)}, f32[512,256]{1,0:T(8,128)}, u32[]{:S(2)}, u32[]{:S(2)}) collective-permute-start(f32[512,256]{1,0:T(8,128)} %pack.2.refs_4_), channel_id=1, source_target_pairs={{0,2},{2,4},{4,6},{6,7},{7,5},{5,3},{3,1},{1,0},{8,10},{10,12},{12... | collective-permute-start | bytes 1572872 | tf_op jit(solution)/shard_map/ppermute | solution.py:25
  32.3 13.1 %collective-permute-start.4 = (f32[512,256]{1,0:T(8,128)}, f32[512,256]{1,0:T(8,128)}, u32[]{:S(2)}, u32[]{:S(2)}) collective-permute-start(f32[512,256]{1,0:T(8,128)} %pack.2.refs_4_), channel_id=1, source_target_pairs={{0,1},{2,0},{4,2},{6,4},{7,6},{5,7},{3,5},{1,3},{8,9},{10,8},{12,1... | collective-permute-start | bytes 1572872 | tf_op jit(solution)/shard_map/ppermute | solution.py:25
  63.2 41.1 %collective-permute-start.14 = (f32[2,2,128,1024]{3,2,1,0:T(8,128)}, f32[2,2,128,1024]{3,2,1,0:T(8,128)S(1)}, u32[]{:S(2)}, u32[]{:S(2)}) collective-permute-start(f32[2,2,128,1024]{3,2,1,0:T(8,128)} %collective-permute-done.1.refs_0_.refs_1_.refs_4_.refs_5_), channel_id=1, source_target_pairs={{0,8},{8,0},{16,24},{24,16},{1,9},{9,1},{17,25},{25,17},{2,10},{10... | collective-permute-start | bytes 6291464 | tf_op jit(solution)/shard_map/ppermute | solution.py:29
  63.2 15.0 %collective-permute-start.18 = (f32[512,256]{1,0:T(8,128)}, f32[512,256]{1,0:T(8,128)S(1)}, u32[]{:S(2)}, u32[]{:S(2)}) collective-permute-start(f32[512,256]{1,0:T(8,128)} %collective-permute-done.5.refs_9_), channel_id=1, source_target_pairs={{0,1},{2,0},{4,2},{6,4},{7,6},{5,7},{3,5},{1,3},{8,9},{10,8},{12,1... | collective-permute-start | bytes 1572872 | tf_op jit(solution)/shard_map/ppermute | solution.py:25
  63.8 15.0 %collective-permute-start.15 = (f32[512,256]{1,0:T(8,128)}, f32[512,256]{1,0:T(8,128)S(1)}, u32[]{:S(2)}, u32[]{:S(2)}) collective-permute-start(f32[512,256]{1,0:T(8,128)} %collective-permute-done.2.refs_6_), channel_id=1, source_target_pairs={{0,2},{2,4},{4,6},{6,7},{7,5},{5,3},{3,1},{1,0},{8,10},{10,12},{12... | collective-permute-start | bytes 1572872 | tf_op jit(solution)/shard_map/ppermute | solution.py:25
  65.2 24.8 %collective-permute-start.23 = (f32[512,256]{1,0:T(8,128)S(1)}, f32[512,256]{1,0:T(8,128)S(1)}, u32[]{:S(2)}, u32[]{:S(2)}) collective-permute-start(f32[512,256]{1,0:T(8,128)S(1)} %collective-permute-done.3.refs_7_), channel_id=1, source_target_pairs={{0,2},{2,4},{4,6},{6,7},{7,5},{5,3},{3,1},{1,0},{8,10},{10,12},{12... | collective-permute-start | bytes 1572872 | tf_op jit(solution)/shard_map/ppermute | solution.py:25
  65.9 24.6 %collective-permute-start.25 = (f32[512,256]{1,0:T(8,128)}, f32[512,256]{1,0:T(8,128)S(1)}, u32[]{:S(2)}, u32[]{:S(2)}) collective-permute-start(f32[512,256]{1,0:T(8,128)} %collective-permute-done.4.refs_8_), channel_id=1, source_target_pairs={{0,1},{2,0},{4,2},{6,4},{7,6},{5,7},{3,5},{1,3},{8,9},{10,8},{12,1... | collective-permute-start | bytes 1572872 | tf_op jit(solution)/shard_map/ppermute | solution.py:25
  78.2 24.0 %collective-permute-start.19 = (f32[512,256]{1,0:T(8,128)S(1)}, f32[512,256]{1,0:T(8,128)S(1)}, u32[]{:S(2)}, u32[]{:S(2)}) collective-permute-start(f32[512,256]{1,0:T(8,128)S(1)} %collective-permute-done.18.refs_7_.refs_13_), channel_id=1, source_target_pairs={{0,1},{2,0},{4,2},{6,4},{7,6},{5,7},{3,5},{1,3},{8,9},{10,8},{12,1... | collective-permute-start | bytes 1572872 | tf_op jit(solution)/shard_map/ppermute | solution.py:25
  78.8 23.6 %collective-permute-start.16 = (f32[512,256]{1,0:T(8,128)S(1)}, f32[512,256]{1,0:T(8,128)S(1)}, u32[]{:S(2)}, u32[]{:S(2)}) collective-permute-start(f32[512,256]{1,0:T(8,128)S(1)} %collective-permute-done.15.refs_4_.refs_10_), channel_id=1, source_target_pairs={{0,2},{2,4},{4,6},{6,7},{7,5},{5,3},{3,1},{1,0},{8,10},{10,12},{12... | collective-permute-start | bytes 1572872 | tf_op jit(solution)/shard_map/ppermute | solution.py:25
  90.0 10.1 %collective-permute-start.21 = (f32[8,8,128]{2,1,0:T(8,128)S(1)}, f32[8,8,128]{2,1,0:T(8,128)S(1)}, u32[]{:S(2)}, u32[]{:S(2)}) collective-permute-start(f32[8,8,128]{2,1,0:T(8,128)S(1)} %constant_dynamic-update-slice_fusion.refs_10_.refs_12_.refs_8_), channel_id=1, source_target_pairs={{0,16},{8,24},{16,0},{24,8},{1,17},{9,25},{17,1},{25,9},{2,18},{10... | collective-permute-start | bytes 98312 | tf_op jit(solution)/shard_map/ppermute | solution.py:29
  90.5 11.1 %collective-permute-start.22 = (f32[8,8,128]{2,1,0:T(8,128)S(1)}, f32[8,8,128]{2,1,0:T(8,128)S(1)}, u32[]{:S(2)}, u32[]{:S(2)}) collective-permute-start(f32[8,8,128]{2,1,0:T(8,128)S(1)} %collective-permute-done.13.refs_11_.refs_9_.refs_13_), channel_id=1, source_target_pairs={{0,16},{8,24},{16,0},{24,8},{1,17},{9,25},{17,1},{25,9},{2,18},{10... | collective-permute-start | bytes 98312 | tf_op jit(solution)/shard_map/ppermute | solution.py:29
  100.1 20.7 %collective-permute-start.24 = (f32[512,256]{1,0:T(8,128)S(1)}, f32[512,256]{1,0:T(8,128)S(1)}, u32[]{:S(2)}, u32[]{:S(2)}) collective-permute-start(f32[512,256]{1,0:T(8,128)S(1)} %collective-permute-done.23.refs_5_.refs_11_), channel_id=1, source_target_pairs={{0,2},{2,4},{4,6},{6,7},{7,5},{5,3},{3,1},{1,0},{8,10},{10,12},{12... | collective-permute-start | bytes 1572872 | tf_op jit(solution)/shard_map/ppermute | solution.py:25
  101.6 19.2 %collective-permute-start.26 = (f32[512,256]{1,0:T(8,128)S(1)}, f32[512,256]{1,0:T(8,128)S(1)}, u32[]{:S(2)}, u32[]{:S(2)}) collective-permute-start(f32[512,256]{1,0:T(8,128)S(1)} %collective-permute-done.25.refs_6_.refs_12_), channel_id=1, source_target_pairs={{0,1},{2,0},{4,2},{6,4},{7,6},{5,7},{3,5},{1,3},{8,9},{10,8},{12,1... | collective-permute-start | bytes 1572872 | tf_op jit(solution)/shard_map/ppermute | solution.py:25
  102.2 31.8 %collective-permute-start.20 = (f32[512,256]{1,0:T(8,128)S(1)}, f32[512,256]{1,0:T(8,128)S(1)}, u32[]{:S(2)}, u32[]{:S(2)}) collective-permute-start(f32[512,256]{1,0:T(8,128)S(1)} %collective-permute-done.19.refs_11_), channel_id=1, source_target_pairs={{0,1},{2,0},{4,2},{6,4},{7,6},{5,7},{3,5},{1,3},{8,9},{10,8},{12,1... | collective-permute-start | bytes 1572872 | tf_op jit(solution)/shard_map/ppermute | solution.py:25
  102.4 31.6 %collective-permute-start.17 = (f32[512,256]{1,0:T(8,128)S(1)}, f32[512,256]{1,0:T(8,128)S(1)}, u32[]{:S(2)}, u32[]{:S(2)}) collective-permute-start(f32[512,256]{1,0:T(8,128)S(1)} %collective-permute-done.16.refs_8_), channel_id=1, source_target_pairs={{0,2},{2,4},{4,6},{6,7},{7,5},{5,3},{3,1},{1,0},{8,10},{10,12},{12... | collective-permute-start | bytes 1572872 | tf_op jit(solution)/shard_map/ppermute | solution.py:25
  143.8 13.2 %collective-permute-start.27 = (f32[256,128]{1,0:T(8,128)S(1)}, f32[256,128]{1,0:T(8,128)S(1)}, u32[]{:S(2)}, u32[]{:S(2)}) collective-permute-start(f32[256,128]{1,0:T(8,128)S(1)} %get-tuple-element.21), channel_id=1, source_target_pairs={{0,0},{1,1},{2,8},{3,9},{4,16},{5,17},{6,24},{7,25},{8,2},{9,3},{1... | collective-permute-start | bytes 393224 | tf_op jit(solution)/shard_map/ppermute | solution.py:476
  147.1 19.1 %collective-permute-start.28 = (f32[256,128]{1,0:T(8,128)S(1)}, f32[256,128]{1,0:T(8,128)S(1)}, u32[]{:S(2)}, u32[]{:S(2)}) collective-permute-start(f32[256,128]{1,0:T(8,128)S(1)} %get-tuple-element.22), channel_id=1, source_target_pairs={{0,1},{1,2},{2,9},{3,10},{4,17},{5,18},{6,25},{7,26},{8,3},{9,4},{... | collective-permute-start | bytes 393224 | tf_op jit(solution)/shard_map/ppermute | solution.py:476
  149.3 17.0 %collective-permute-start.29 = (f32[256,128]{1,0:T(8,128)S(1)}, f32[256,128]{1,0:T(8,128)S(1)}, u32[]{:S(2)}, u32[]{:S(2)}) collective-permute-start(f32[256,128]{1,0:T(8,128)S(1)} %get-tuple-element.23), channel_id=1, source_target_pairs={{0,2},{1,3},{2,10},{3,11},{4,18},{5,19},{6,26},{7,27},{8,4},{9,5},... | collective-permute-start | bytes 393224 | tf_op jit(solution)/shard_map/ppermute | solution.py:476
  151.4 19.3 %collective-permute-start.30 = (f32[256,128]{1,0:T(8,128)S(1)}, f32[256,128]{1,0:T(8,128)S(1)}, u32[]{:S(2)}, u32[]{:S(2)}) collective-permute-start(f32[256,128]{1,0:T(8,128)S(1)} %get-tuple-element.24), channel_id=1, source_target_pairs={{0,3},{1,4},{2,11},{3,12},{4,19},{5,20},{6,27},{7,28},{8,5},{9,6},... | collective-permute-start | bytes 393224 | tf_op jit(solution)/shard_map/ppermute | solution.py:476
  152.7 18.0 %collective-permute-start.31 = (f32[256,128]{1,0:T(8,128)S(1)}, f32[256,128]{1,0:T(8,128)S(1)}, u32[]{:S(2)}, u32[]{:S(2)}) collective-permute-start(f32[256,128]{1,0:T(8,128)S(1)} %get-tuple-element.25), channel_id=1, source_target_pairs={{0,4},{1,5},{2,12},{3,13},{4,20},{5,21},{6,28},{7,29},{8,6},{9,7},... | collective-permute-start | bytes 393224 | tf_op jit(solution)/shard_map/ppermute | solution.py:476
  157.0 13.8 %collective-permute-start.32 = (f32[256,128]{1,0:T(8,128)S(1)}, f32[256,128]{1,0:T(8,128)S(1)}, u32[]{:S(2)}, u32[]{:S(2)}) collective-permute-start(f32[256,128]{1,0:T(8,128)S(1)} %get-tuple-element.26), channel_id=1, source_target_pairs={{0,5},{1,6},{2,13},{3,14},{4,21},{5,22},{6,29},{7,30},{8,7},{9,0},... | collective-permute-start | bytes 393224 | tf_op jit(solution)/shard_map/ppermute | solution.py:476
  166.2 6.2 %collective-permute-start.33 = (f32[256,128]{1,0:T(8,128)S(1)}, f32[256,128]{1,0:T(8,128)S(1)}, u32[]{:S(2)}, u32[]{:S(2)}) collective-permute-start(f32[256,128]{1,0:T(8,128)S(1)} %get-tuple-element.27), channel_id=1, source_target_pairs={{0,6},{1,7},{2,14},{3,15},{4,22},{5,23},{6,30},{7,31},{8,0},{9,1},... | collective-permute-start | bytes 393224 | tf_op jit(solution)/shard_map/ppermute | solution.py:476
  166.2 8.7 %collective-permute-start.34 = (f32[256,128]{1,0:T(8,128)S(1)}, f32[256,128]{1,0:T(8,128)S(1)}, u32[]{:S(2)}, u32[]{:S(2)}) collective-permute-start(f32[256,128]{1,0:T(8,128)S(1)} %get-tuple-element.28), channel_id=1, source_target_pairs={{0,7},{1,0},{2,15},{3,8},{4,23},{5,16},{6,31},{7,24},{8,1},{9,2},{... | collective-permute-start | bytes 393224 | tf_op jit(solution)/shard_map/ppermute | solution.py:476
  (20 other events, 211.8 us)

commit v5 on v4

--- a/solution.py
+++ b/solution.py
@@ -76,14 +76,14 @@
     )(columns)
 
 
-def unit_kernel(sc_ref, *refs, n_p, kw, steps, places, fresh, emit):
+def unit_kernel(sc_ref, *refs, n_p, which, kw, steps, places, fresh, emit):
     n_x = len(places)
     p_refs, x_refs = refs[: 2 * n_p], refs[2 * n_p : 2 * (n_p + n_x)]
     a_refs = refs[2 * (n_p + n_x) : 3 * n_p + 2 * n_x]
     c_in, *c_outs, y_ref, w_ref, sem = refs[3 * n_p + 2 * n_x :]
     step = pl.program_id(0)
     n_l, _, rows, _ = p_refs[0].shape
-    n_chan, n_ch, _ = a_refs[0].shape
+    n_chan, _, n_ch, _ = a_refs[0].shape
     if fresh:
         fetch = None
     else:
@@ -166,11 +166,11 @@
             s = sc_ref[places[0] + t]
             me = sc_ref[1]
             coef = []
-            for a_ref in a_refs:
+            for a_ref, w in zip(a_refs, which):
                 v = None
                 for d in range(SPAN):
                     at = s + d - R
-                    own = a_ref[lax.rem(me - at + 2 * n_chan, n_chan)]
+                    own = a_ref[lax.rem(me - at + 2 * n_chan, n_chan), w]
                     own = jnp.where((at >= 0) & (at < n_chan), own, 0.0)
                     v = own if v is None else jnp.where(lax.rem(grp, LANES // n_l // n_ch) == d, own, v)
                 coef += [pltpu.roll(v, LANES - l * (LANES // n_l), 1) if l else v for l in range(n_l)]
@@ -231,16 +231,16 @@
         args += [top, bottom]
     fresh = total is None
     if fresh:
-        total = coefs[0]
-    in_specs += [pl.BlockSpec(c.shape, lambda g, sc: (0, 0, 0)) for c in coefs]
+        total = coefs[0][0]
+    in_specs += [pl.BlockSpec(c.shape, lambda g, sc: (0, 0, 0, 0)) for c, _ in coefs]
     in_specs += [pl.BlockSpec(memory_space=pl.ANY)]
-    args += [*coefs, total]
+    args += [*[c for c, _ in coefs], total]
     flops = 2 * 3 * n * n_l * rows * wide * (2 * nb + SPAN * LANES) * len(chunks)
     n_chan = shape[0] - 2 * R
     outs = [jax.ShapeDtypeStruct(shape[1:], F32)] * n_chan if emit else [jax.ShapeDtypeStruct(shape, F32)]
     result = pl.pallas_call(
         functools.partial(
-            unit_kernel, n_p=n, kw=kw, steps=steps, places=tuple(c[2] for c in chunks), fresh=fresh, emit=emit
+            unit_kernel, n_p=n, which=tuple(w for _, w in coefs), kw=kw, steps=steps, places=tuple(c[2] for c in chunks), fresh=fresh, emit=emit
         ),
         out_shape=outs,
         grid_spec=pltpu.PrefetchScalarGridSpec(
@@ -351,6 +351,19 @@
     return out.reshape(n_ch, out_rows, lanes)
 
 
+def after(value, *others):
+    def copy_kernel(value_ref, *refs):
+        refs[-1][...] = value_ref[...]
+
+    return pl.pallas_call(
+        copy_kernel,
+        out_shape=jax.ShapeDtypeStruct(value.shape, value.dtype),
+        in_specs=[pl.BlockSpec(memory_space=pltpu.VMEM)] + [pl.BlockSpec(memory_space=pl.ANY) for _ in others],
+        out_specs=pl.BlockSpec(memory_space=pltpu.VMEM),
+        name="after",
+    )(value, *others)
+
+
 def mixing_blocks(coefficients, channel_cols, used_slots, lambda_low, lambda_high, chan_index, mult_index):
     n_ch, slots, lam = coefficients.shape
     local = channel_cols - (chan_index - R) * n_ch
@@ -415,21 +428,36 @@
     sent = mixing_blocks(
         coefficients, channel_cols, used_slots, lambda_low, lambda_high, chan_index, mult_index
     )
-    near_coefs = [sent]
+    near_sent = [sent]
+    bit = n_mult // 4
+    while bit:
+        near_sent += [flip(p, "mult", bit) for p in near_sent]
+        bit //= 2
+    sent = jnp.stack(near_sent)
+    ahead, behind = list(mine), list(mine)
+
+    def advance():
+        for part in range(2):
+            ahead[part] = ring_shift(ahead[part], "chan", 1)
+            behind[part] = ring_shift(behind[part], "chan", -1)
+
+    advance()
+    gathered = [after(sent, ahead[0], behind[0])]
     for by in range(1, n_chan):
-        near_coefs.append(
+        gathered.append(
             lax.ppermute(sent, "chan", [(i, (i + by) % n_chan) for i in range(n_chan)])
         )
-    near_coefs = [jnp.stack(near_coefs)]
+    gathered = jnp.stack(gathered)
+    near_coefs = [(gathered, w) for w in range(len(near_sent))]
 
     near_sets = [panels]
     bit = n_mult // 4
     while bit:
         near_sets += [flip(p, "mult", bit) for p in near_sets]
-        near_coefs += [flip(p, "mult", bit) for p in near_coefs]
         bit //= 2
     far = [flip(panels, "mult", n_mult // 2)]
-    far_coefs = [flip(c, "mult", n_mult // 2) for c in near_coefs]
+    far_gathered = flip(gathered, "mult", n_mult // 2)
+    far_coefs = [(far_gathered, w) for w in range(len(near_sent))]
 
     shape = (n_chan + 2 * R, 2 * rows, LANES)
 
@@ -438,12 +466,10 @@
 
     full_steps, switch = steps_of(n_chan)
     total = None
-    ahead, behind = list(mine), list(mine)
     held, late = [(*mine, spot(0))], []
     for step in range(1, full_steps + 1):
-        for part in range(2):
-            ahead[part] = ring_shift(ahead[part], "chan", 1)
-            behind[part] = ring_shift(behind[part], "chan", -1)
+        if step > 1:
+            advance()
         held += [(*ahead, spot(-step)), (*behind, spot(step))]
         if step <= switch:
             total = add(total, near_sets, near_coefs, held)

time: 180 us -> 191 us (1.061)
  the two profiles are of different devices: /device:TPU:2 before, /device:TPU:14 now
where the time goes in v5:
time: 191 us; the launch traced here: 190 us
  Pallas kernels  75.6 us (40%)
  waiting for transfers between devices  65.1 us (34%)
  starting transfers between devices  44.4 us (23%)
  local copies, waits for them, and re-layouts  4.3 us (2%)
    pallas_call x5, Pallas kernels, unit(): pl.pallas_call(functools.partial(unit_kernel, n_p=n, which=tuple((w for _...  58.4 us
    ppermute x14, waiting for transfers between devices, ring_shift(): lax.ppermute(value, axis, [(order[i], order[(i + by) % n]) for i in range...  27.3 us
    ppermute x7, waiting for transfers between devices, body(): lax.ppermute(sent, 'chan', [(i, (i + by) % n_chan) for i in range(n_chan)])  21.5 us
    ppermute x8, waiting for transfers between devices, body(): pieces.append(lax.ppermute(sends[s], ('mult', 'chan'), pairs))  16.3 us
    ppermute x7, starting transfers between devices, body(): lax.ppermute(sent, 'chan', [(i, (i + by) % n_chan) for i in range(n_chan)])  16.1 us
    ppermute x14, starting transfers between devices, ring_shift(): lax.ppermute(value, axis, [(order[i], order[(i + by) % n]) for i in range...  15.4 us
    ppermute x8, starting transfers between devices, body(): pieces.append(lax.ppermute(sends[s], ('mult', 'chan'), pairs))  11.5 us
    pallas_call x2, Pallas kernels, pack(): pl.pallas_call(functools.partial(pack_kernel, kw=kw), out_shape=jax.Shape...  7.3 us
  transfers between devices with their start and end apart: 34, of which 16 were waited for; matrix products, arithmetic and copies ran while one was open for 1% of the time, Pallas kernels for 30%

profile of v5, /device:TPU:14, one launch (start us, length us, event | category | flops | bytes accessed | tf_op | source)
XLA Modules:
  0.0 190.1 jit_solution(3545825566625392049)
XLA Ops:
  0.0 3.6 %pack.2.refs_4_ = f32[512,256]{1,0:T(8,128)} custom-call(f32[8,1024,128]{2,1,0:T(8,128)} %col_ref.5), custom_call_target="tpu_custom_call" | custom-call | tf_op jit(solution)/shard_map/pack/pallas_call | solution.py:69
  5.6 3.7 %pack.3.refs_5_ = f32[512,256]{1,0:T(8,128)} custom-call(f32[8,1024,128]{2,1,0:T(8,128)} %col_ref.5), custom_call_target="tpu_custom_call" | custom-call | tf_op jit(solution)/shard_map/pack/pallas_call | solution.py:69
  13.0 5.6 %collective-permute-done.2.refs_0_.refs_6_ = f32[512,256]{1,0:T(8,128)S(1)} collective-permute-done((f32[512,256]{1,0:T(8,128)}, f32[512,256]{1,0:T(8,128)S(1)}, u32[]{:S(2)}, u32[]{:S(2)}) %collective-permute-start.2) | collective-permute-done | bytes 524320 | tf_op jit(solution)/shard_map/ppermute | solution.py:25
  19.1 2.6 %collective-permute-start.7 = (f32[2,8,128]{2,1,0:T(8,128)S(1)}, f32[2,8,128]{2,1,0:T(8,128)S(1)}, u32[]{:S(2)}, u32[]{:S(2)}) collective-permute-start(f32[2,8,128]{2,1,0:T(8,128)S(1)} %pad_maximum_fusion.value_ref), channel_id=1, source_target_pairs={{0,1},{1,2},{2,3},{3,4},{4,5},{5,6},{6,7},{7,0},{8,9},{9,10},{10,1... | collective-permute-start | bytes 24584 | tf_op jit(solution)/shard_map/ppermute | solution.py:448
  23.8 4.4 %collective-permute-done.7 = f32[2,8,128]{2,1,0:T(8,128)S(1)} collective-permute-done((f32[2,8,128]{2,1,0:T(8,128)S(1)}, f32[2,8,128]{2,1,0:T(8,128)S(1)}, u32[]{:S(2)}, u32[]{:S(2)}) %collective-permute-start.7) | collective-permute-done | bytes 8224 | tf_op jit(solution)/shard_map/ppermute | solution.py:448
  29.7 2.3 %collective-permute-done.8 = f32[2,8,128]{2,1,0:T(8,128)S(1)} collective-permute-done((f32[2,8,128]{2,1,0:T(8,128)}, f32[2,8,128]{2,1,0:T(8,128)S(1)}, u32[]{:S(2)}, u32[]{:S(2)}) %collective-permute-start.8) | collective-permute-done | bytes 8224 | tf_op jit(solution)/shard_map/ppermute | solution.py:448
  32.0 4.5 %collective-permute-start.9 = (f32[2,8,128]{2,1,0:T(8,128)}, f32[2,8,128]{2,1,0:T(8,128)S(1)}, u32[]{:S(2)}, u32[]{:S(2)}) collective-permute-start(f32[2,8,128]{2,1,0:T(8,128)} %copy-done.16), channel_id=1, source_target_pairs={{0,3},{1,4},{2,5},{3,6},{4,7},{5,0},{6,1},{7,2},{8,11},{9,12},{10,... | collective-permute-start | bytes 24584 | tf_op jit(solution)/shard_map/ppermute | solution.py:448
  36.5 3.2 %collective-permute-done.9 = f32[2,8,128]{2,1,0:T(8,128)S(1)} collective-permute-done((f32[2,8,128]{2,1,0:T(8,128)}, f32[2,8,128]{2,1,0:T(8,128)S(1)}, u32[]{:S(2)}, u32[]{:S(2)}) %collective-permute-start.9) | collective-permute-done | bytes 8224 | tf_op jit(solution)/shard_map/ppermute | solution.py:448
  40.1 4.4 %collective-permute-done.10 = f32[2,8,128]{2,1,0:T(8,128)S(1)} collective-permute-done((f32[2,8,128]{2,1,0:T(8,128)}, f32[2,8,128]{2,1,0:T(8,128)S(1)}, u32[]{:S(2)}, u32[]{:S(2)}) %collective-permute-start.10) | collective-permute-done | bytes 8224 | tf_op jit(solution)/shard_map/ppermute | solution.py:448
  44.5 3.8 %collective-permute-start.11 = (f32[2,8,128]{2,1,0:T(8,128)}, f32[2,8,128]{2,1,0:T(8,128)S(1)}, u32[]{:S(2)}, u32[]{:S(2)}) collective-permute-start(f32[2,8,128]{2,1,0:T(8,128)} %copy-done.16), channel_id=1, source_target_pairs={{0,5},{1,6},{2,7},{3,0},{4,1},{5,2},{6,3},{7,4},{8,13},{9,14},{10,... | collective-permute-start | bytes 24584 | tf_op jit(solution)/shard_map/ppermute | solution.py:448
  48.3 1.8 collective-permute-done.11
  50.2 2.0 %collective-permute-start.12 = (f32[2,8,128]{2,1,0:T(8,128)}, f32[2,8,128]{2,1,0:T(8,128)S(1)}, u32[]{:S(2)}, u32[]{:S(2)}) collective-permute-start(f32[2,8,128]{2,1,0:T(8,128)} %copy-done.16), channel_id=1, source_target_pairs={{0,6},{1,7},{2,0},{3,1},{4,2},{5,3},{6,4},{7,5},{8,14},{9,15},{10,... | collective-permute-start | bytes 24584 | tf_op jit(solution)/shard_map/ppermute | solution.py:448
  55.2 3.6 %collective-permute-done.13 = f32[2,8,128]{2,1,0:T(8,128)S(1)} collective-permute-done((f32[2,8,128]{2,1,0:T(8,128)}, f32[2,8,128]{2,1,0:T(8,128)S(1)}, u32[]{:S(2)}, u32[]{:S(2)}) %collective-permute-start.13) | collective-permute-done | bytes 8224 | tf_op jit(solution)/shard_map/ppermute | solution.py:448
  60.9 11.0 %unit.5.refs_10_ = f32[12,256,128]{2,1,0:T(8,128)S(1)} custom-call(s32[11]{0:T(128)S(1)} %pad_add_fusion.sc_ref, f32[2,2,128,1024]{3,2,1,0:T(8,128)S(1)} %copy-done, f32[2,2,128,1024]{3,2,1,0:T(8,128)S(1)} %copy-done, f32[2,2,128,1024]{3,2,1,0:T(8,128)} %collective-permute-done.refs_2_.refs_3_, f32[2,2,128,1024]{3,2,1,0:T(8,128)} %collective-permute-done.refs_2_.refs_3_, ...), custom_call_target="tpu_custom_call" | custom-call | flops 6341787648 | bytes 4194304 | tf_op jit(solution)/shard_map/unit/pallas_call | solution.py:241
  72.0 2.8 %collective-permute-start.18 = (f32[512,256]{1,0:T(8,128)}, f32[512,256]{1,0:T(8,128)S(1)}, u32[]{:S(2)}, u32[]{:S(2)}) collective-permute-start(f32[512,256]{1,0:T(8,128)} %collective-permute-done.5.refs_9_), channel_id=1, source_target_pairs={{0,1},{2,0},{4,2},{6,4},{7,6},{5,7},{3,5},{1,3},{8,9},{10,8},{12,1... | collective-permute-start | bytes 1572872 | tf_op jit(solution)/shard_map/ppermute | solution.py:25
  76.9 10.6 %collective-permute-done.18.refs_7_.refs_13_ = f32[512,256]{1,0:T(8,128)S(1)} collective-permute-done((f32[512,256]{1,0:T(8,128)}, f32[512,256]{1,0:T(8,128)S(1)}, u32[]{:S(2)}, u32[]{:S(2)}) %collective-permute-start.18) | collective-permute-done | bytes 524320 | tf_op jit(solution)/shard_map/ppermute | solution.py:25
  87.5 2.4 %collective-permute-start.19 = (f32[512,256]{1,0:T(8,128)S(1)}, f32[512,256]{1,0:T(8,128)S(1)}, u32[]{:S(2)}, u32[]{:S(2)}) collective-permute-start(f32[512,256]{1,0:T(8,128)S(1)} %collective-permute-done.18.refs_7_.refs_13_), channel_id=1, source_target_pairs={{0,1},{2,0},{4,2},{6,4},{7,6},{5,7},{3,5},{1,3},{8,9},{10,8},{12,1... | collective-permute-start | bytes 1572872 | tf_op jit(solution)/shard_map/ppermute | solution.py:25
  89.8 11.0 %collective-permute-done.22.refs_5_.refs_11_ = f32[512,256]{1,0:T(8,128)S(1)} collective-permute-done((f32[512,256]{1,0:T(8,128)}, f32[512,256]{1,0:T(8,128)S(1)}, u32[]{:S(2)}, u32[]{:S(2)}) %collective-permute-start.22) | collective-permute-done | bytes 524320 | tf_op jit(solution)/shard_map/ppermute | solution.py:25
  101.4 8.0 %unit.6.refs_16_ = f32[12,256,128]{2,1,0:T(8,128)S(1)} custom-call(s32[11]{0:T(128)S(1)} %pad_add_fusion.sc_ref, f32[2,2,128,1024]{3,2,1,0:T(8,128)S(1)} %copy-done, f32[2,2,128,1024]{3,2,1,0:T(8,128)S(1)} %copy-done, f32[2,2,128,1024]{3,2,1,0:T(8,128)} %collective-permute-done.refs_2_.refs_3_, ...), custom_call_target="tpu_custom_call", output_to_operand_aliasing={{}: (11, {})} | custom-call | flops 4227858432 | bytes 4194304 | tf_op jit(solution)/shard_map/unit/pallas_call | solution.py:241
  109.4 2.1 %collective-permute-start.25 = (f32[512,256]{1,0:T(8,128)S(1)}, f32[512,256]{1,0:T(8,128)S(1)}, u32[]{:S(2)}, u32[]{:S(2)}) collective-permute-start(f32[512,256]{1,0:T(8,128)S(1)} %collective-permute-done.24.refs_6_.refs_12_), channel_id=1, source_target_pairs={{0,1},{2,0},{4,2},{6,4},{7,6},{5,7},{3,5},{1,3},{8,9},{10,8},{12,1... | collective-permute-start | bytes 1572872 | tf_op jit(solution)/shard_map/ppermute | solution.py:25
  111.5 1.9 collective-permute-start.20
  113.5 16.5 %unit.7.refs_16_ = f32[12,256,128]{2,1,0:T(8,128)S(1)} custom-call(s32[11]{0:T(128)S(1)} %pad_add_fusion.sc_ref, f32[2,2,128,1024]{3,2,1,0:T(8,128)} %collective-permute-done.1.refs_0_.refs_1_.refs_4_.refs_5_, f32[2,2,128,1024]{3,2,1,0:T(8,128)} %collective-permute-done.1.refs_0_.refs_1_.refs_4_.refs_5_, ...), custom_call_target="tpu_custom_call", output_to_operand_aliasing={{}: (17, {})} | custom-call | flops 10569646080 | bytes 4194304 | tf_op jit(solution)/shard_map/unit/pallas_call | solution.py:241
  130.0 13.1 %unit.8.refs_14_ = f32[12,256,128]{2,1,0:T(8,128)S(1)} custom-call(s32[11]{0:T(128)S(1)} %pad_add_fusion.sc_ref, f32[2,2,128,1024]{3,2,1,0:T(8,128)S(1)} %copy-done, f32[2,2,128,1024]{3,2,1,0:T(8,128)S(1)} %copy-done, f32[2,2,128,1024]{3,2,1,0:T(8,128)} %collective-permute-done.refs_2_.refs_3_, ...), custom_call_target="tpu_custom_call", output_to_operand_aliasing={{}: (17, {})} | custom-call | flops 8455716864 | bytes 8388608 | tf_op jit(solution)/shard_map/unit/pallas_call | solution.py:241
  143.2 9.8 %unit.9 = (f32[256,128]{1,0:T(8,128)S(1)}, f32[256,128]{1,0:T(8,128)S(1)}, f32[256,128]{1,0:T(8,128)S(1)}, f32[256,128]{1,0:T(8,128)S(1)}, f32[256,128]{1,0:T(8,...) custom-call(s32[11]{0:T(128)S(1)} %pad_add_fusion.sc_ref, ...), custom_call_target="tpu_custom_call" | custom-call | flops 4227858432 | bytes 8388608 | tf_op jit(solution)/shard_map/unit/pallas_call | solution.py:241
  153.0 1.9 %collective-permute-start.26 = (f32[256,128]{1,0:T(8,128)S(1)}, f32[256,128]{1,0:T(8,128)S(1)}, u32[]{:S(2)}, u32[]{:S(2)}) collective-permute-start(f32[256,128]{1,0:T(8,128)S(1)} %get-tuple-element.21), channel_id=1, source_target_pairs={{0,0},{1,1},{2,8},{3,9},{4,16},{5,17},{6,24},{7,25},{8,2},{9,3},{1... | collective-permute-start | bytes 393224 | tf_op jit(solution)/shard_map/ppermute | solution.py:502
  156.2 3.1 %collective-permute-start.28 = (f32[256,128]{1,0:T(8,128)S(1)}, f32[256,128]{1,0:T(8,128)S(1)}, u32[]{:S(2)}, u32[]{:S(2)}) collective-permute-start(f32[256,128]{1,0:T(8,128)S(1)} %get-tuple-element.23), channel_id=1, source_target_pairs={{0,2},{1,3},{2,10},{3,11},{4,18},{5,19},{6,26},{7,27},{8,4},{9,5},... | collective-permute-start | bytes 393224 | tf_op jit(solution)/shard_map/ppermute | solution.py:502
  159.4 4.4 %collective-permute-start.29 = (f32[256,128]{1,0:T(8,128)S(1)}, f32[256,128]{1,0:T(8,128)S(1)}, u32[]{:S(2)}, u32[]{:S(2)}) collective-permute-start(f32[256,128]{1,0:T(8,128)S(1)} %get-tuple-element.24), channel_id=1, source_target_pairs={{0,3},{1,4},{2,11},{3,12},{4,19},{5,20},{6,27},{7,28},{8,5},{9,6},... | collective-permute-start | bytes 393224 | tf_op jit(solution)/shard_map/ppermute | solution.py:502
  164.4 8.2 %collective-permute-done.27 = f32[256,128]{1,0:T(8,128)S(1)} collective-permute-done((f32[256,128]{1,0:T(8,128)S(1)}, f32[256,128]{1,0:T(8,128)S(1)}, u32[]{:S(2)}, u32[]{:S(2)}) %collective-permute-start.27) | collective-permute-done | bytes 131104 | tf_op jit(solution)/shard_map/ppermute | solution.py:502
  172.7 4.3 %shifted.1 = f32[8,256,128]{2,1,0:T(8,128)} custom-call(s32[11]{0:T(128)} %copy-done.7, f32[8]{0:T(128)} %energy_ref.1, f32[2]{0:T(128)} %contour_ref.1, f32[8,1024,128]{2,1,0:T(8,128)} %col_ref.5), custom_call_target="tpu_custom_call" | custom-call | tf_op jit(solution)/shard_map/shifted/pallas_call | solution.py:287
  178.5 2.7 %collective-permute-done.30 = f32[256,128]{1,0:T(8,128)S(1)} collective-permute-done((f32[256,128]{1,0:T(8,128)S(1)}, f32[256,128]{1,0:T(8,128)S(1)}, u32[]{:S(2)}, u32[]{:S(2)}) %collective-permute-start.30) | collective-permute-done | bytes 131104 | tf_op jit(solution)/shard_map/ppermute | solution.py:502
  181.2 3.3 %collective-permute-done.31 = f32[256,128]{1,0:T(8,128)S(1)} collective-permute-done((f32[256,128]{1,0:T(8,128)S(1)}, f32[256,128]{1,0:T(8,128)S(1)}, u32[]{:S(2)}, u32[]{:S(2)}) %collective-permute-start.31) | collective-permute-done | bytes 131104 | tf_op jit(solution)/shard_map/ppermute | solution.py:502
  185.8 4.3 %finish.1 = f32[8,2,128,128]{3,2,1,0:T(8,128)} custom-call(s32[11]{0:T(128)} %copy-done.7, f32[8,2,128,128]{3,2,1,0:T(8,128)} %bitcast.49, f32[2,128,128]{2,1,0:T(8,128)} %bitcast.50, f32[2,128,128]{2,1,0:T(8,128)} %bitcast.51, f32[2,128,128]{2,1,0:T(8,128)} %bitcast.52, f32[2,128,128]{2,1,0:T(8,128)} %bitcast.53, f32[2,128,128]{2,1,0:T(8,128)} %bitcast.54, ...), custom_call_target="tpu_custom_call" | custom-call | tf_op jit(solution)/shard_map/finish/pallas_call | solution.py:334
  (115 shorter events, 22.9 us)
Async XLA Ops:
  3.6 15.0 %collective-permute-start.2 = (f32[512,256]{1,0:T(8,128)}, f32[512,256]{1,0:T(8,128)S(1)}, u32[]{:S(2)}, u32[]{:S(2)}) collective-permute-start(f32[512,256]{1,0:T(8,128)} %pack.2.refs_4_), channel_id=1, source_target_pairs={{0,2},{2,4},{4,6},{6,7},{7,5},{5,3},{3,1},{1,0},{8,10},{10,12},{12... | collective-permute-start | bytes 1572872 | tf_op jit(solution)/shard_map/ppermute | solution.py:25
  4.0 15.1 %collective-permute-start.4 = (f32[512,256]{1,0:T(8,128)}, f32[512,256]{1,0:T(8,128)}, u32[]{:S(2)}, u32[]{:S(2)}) collective-permute-start(f32[512,256]{1,0:T(8,128)} %pack.2.refs_4_), channel_id=1, source_target_pairs={{0,1},{2,0},{4,2},{6,4},{7,6},{5,7},{3,5},{1,3},{8,9},{10,8},{12,1... | collective-permute-start | bytes 1572872 | tf_op jit(solution)/shard_map/ppermute | solution.py:25
  10.0 48.8 %collective-permute-start.3 = (f32[512,256]{1,0:T(8,128)}, f32[512,256]{1,0:T(8,128)}, u32[]{:S(2)}, u32[]{:S(2)}) collective-permute-start(f32[512,256]{1,0:T(8,128)} %pack.3.refs_5_), channel_id=1, source_target_pairs={{0,2},{2,4},{4,6},{6,7},{7,5},{5,3},{3,1},{1,0},{8,10},{10,12},{12... | collective-permute-start | bytes 1572872 | tf_op jit(solution)/shard_map/ppermute | solution.py:25
  10.5 48.3 %collective-permute-start = (f32[2,2,128,1024]{3,2,1,0:T(8,128)S(1)}, f32[2,2,128,1024]{3,2,1,0:T(8,128)}, u32[]{:S(2)}, u32[]{:S(2)}) collective-permute-start(f32[2,2,128,1024]{3,2,1,0:T(8,128)S(1)} %copy-done), channel_id=1, source_target_pairs={{0,8},{8,0},{16,24},{24,16},{1,9},{9,1},{17,25},{25,17},{2,10},{10... | collective-permute-start | bytes 6291464 | tf_op jit(solution)/shard_map/ppermute | solution.py:29
  11.4 47.3 %collective-permute-start.5 = (f32[512,256]{1,0:T(8,128)}, f32[512,256]{1,0:T(8,128)}, u32[]{:S(2)}, u32[]{:S(2)}) collective-permute-start(f32[512,256]{1,0:T(8,128)} %pack.3.refs_5_), channel_id=1, source_target_pairs={{0,1},{2,0},{4,2},{6,4},{7,6},{5,7},{3,5},{1,3},{8,9},{10,8},{12,1... | collective-permute-start | bytes 1572872 | tf_op jit(solution)/shard_map/ppermute | solution.py:25
  18.6 53.4 %collective-permute-start.1 = (f32[2,2,128,1024]{3,2,1,0:T(8,128)S(1)}, f32[2,2,128,1024]{3,2,1,0:T(8,128)}, u32[]{:S(2)}, u32[]{:S(2)}) collective-permute-start(f32[2,2,128,1024]{3,2,1,0:T(8,128)S(1)} %copy-done), channel_id=1, source_target_pairs={{0,16},{8,24},{16,0},{24,8},{1,17},{9,25},{17,1},{25,9},{2,18},{10... | collective-permute-start | bytes 6291464 | tf_op jit(solution)/shard_map/ppermute | solution.py:29
  19.1 9.0 %collective-permute-start.7 = (f32[2,8,128]{2,1,0:T(8,128)S(1)}, f32[2,8,128]{2,1,0:T(8,128)S(1)}, u32[]{:S(2)}, u32[]{:S(2)}) collective-permute-start(f32[2,8,128]{2,1,0:T(8,128)S(1)} %pad_maximum_fusion.value_ref), channel_id=1, source_target_pairs={{0,1},{1,2},{2,3},{3,4},{4,5},{5,6},{6,7},{7,0},{8,9},{9,10},{10,1... | collective-permute-start | bytes 24584 | tf_op jit(solution)/shard_map/ppermute | solution.py:448
  28.1 3.9 %collective-permute-start.8 = (f32[2,8,128]{2,1,0:T(8,128)}, f32[2,8,128]{2,1,0:T(8,128)S(1)}, u32[]{:S(2)}, u32[]{:S(2)}) collective-permute-start(f32[2,8,128]{2,1,0:T(8,128)} %copy-done.16), channel_id=1, source_target_pairs={{0,2},{1,3},{2,4},{3,5},{4,6},{5,7},{6,0},{7,1},{8,10},{9,11},{10,... | collective-permute-start | bytes 24584 | tf_op jit(solution)/shard_map/ppermute | solution.py:448
  32.0 7.7 %collective-permute-start.9 = (f32[2,8,128]{2,1,0:T(8,128)}, f32[2,8,128]{2,1,0:T(8,128)S(1)}, u32[]{:S(2)}, u32[]{:S(2)}) collective-permute-start(f32[2,8,128]{2,1,0:T(8,128)} %copy-done.16), channel_id=1, source_target_pairs={{0,3},{1,4},{2,5},{3,6},{4,7},{5,0},{6,1},{7,2},{8,11},{9,12},{10,... | collective-permute-start | bytes 24584 | tf_op jit(solution)/shard_map/ppermute | solution.py:448
  39.7 4.8 %collective-permute-start.10 = (f32[2,8,128]{2,1,0:T(8,128)}, f32[2,8,128]{2,1,0:T(8,128)S(1)}, u32[]{:S(2)}, u32[]{:S(2)}) collective-permute-start(f32[2,8,128]{2,1,0:T(8,128)} %copy-done.16), channel_id=1, source_target_pairs={{0,4},{1,5},{2,6},{3,7},{4,0},{5,1},{6,2},{7,3},{8,12},{9,13},{10,... | collective-permute-start | bytes 24584 | tf_op jit(solution)/shard_map/ppermute | solution.py:448
  44.5 5.7 %collective-permute-start.11 = (f32[2,8,128]{2,1,0:T(8,128)}, f32[2,8,128]{2,1,0:T(8,128)S(1)}, u32[]{:S(2)}, u32[]{:S(2)}) collective-permute-start(f32[2,8,128]{2,1,0:T(8,128)} %copy-done.16), channel_id=1, source_target_pairs={{0,5},{1,6},{2,7},{3,0},{4,1},{5,2},{6,3},{7,4},{8,13},{9,14},{10,... | collective-permute-start | bytes 24584 | tf_op jit(solution)/shard_map/ppermute | solution.py:448
  54.0 4.8 %collective-permute-start.13 = (f32[2,8,128]{2,1,0:T(8,128)}, f32[2,8,128]{2,1,0:T(8,128)S(1)}, u32[]{:S(2)}, u32[]{:S(2)}) collective-permute-start(f32[2,8,128]{2,1,0:T(8,128)} %copy-done.16), channel_id=1, source_target_pairs={{0,7},{1,0},{2,1},{3,2},{4,3},{5,4},{6,5},{7,6},{8,15},{9,8},{10,9... | collective-permute-start | bytes 24584 | tf_op jit(solution)/shard_map/ppermute | solution.py:448
  71.9 41.6 %collective-permute-start.14 = (f32[2,2,128,1024]{3,2,1,0:T(8,128)}, f32[2,2,128,1024]{3,2,1,0:T(8,128)S(1)}, u32[]{:S(2)}, u32[]{:S(2)}) collective-permute-start(f32[2,2,128,1024]{3,2,1,0:T(8,128)} %collective-permute-done.1.refs_0_.refs_1_.refs_4_.refs_5_), channel_id=1, source_target_pairs={{0,8},{8,0},{16,24},{24,16},{1,9},{9,1},{17,25},{25,17},{2,10},{10... | collective-permute-start | bytes 6291464 | tf_op jit(solution)/shard_map/ppermute | solution.py:29
  72.0 15.4 %collective-permute-start.18 = (f32[512,256]{1,0:T(8,128)}, f32[512,256]{1,0:T(8,128)S(1)}, u32[]{:S(2)}, u32[]{:S(2)}) collective-permute-start(f32[512,256]{1,0:T(8,128)} %collective-permute-done.5.refs_9_), channel_id=1, source_target_pairs={{0,1},{2,0},{4,2},{6,4},{7,6},{5,7},{3,5},{1,3},{8,9},{10,8},{12,1... | collective-permute-start | bytes 1572872 | tf_op jit(solution)/shard_map/ppermute | solution.py:25
  74.8 15.0 %collective-permute-start.15 = (f32[512,256]{1,0:T(8,128)S(1)}, f32[512,256]{1,0:T(8,128)S(1)}, u32[]{:S(2)}, u32[]{:S(2)}) collective-permute-start(f32[512,256]{1,0:T(8,128)S(1)} %copy-done.5), channel_id=1, source_target_pairs={{0,2},{2,4},{4,6},{6,7},{7,5},{5,3},{3,1},{1,0},{8,10},{10,12},{12... | collective-permute-start | bytes 1572872 | tf_op jit(solution)/shard_map/ppermute | solution.py:25
  74.8 26.0 %collective-permute-start.22 = (f32[512,256]{1,0:T(8,128)}, f32[512,256]{1,0:T(8,128)S(1)}, u32[]{:S(2)}, u32[]{:S(2)}) collective-permute-start(f32[512,256]{1,0:T(8,128)} %collective-permute-done.3.refs_7_), channel_id=1, source_target_pairs={{0,2},{2,4},{4,6},{6,7},{7,5},{5,3},{3,1},{1,0},{8,10},{10,12},{12... | collective-permute-start | bytes 1572872 | tf_op jit(solution)/shard_map/ppermute | solution.py:25
  76.1 25.2 %collective-permute-start.24 = (f32[512,256]{1,0:T(8,128)}, f32[512,256]{1,0:T(8,128)S(1)}, u32[]{:S(2)}, u32[]{:S(2)}) collective-permute-start(f32[512,256]{1,0:T(8,128)} %collective-permute-done.4.refs_1_.refs_8_), channel_id=1, source_target_pairs={{0,1},{2,0},{4,2},{6,4},{7,6},{5,7},{3,5},{1,3},{8,9},{10,8},{12,1... | collective-permute-start | bytes 1572872 | tf_op jit(solution)/shard_map/ppermute | solution.py:25
  87.5 24.0 %collective-permute-start.19 = (f32[512,256]{1,0:T(8,128)S(1)}, f32[512,256]{1,0:T(8,128)S(1)}, u32[]{:S(2)}, u32[]{:S(2)}) collective-permute-start(f32[512,256]{1,0:T(8,128)S(1)} %collective-permute-done.18.refs_7_.refs_13_), channel_id=1, source_target_pairs={{0,1},{2,0},{4,2},{6,4},{7,6},{5,7},{3,5},{1,3},{8,9},{10,8},{12,1... | collective-permute-start | bytes 1572872 | tf_op jit(solution)/shard_map/ppermute | solution.py:25
  89.8 23.5 %collective-permute-start.16 = (f32[512,256]{1,0:T(8,128)S(1)}, f32[512,256]{1,0:T(8,128)S(1)}, u32[]{:S(2)}, u32[]{:S(2)}) collective-permute-start(f32[512,256]{1,0:T(8,128)S(1)} %collective-permute-done.15.refs_4_.refs_10_), channel_id=1, source_target_pairs={{0,2},{2,4},{4,6},{6,7},{7,5},{5,3},{3,1},{1,0},{8,10},{10,12},{12... | collective-permute-start | bytes 1572872 | tf_op jit(solution)/shard_map/ppermute | solution.py:25
  100.9 8.5 %collective-permute-start.21 = (f32[8,2,8,128]{3,2,1,0:T(8,128)S(1)}, f32[8,2,8,128]{3,2,1,0:T(8,128)S(1)}, u32[]{:S(2)}, u32[]{:S(2)}) collective-permute-start(f32[8,2,8,128]{3,2,1,0:T(8,128)S(1)} %constant_dynamic-update-slice_fusion.refs_10_.refs_11_.refs_12_.refs_8_.refs_9_.refs_13_), channel_id=1, source_target_pairs={{0,16},{8,24},{16,0},{24,8},{1,17},{9,25},{17,1},{25,9},{2,18},{10... | collective-permute-start | bytes 196616 | tf_op jit(solution)/shard_map/ppermute | solution.py:29
  101.4 28.6 %collective-permute-start.23 = (f32[512,256]{1,0:T(8,128)S(1)}, f32[512,256]{1,0:T(8,128)S(1)}, u32[]{:S(2)}, u32[]{:S(2)}) collective-permute-start(f32[512,256]{1,0:T(8,128)S(1)} %collective-permute-done.22.refs_5_.refs_11_), channel_id=1, source_target_pairs={{0,2},{2,4},{4,6},{6,7},{7,5},{5,3},{3,1},{1,0},{8,10},{10,12},{12... | collective-permute-start | bytes 1572872 | tf_op jit(solution)/shard_map/ppermute | solution.py:25
  109.4 20.6 %collective-permute-start.25 = (f32[512,256]{1,0:T(8,128)S(1)}, f32[512,256]{1,0:T(8,128)S(1)}, u32[]{:S(2)}, u32[]{:S(2)}) collective-permute-start(f32[512,256]{1,0:T(8,128)S(1)} %collective-permute-done.24.refs_6_.refs_12_), channel_id=1, source_target_pairs={{0,1},{2,0},{4,2},{6,4},{7,6},{5,7},{3,5},{1,3},{8,9},{10,8},{12,1... | collective-permute-start | bytes 1572872 | tf_op jit(solution)/shard_map/ppermute | solution.py:25
  111.5 31.7 %collective-permute-start.20 = (f32[512,256]{1,0:T(8,128)S(1)}, f32[512,256]{1,0:T(8,128)S(1)}, u32[]{:S(2)}, u32[]{:S(2)}) collective-permute-start(f32[512,256]{1,0:T(8,128)S(1)} %collective-permute-done.19.refs_11_), channel_id=1, source_target_pairs={{0,1},{2,0},{4,2},{6,4},{7,6},{5,7},{3,5},{1,3},{8,9},{10,8},{12,1... | collective-permute-start | bytes 1572872 | tf_op jit(solution)/shard_map/ppermute | solution.py:25
  113.3 29.8 %collective-permute-start.17 = (f32[512,256]{1,0:T(8,128)S(1)}, f32[512,256]{1,0:T(8,128)S(1)}, u32[]{:S(2)}, u32[]{:S(2)}) collective-permute-start(f32[512,256]{1,0:T(8,128)S(1)} %collective-permute-done.16.refs_8_), channel_id=1, source_target_pairs={{0,2},{2,4},{4,6},{6,7},{7,5},{5,3},{3,1},{1,0},{8,10},{10,12},{12... | collective-permute-start | bytes 1572872 | tf_op jit(solution)/shard_map/ppermute | solution.py:25
  153.0 11.5 %collective-permute-start.26 = (f32[256,128]{1,0:T(8,128)S(1)}, f32[256,128]{1,0:T(8,128)S(1)}, u32[]{:S(2)}, u32[]{:S(2)}) collective-permute-start(f32[256,128]{1,0:T(8,128)S(1)} %get-tuple-element.21), channel_id=1, source_target_pairs={{0,0},{1,1},{2,8},{3,9},{4,16},{5,17},{6,24},{7,25},{8,2},{9,3},{1... | collective-permute-start | bytes 393224 | tf_op jit(solution)/shard_map/ppermute | solution.py:502
  154.9 17.7 %collective-permute-start.27 = (f32[256,128]{1,0:T(8,128)S(1)}, f32[256,128]{1,0:T(8,128)S(1)}, u32[]{:S(2)}, u32[]{:S(2)}) collective-permute-start(f32[256,128]{1,0:T(8,128)S(1)} %get-tuple-element.22), channel_id=1, source_target_pairs={{0,1},{1,2},{2,9},{3,10},{4,17},{5,18},{6,25},{7,26},{8,3},{9,4},{... | collective-permute-start | bytes 393224 | tf_op jit(solution)/shard_map/ppermute | solution.py:502
  156.2 16.4 %collective-permute-start.28 = (f32[256,128]{1,0:T(8,128)S(1)}, f32[256,128]{1,0:T(8,128)S(1)}, u32[]{:S(2)}, u32[]{:S(2)}) collective-permute-start(f32[256,128]{1,0:T(8,128)S(1)} %get-tuple-element.23), channel_id=1, source_target_pairs={{0,2},{1,3},{2,10},{3,11},{4,18},{5,19},{6,26},{7,27},{8,4},{9,5},... | collective-permute-start | bytes 393224 | tf_op jit(solution)/shard_map/ppermute | solution.py:502
  159.4 19.1 %collective-permute-start.29 = (f32[256,128]{1,0:T(8,128)S(1)}, f32[256,128]{1,0:T(8,128)S(1)}, u32[]{:S(2)}, u32[]{:S(2)}) collective-permute-start(f32[256,128]{1,0:T(8,128)S(1)} %get-tuple-element.24), channel_id=1, source_target_pairs={{0,3},{1,4},{2,11},{3,12},{4,19},{5,20},{6,27},{7,28},{8,5},{9,6},... | collective-permute-start | bytes 393224 | tf_op jit(solution)/shard_map/ppermute | solution.py:502
  163.8 17.4 %collective-permute-start.30 = (f32[256,128]{1,0:T(8,128)S(1)}, f32[256,128]{1,0:T(8,128)S(1)}, u32[]{:S(2)}, u32[]{:S(2)}) collective-permute-start(f32[256,128]{1,0:T(8,128)S(1)} %get-tuple-element.25), channel_id=1, source_target_pairs={{0,4},{1,5},{2,12},{3,13},{4,20},{5,21},{6,28},{7,29},{8,6},{9,7},... | collective-permute-start | bytes 393224 | tf_op jit(solution)/shard_map/ppermute | solution.py:502
  164.4 20.0 %collective-permute-start.31 = (f32[256,128]{1,0:T(8,128)S(1)}, f32[256,128]{1,0:T(8,128)S(1)}, u32[]{:S(2)}, u32[]{:S(2)}) collective-permute-start(f32[256,128]{1,0:T(8,128)S(1)} %get-tuple-element.26), channel_id=1, source_target_pairs={{0,5},{1,6},{2,13},{3,14},{4,21},{5,22},{6,29},{7,30},{8,7},{9,0},... | collective-permute-start | bytes 393224 | tf_op jit(solution)/shard_map/ppermute | solution.py:502
  172.6 11.8 %collective-permute-start.32 = (f32[256,128]{1,0:T(8,128)S(1)}, f32[256,128]{1,0:T(8,128)S(1)}, u32[]{:S(2)}, u32[]{:S(2)}) collective-permute-start(f32[256,128]{1,0:T(8,128)S(1)} %get-tuple-element.27), channel_id=1, source_target_pairs={{0,6},{1,7},{2,14},{3,15},{4,22},{5,23},{6,30},{7,31},{8,0},{9,1},... | collective-permute-start | bytes 393224 | tf_op jit(solution)/shard_map/ppermute | solution.py:502
  172.7 12.5 %collective-permute-start.33 = (f32[256,128]{1,0:T(8,128)S(1)}, f32[256,128]{1,0:T(8,128)S(1)}, u32[]{:S(2)}, u32[]{:S(2)}) collective-permute-start(f32[256,128]{1,0:T(8,128)S(1)} %get-tuple-element.28), channel_id=1, source_target_pairs={{0,7},{1,0},{2,15},{3,8},{4,23},{5,16},{6,31},{7,24},{8,1},{9,2},{... | collective-permute-start | bytes 393224 | tf_op jit(solution)/shard_map/ppermute | solution.py:502
  (24 other events, 346.4 us)
